TPU v7x, 1024 devices: a whole 4x4x32 slice. The times are simulated.
1024 devices in a mesh: dp: 64 (over x_lo, z), expert: 16 (over x_hi, y, core).
Axes of the slice: x: 4 (x_hi: 2, x_lo: 2; x = x_hi * 2 + x_lo), y: 4, z: 32, core: 2. Of those that a mesh axis runs over, the one named last changes fastest.
Arguments:
- tokens: bfloat16 [32768, 3584], P('dp'), may hold values from -16 to 16
- grad_out: bfloat16 [32768, 3584], P('dp'), may hold values from -6 to 6
- route_rows: int32 [32768], P('dp'), may hold values from 0 to 511, as said below
- route_gate: float32 [32768], P('dp'), may hold values from 0.1 to 1
- block_count: int32 [64], P('dp'), may hold values from 0 to 4, as said below
- gate_weight: bfloat16 [3584, 2048], P('dp', 'expert'), may hold values from -0.25 to 0.25
- up_weight: bfloat16 [3584, 2048], P('dp', 'expert'), may hold values from -0.25 to 0.25
- down_weight_t: bfloat16 [3584, 2048], P('dp', 'expert'), may hold values from -0.125 to 0.125
Outputs:
- grad_tokens: bfloat16 [32768, 3584], P('dp', 'expert')
- grad_gate_weight: float32 [3584, 2048], P('dp', 'expert')
- grad_up_weight: float32 [3584, 2048], P('dp', 'expert')
Inputs may be any that keep to these rules, and one draw needn't show every extreme that they name: `route_rows`: each index of dp holds 512 entries that are a permutation of 0 to 511. Slots 0 to block_count * 128 - 1 of an index of dp are live, its other slots empty; some index has all 4 blocks live and some index none.
All inputs are finite; a program needn't handle non-finite values.
Results may differ from a plain program's by a relative error of at most 0.017.
Values may be sent and summed in bfloat16 or wider, within the bound.
No kernel may reach another device: no remote copies, remote signals or barrier semaphores. Data moves between devices by JAX's collectives and lax.ppermute only.
A program may use at most 64 MiB of HBM per device.

v0:
```python
import jax
import jax.numpy as jnp
from jax import lax
from jax.sharding import PartitionSpec as P

BLOCK = 128


ROWS_CONTRACT = (((0,), (0,)), ((), ()))
COLS_CONTRACT = (((1,), (1,)), ((), ()))


def local(
    tokens, grad_out, route_rows, route_gate, block_count, gate_weight, up_weight, down_weight_t
):
    block_rows = BLOCK
    hidden_width = gate_weight.shape[1]
    slot_count = route_rows.shape[0]
    feature_count = tokens.shape[1]
    live_blocks = block_count[0]
    token_slots = jnp.take(tokens, route_rows, axis=0)
    gate_panel, up_panel, down_panel = (
        lax.all_gather(gate_weight, "dp", axis=0, tiled=True),
        lax.all_gather(up_weight, "dp", axis=0, tiled=True),
        lax.all_gather(down_weight_t, "dp", axis=0, tiled=True),
    )

    def backward_rows(rows_block):
        cotangent_block = jnp.take(grad_out, rows_block, axis=0)
        return jnp.dot(cotangent_block, down_panel, preferred_element_type=jnp.float32)

    both_panels = jnp.concatenate([gate_panel, up_panel], axis=1)

    def slot_grads(block_index):
        offset = block_index * block_rows
        rows_block = lax.dynamic_slice_in_dim(route_rows, offset, block_rows, 0)
        token_block = lax.dynamic_slice_in_dim(token_slots, offset, block_rows, 0)
        weight_block = lax.dynamic_slice_in_dim(route_gate, offset, block_rows, 0)
        projected = jnp.dot(token_block, both_panels, preferred_element_type=jnp.float32)
        gate_val = projected[:, :hidden_width]
        up_val = projected[:, hidden_width:]
        hidden_grad = weight_block[:, None] * backward_rows(rows_block)
        gate_sigmoid = jax.nn.sigmoid(gate_val)
        grad_up = hidden_grad * (gate_val * gate_sigmoid)
        grad_gate = hidden_grad * up_val * gate_sigmoid * (1.0 + gate_val * (1.0 - gate_sigmoid))
        return jnp.concatenate([grad_gate, grad_up], axis=1).astype(jnp.bfloat16)

    def input_block(grads_block):
        return lax.dot_general(
            grads_block, both_panels, COLS_CONTRACT, preferred_element_type=jnp.float32
        )

    empty_grads = jnp.zeros((slot_count, 2 * hidden_width), jnp.bfloat16)
    empty_inputs = jnp.zeros((slot_count, feature_count), jnp.float32)

    def step_both(block_index, running):
        grads_buffer, input_buffer = running
        grads_block = slot_grads(block_index)
        offset = block_index * block_rows
        grads_buffer = lax.dynamic_update_slice_in_dim(grads_buffer, grads_block, offset, 0)
        input_buffer = lax.dynamic_update_slice_in_dim(
            input_buffer, input_block(grads_block), offset, 0
        )
        return (grads_buffer, input_buffer)

    grads_buffer, input_buffer = lax.fori_loop(
        0, live_blocks, step_both, (empty_grads, empty_inputs)
    )
    weight_share = lax.psum_scatter(
        lax.dot_general(
            token_slots, grads_buffer, ROWS_CONTRACT, preferred_element_type=jnp.float32
        ),
        "dp",
        scatter_dimension=0,
        tiled=True,
    )
    summed_inputs = lax.psum_scatter(
        input_buffer.astype(jnp.bfloat16), "expert", scatter_dimension=1, tiled=True
    )
    grad_tokens = jnp.zeros(summed_inputs.shape, jnp.bfloat16).at[route_rows].set(summed_inputs)
    grad_scale = float(lax.axis_size("dp") * slot_count) ** (-0.5)
    grad_gate_weight = weight_share[:, :hidden_width] * grad_scale
    grad_up_weight = weight_share[:, hidden_width:] * grad_scale
    return (grad_tokens, grad_gate_weight, grad_up_weight)


def solution(mesh):
    in_specs = (
        P("dp", None),
        P("dp", None),
        P("dp"),
        P("dp"),
        P("dp"),
        P("dp", "expert"),
        P("dp", "expert"),
        P("dp", "expert"),
    )
    out_specs = (P("dp", "expert"), P("dp", "expert"), P("dp", "expert"))
    return jax.shard_map(local, mesh=mesh, in_specs=in_specs, out_specs=out_specs, check_vma=False)
```

profile of v0, /device:TPU:24, one launch (start us, length us, event | category | flops | bytes accessed | tf_op | source)
XLA Modules:
  0.0 869.0 jit_solution(738048448858521974)
XLA Ops:
  7.2 0.0 reduce-scatter.7.cloned.1.call-start
  7.2 0.7 compare_and_fusion.1
  7.9 0.7 compare_select_fusion.1
  8.6 139.1 %all_gather.10 = bf16[3584,128]{1,0:T(8,128)(2,1)S(1)} all-gather(bf16[56,128]{1,0:T(8,128)(2,1)} %param.15), channel_id=1, replica_groups=mesh['dp'=64,'expert'=16] {'dp'}, dimensions={0}, use_global_device_ids=true | all-gather | bytes 931840 | tf_op jit(solution)/shard_map/all_gather | solution.py:23
  147.7 121.8 %all_gather.11 = bf16[3584,128]{1,0:T(8,128)(2,1)S(1)} all-gather(bf16[56,128]{1,0:T(8,128)(2,1)} %param.16), channel_id=1, replica_groups=mesh['dp'=64,'expert'=16] {'dp'}, dimensions={0}, use_global_device_ids=true | all-gather | bytes 931840 | tf_op jit(solution)/shard_map/all_gather | solution.py:24
  269.5 132.9 %all_gather.9 = bf16[3584,128]{1,0:T(8,128)(2,1)} all-gather(bf16[56,128]{1,0:T(8,128)(2,1)} %param.17), channel_id=1, replica_groups=mesh['dp'=64,'expert'=16] {'dp'}, dimensions={0}, use_global_device_ids=true | all-gather | bytes 931840 | tf_op jit(solution)/shard_map/all_gather | solution.py:25
  402.4 0.2 pad_maximum_fusion.2
  402.6 10.4 %gather_fusion.1 = bf16[512,3584]{1,0:T(8,128)(2,1)} fusion(bf16[512,3584]{1,0:T(8,128)(2,1)} %param.10, s32[1024]{0:T(1024)S(1)} %pad_clamp_fusion.1), kind=kCustom, calls=%fused_computation.1 | custom fusion | bytes 7342080 | tf_op jit(solution)/shard_map/jit(_take)/gather | solution.py:21
  413.0 4.3 broadcast_select_fusion
  417.4 2.1 broadcast_in_dim.38
  419.4 24.9 %while.12 = (s32[]{:T(128)}, bf16[512,256]{0,1:T(8,128)(2,1)S(1)}, bf16[512,3584]{1,0:T(8,128)(2,1)}, s32[]{:T(128)}, f32[512]{0:T(512)}, /*index=5*/s32[512]{0:...) while((s32[]{:T(128)}, bf16[512,256]{0,1:T(8,128)(2,1)S(1)}, ...), condition=%wide.region_1.2_spmd, body=%wide.region_0.1_spmd.sunk | while | flops 588154624 | bytes 10624967 | solution.py:66
  420.1 0.8 dynamic_slice.16
  420.9 0.8 compare_and_fusion.3
  421.6 2.0 fusion.31
  423.7 4.5 gather_fusion
  428.2 1.7 fusion.32
  429.9 1.7 convolution_dynamic-update-slice_fusion.2
  432.3 0.8 dynamic_slice.16
  433.0 0.8 compare_and_fusion.3
  433.8 2.0 fusion.31
  435.8 4.5 gather_fusion
  440.3 1.7 fusion.32
  442.1 1.7 convolution_dynamic-update-slice_fusion.2
  444.4 5.9 copy.21
  450.4 0.2 reduce-scatter.5.cloned.1.call-start
  450.6 5.0 fusion.14
  455.7 130.3 %reduce-scatter.7.cloned.1.call-done = bf16[224,512]{1,0:T(8,128)(2,1)} async-done(((bf16[3584,512]{1,0:T(8,128)(2,1)}), bf16[224,512]{1,0:T(8,128)(2,1)}) %reduce-scatter.7.cloned.1.call-update) | async-done | bytes 229392
  585.9 1.1 copy.22
  587.0 2.4 scatter_custom_fusion
  589.4 0.8 copy.19
  590.2 270.5 %reduce-scatter.5.cloned.1.call-done = f32[56,256]{1,0:T(8,128)} async-done(((f32[3584,256]{1,0:T(8,128)}), f32[56,256]{1,0:T(8,128)}) %reduce-scatter.5.cloned.1.call-update) | async-done | bytes 57360 | tf_op jit(solution)/shard_map/reduce_scatter | solution.py:69
  860.8 1.4 slice_multiply_fusion.1
  (8 shorter events, 0.1 us)
Async XLA Ops:
  7.2 578.8 %reduce-scatter.7.cloned.1.call-start = ((), (), s32[]{:S(2)}) async-start(), calls=%async_computation.3 | async-start | bytes 3899392
  450.4 410.4 %reduce-scatter.5.cloned.1.call-start = ((), (), s32[]{:S(2)}) async-start(), calls=%async_computation.2 | async-start | bytes 3727360 | tf_op jit(solution)/shard_map/reduce_scatter | solution.py:69
Sparse Core Ops, SparseCore 0:
  450.5 135.4 reduce-scatter.6
  589.7 271.0 reduce-scatter.4
where the time goes:
time: 870 us; the launch traced here: 869 us
  waiting for transfers between devices  401 us (46%)
  blocking collectives  394 us (45%)
  local copies, waits for them, and re-layouts  33.3 us (4%)
  matrix products  15.8 us (2%)
  between operations  14.1 us (2%)
  other arithmetic  8.88 us (1%)
    reduce_scatter x1, waiting for transfers between devices, local(): lax.psum_scatter(lax.dot_general(token_slots, grads_buffer, ROWS_CONTRACT...  271 us
    all_gather x1, blocking collectives, local(): lax.all_gather(gate_weight, 'dp', axis=0, tiled=True)  139 us
    all_gather x1, blocking collectives, local(): lax.all_gather(down_weight_t, 'dp', axis=0, tiled=True)  133 us
    unnamed x3, waiting for transfers between devices  130 us
    all_gather x1, blocking collectives, local(): lax.all_gather(up_weight, 'dp', axis=0, tiled=True)  122 us
  transfers between devices with their start and end apart: 2, of which 2 were waited for; matrix products, arithmetic and copies ran while one was open for 1% of the time, Pallas kernels for 0%

commit v1 on v0

v1 whole, which is shorter than its diff:
```python
import jax
import jax.numpy as jnp
from jax import lax
from jax.sharding import Mesh, PartitionSpec as P

BLOCK = 128
SIZES = {"side": 2, "far": 16, "near": 2, "wide": 2, "ring": 4, "core": 2}
SIDE, FAR, NEAR, WIDE, RING, CORE = SIZES.values()
DP = ("side", "far", "near")
QUAD = ("side", "near")
EXPERT = ("wide", "ring", "core")

ROWS_CONTRACT = (((0,), (0,)), ((), ()))
COLS_CONTRACT = (((1,), (1,)), ((), ()))


def summed(terms):
    total = terms[0].astype(jnp.float32)
    for term in terms[1:]:
        total = total + term.astype(jnp.float32)
    return total


def shifted_term(parts, axis, dim, shift):
    count = SIZES[axis]
    index = lax.axis_index(axis)
    sent = lax.dynamic_index_in_dim(parts, (index + shift) % count, dim, keepdims=False)
    if shift == 0:
        return sent
    return lax.ppermute(sent, axis, [(i, (i + shift) % count) for i in range(count)])


def permuted_sum(parts, axis, dim):
    shifts = [0, 1, SIZES[axis] - 1] + list(range(2, SIZES[axis] - 1))
    shifts = shifts[: SIZES[axis]]
    return summed([shifted_term(parts, axis, dim, shift) for shift in shifts])


def exchanged_sum(parts, axes):
    terms = lax.all_to_all(parts, axes, 0, 0, tiled=True)
    return summed([terms[i] for i in range(terms.shape[0])])


def local(
    tokens, grad_out, route_rows, route_gate, block_count, gate_weight, up_weight, down_weight_t
):
    own_rows, hidden_width = gate_weight.shape
    slot_count = route_rows.shape[0]
    feature_count = tokens.shape[1]

    slots = jnp.arange(slot_count, dtype=jnp.int32)
    slot_gate = jnp.where(slots // BLOCK < block_count[0], route_gate, 0.0)
    carried = route_rows[:, None] == slots[None, :]
    token_gate = jnp.sum(jnp.where(carried, slot_gate[:, None], 0.0), axis=0)

    owned = jnp.concatenate([gate_weight, up_weight, down_weight_t], axis=1)
    far_rows = lax.all_gather(owned, "far", axis=0, tiled=True)
    quads = jnp.broadcast_to(far_rows[None], (SIDE * NEAR, *far_rows.shape))
    quads = lax.all_to_all(quads, QUAD, 0, 0, tiled=True)
    panels = quads.reshape(SIDE, NEAR, FAR, own_rows, 3 * hidden_width)
    panels = panels.swapaxes(1, 2).reshape(feature_count, 3 * hidden_width)
    both_panels = panels[:, : 2 * hidden_width]
    down_panel = panels[:, 2 * hidden_width :]

    projected = jnp.dot(tokens, both_panels, preferred_element_type=jnp.float32)
    back = jnp.dot(grad_out, down_panel, preferred_element_type=jnp.float32)
    gate_val = projected[:, :hidden_width]
    up_val = projected[:, hidden_width:]
    hidden_grad = token_gate[:, None] * back
    gate_sigmoid = jax.nn.sigmoid(gate_val)
    grad_up = hidden_grad * (gate_val * gate_sigmoid)
    grad_gate = hidden_grad * up_val * gate_sigmoid * (1.0 + gate_val * (1.0 - gate_sigmoid))
    grads = jnp.concatenate([grad_gate, grad_up], axis=1).astype(jnp.bfloat16)

    weight_terms = lax.dot_general(
        tokens, grads, ROWS_CONTRACT, preferred_element_type=jnp.float32
    ).astype(jnp.bfloat16)
    by_quad = weight_terms.reshape(SIDE, FAR, NEAR, own_rows, 2 * hidden_width)
    by_quad = by_quad.swapaxes(1, 2).reshape(SIDE * NEAR, FAR, own_rows, 2 * hidden_width)
    quad_sum = exchanged_sum(by_quad, QUAD).astype(jnp.bfloat16)
    weight_share = exchanged_sum(quad_sum, "far")
    grad_scale = float(SIDE * FAR * NEAR * slot_count) ** (-0.5)
    weight_share = weight_share * grad_scale

    input_terms = lax.dot_general(
        both_panels, grads, COLS_CONTRACT, preferred_element_type=jnp.float32
    ).astype(jnp.bfloat16)
    own_features = feature_count // (WIDE * RING * CORE)
    by_expert = input_terms.reshape(WIDE, RING, CORE, own_features, slot_count)
    core_sum = permuted_sum(by_expert, "core", 2).astype(jnp.bfloat16)
    ring_sum = permuted_sum(core_sum, "ring", 1).astype(jnp.bfloat16)
    wide_sum = permuted_sum(ring_sum, "wide", 0).astype(jnp.bfloat16)
    grad_tokens = wide_sum.T
    return grad_tokens, weight_share[:, :hidden_width], weight_share[:, hidden_width:]


def solution(mesh):
    fine_mesh = Mesh(mesh.devices.reshape(tuple(SIZES.values())), tuple(SIZES))
    in_specs = (P(DP, None), P(DP, None), P(DP), P(DP), P(DP)) + (P(DP, EXPERT),) * 3
    out_specs = (P(DP, EXPERT),) * 3
    return jax.shard_map(
        local, mesh=fine_mesh, in_specs=in_specs, out_specs=out_specs, check_vma=False
    )
```

time: 870 us -> 198 us (0.23)
  blocking collectives: 394 us -> 54.2 us
  waiting for transfers between devices: 401 us -> 71.5 us
  starting transfers between devices: 0.26 us -> 36.7 us
  local copies, waits for them, and re-layouts: 33.3 us -> 18.1 us
  between operations: 14.1 us -> 1.55 us
  matrix products: 15.8 us -> 5.99 us
    all_gather x3 -> x1, blocking collectives: 394 us -> 54.2 us  [local(): far_rows = lax.all_gather(owned, 'far', axis=0, tiled=True)]
    reduce_scatter x1 -> x0, waiting for transfers between devices: 271 us -> none  [local(): lax.psum_scatter(lax.dot_general(token_slots, grads_buffer, ROWS_CONTRACT...]
    unnamed x3 -> x0, waiting for transfers between devices: 130 us -> none
    all_to_all x0 -> x3, waiting for transfers between devices: none -> 49.8 us  [the longest x2 26 us: exchanged_sum(): terms = lax.all_to_all(parts, axes, 0, 0, tiled=True)]
    ppermute x0 -> x5, waiting for transfers between devices: none -> 21.7 us  [shifted_term(): lax.ppermute(sent, axis, [(i, (i + shift) % count) for i in range(count)])]
    all_to_all x0 -> x3, starting transfers between devices: none -> 20.9 us  [the longest x2 17.1 us: exchanged_sum(): terms = lax.all_to_all(parts, axes, 0, 0, tiled=True)]
    gather x3 -> x0, local copies, waits for them, and re-layouts: 19.5 us -> none  [the longest x1 10.4 us: local(): token_slots = jnp.take(tokens, route_rows, axis=0)]
    ppermute x0 -> x5, starting transfers between devices: none -> 15.8 us  [shifted_term(): lax.ppermute(sent, axis, [(i, (i + shift) % count) for i in range(count)])]
  transfers between devices with their start and end apart: 2 -> 8, of which waited for: 2 -> 6; matrix products, arithmetic and copies ran while one was open for 1% -> 6% of each run, Pallas kernels for 0% -> 0%
where the time goes in v1:
time: 198 us; the launch traced here: 196 us
  waiting for transfers between devices  71.5 us (36%)
  blocking collectives  54.2 us (27%)
  starting transfers between devices  36.7 us (19%)
  local copies, waits for them, and re-layouts  18.1 us (9%)
  other arithmetic  8.23 us (4%)
  matrix products  5.99 us (3%)
    all_gather x1, blocking collectives, local(): far_rows = lax.all_gather(owned, 'far', axis=0, tiled=True)  54.2 us
    all_to_all x2, waiting for transfers between devices, exchanged_sum(): terms = lax.all_to_all(parts, axes, 0, 0, tiled=True)  26 us
    all_to_all x1, waiting for transfers between devices, local(): quads = lax.all_to_all(quads, QUAD, 0, 0, tiled=True)  23.8 us
    ppermute x5, waiting for transfers between devices, shifted_term(): lax.ppermute(sent, axis, [(i, (i + shift) % count) for i in range(count)])  21.7 us
    all_to_all x2, starting transfers between devices, exchanged_sum(): terms = lax.all_to_all(parts, axes, 0, 0, tiled=True)  17.1 us
    ppermute x5, starting transfers between devices, shifted_term(): lax.ppermute(sent, axis, [(i, (i + shift) % count) for i in range(count)])  15.8 us
  transfers between devices with their start and end apart: 8, of which 6 were waited for; matrix products, arithmetic and copies ran while one was open for 6% of the time, Pallas kernels for 0%

profile of v1, /device:TPU:24, one launch (start us, length us, event | category | flops | bytes accessed | tf_op | source)
XLA Modules:
  0.0 196.2 jit_solution(9138053814038212233)
XLA Ops:
  0.6 0.8 pad_maximum_fusion.3
  1.4 54.2 %all_gather.3 = bf16[896,384]{1,0:T(8,128)(2,1)S(1)} all-gather(bf16[56,384]{1,0:T(8,128)(2,1)S(1)} %pad_maximum_fusion.3), channel_id=1, replica_groups=mesh['side'=2,'far'=16,'near'=2,'wide'=2,'ring'=4,'core'=2] {'far'}, dimensions={0}, use_global_device_ids=true | all-gather | bytes 731136 | tf_op jit(solution)/shard_map/all_gather | solution.py:57
  55.6 1.8 broadcast_in_dim.26
  57.4 3.8 %all-to-all-start = ((bf16[4,896,384]{2,1,0:T(8,128)(2,1)}), bf16[4,896,384]{2,1,0:T(8,128)(2,1)S(1)}, u32[]{:S(2)}, u32[]{:S(2)}) async-start(bf16[4,896,384]{2,1,0:T(8,128)(2,1)} %broadcast_in_dim.26), calls=%async_computation | async-start | bytes 5505024 | tf_op jit(solution)/shard_map/all_to_all | solution.py:59
  62.1 23.8 %all-to-all-done = bf16[4,896,384]{2,1,0:T(8,128)(2,1)S(1)} async-done(((bf16[4,896,384]{2,1,0:T(8,128)(2,1)}), bf16[4,896,384]{2,1,0:T(8,128)(2,1)S(1)}, u32[]{:S(2)}, u32[]{:S(2)}) %all-to-all-start) | async-done | bytes 2752544 | tf_op jit(solution)/shard_map/all_to_all | solution.py:59
  85.8 1.5 copy-done
  87.4 2.2 %copy.22 = bf16[2,16,2,56,384]{4,3,2,1,0:T(8,128)(2,1)S(1)} copy(bf16[2,16,2,56,384]{4,3,1,2,0:T(8,128)(2,1)} %bitcast.57) | data formatting | bytes 5505024 | tf_op jit(solution)/shard_map/transpose | solution.py:61
  90.3 1.2 fusion.5
  91.4 0.9 copy-done.5
  92.3 1.4 fusion.17
  93.7 2.3 %fusion = bf16[3584,256]{0,1:T(8,128)(2,1)} fusion(bf16[512,3584]{1,0:T(8,128)(2,1)S(1)} %copy-done.1, bf16[512,128]{0,1:T(8,128)(2,1)S(1)} %get-tuple-element.9, bf16[512,128]{0,1:T(8,128)(2,1)S(1)} %get-tuple-element.8), kind=kOutput, calls=%fused_computation.2 | convolution fusion | flops 940965888 | bytes 5767168 | tf_op jit(solution)/shard_map/dot_general | solution.py:75
  96.0 3.8 %copy.25 = bf16[3584,256]{1,0:T(8,128)(2,1)} copy(bf16[3584,256]{0,1:T(8,128)(2,1)} %fusion) | data formatting | bytes 3670016 | tf_op jit(solution)/shard_map/convert_element_type | solution.py:77
  99.8 2.9 %copy.26 = bf16[2,2,16,56,256]{4,3,2,1,0:T(8,128)(2,1)} copy(bf16[2,2,16,56,256]{4,3,1,2,0:T(8,128)(2,1)} %bitcast.59) | data formatting | bytes 3670016 | tf_op jit(solution)/shard_map/transpose | solution.py:79
  102.7 4.4 %all-to-all-start.1 = ((bf16[4,16,56,256]{3,2,1,0:T(8,128)(2,1)}), bf16[4,16,56,256]{3,2,1,0:T(8,128)(2,1)}, u32[]{:S(2)}, u32[]{:S(2)}) async-start(bf16[4,16,56,256]{3,2,1,0:T(8,128)(2,1)} %bitcast.58), calls=%async_computation.1 | async-start | bytes 3670016 | tf_op jit(solution)/shard_map/all_to_all | solution.py:40
  107.1 1.1 convolution_convert_fusion
  108.2 1.6 constant_dynamic-slice_fusion.1
  110.0 1.9 collective-permute-start
  111.9 16.4 %all-to-all-done.1 = bf16[4,16,56,256]{3,2,1,0:T(8,128)(2,1)} async-done(((bf16[4,16,56,256]{3,2,1,0:T(8,128)(2,1)}), bf16[4,16,56,256]{3,2,1,0:T(8,128)(2,1)}, u32[]{:S(2)}, u32[]{:S(2)}) %all-to-all-start.1) | async-done | bytes 1835040 | tf_op jit(solution)/shard_map/all_to_all | solution.py:40
  128.3 2.4 %fusion.13 = bf16[16,56,256]{2,1,0:T(8,128)(2,1)} fusion(bf16[4,16,56,256]{3,2,1,0:T(8,128)(2,1)} %all-to-all-done.1), kind=kLoop, calls=%fused_computation.21 | loop fusion | flops 1835008 | bytes 2293760 | tf_op jit(solution)/shard_map/add | solution.py:20
  130.8 12.7 %all-to-all-start.2 = ((bf16[16,56,256]{2,1,0:T(8,128)(2,1)}), bf16[16,56,256]{2,1,0:T(8,128)(2,1)S(1)}, u32[]{:S(2)}, u32[]{:S(2)}) async-start(bf16[16,56,256]{2,1,0:T(8,128)(2,1)} %fusion.13), calls=%async_computation.2 | async-start | bytes 917504 | tf_op jit(solution)/shard_map/all_to_all | solution.py:40
  143.5 2.6 %fusion.1 = bf16[2,4,224,512]{3,2,0,1:T(8,128)(2,1)S(1)} fusion(bf16[2,4,224,512]{3,2,0,1:T(8,128)(2,1)} %collective-permute-done, bf16[2,4,1,224,512]{4,3,2,1,0:T(8,128)(2,1)} %get-tuple-element.3), kind=kLoop, calls=%fused_computation.4 | loop fusion | flops 3670016 | bytes 5505024 | tf_op jit(solution)/shard_map/convert_element_type | solution.py:90
  146.2 1.2 dynamic-slice_bitcast_fusion.2
  147.3 2.2 %collective-permute-start.1 = (bf16[2,224,512]{2,1,0:T(8,128)(2,1)}, bf16[2,224,512]{2,1,0:T(8,128)(2,1)S(1)}, u32[]{:S(2)}, u32[]{:S(2)}) collective-permute-start(bf16[2,224,512]{2,1,0:T(8,128)(2,1)} %get-tuple-element.5), channel_id=1, source_target_pairs={{0,2},{2,4},{4,6},{6,0},{1,3},{3,5},{5,7},{7,1},{8,10},{10,12},{12... | collective-permute-start | bytes 1376264 | tf_op jit(solution)/shard_map/ppermute | solution.py:30
  149.5 3.7 %collective-permute-start.2 = (bf16[2,224,512]{2,1,0:T(8,128)(2,1)}, bf16[2,224,512]{2,1,0:T(8,128)(2,1)S(1)}, u32[]{:S(2)}, u32[]{:S(2)}) collective-permute-start(bf16[2,224,512]{2,1,0:T(8,128)(2,1)} %get-tuple-element.7), channel_id=1, source_target_pairs={{0,6},{2,0},{4,2},{6,4},{1,7},{3,1},{5,3},{7,5},{8,14},{10,8},{12,... | collective-permute-start | bytes 1376264 | tf_op jit(solution)/shard_map/ppermute | solution.py:30
  153.2 3.1 %collective-permute-start.3 = (bf16[2,224,512]{2,1,0:T(8,128)(2,1)}, bf16[2,224,512]{2,1,0:T(8,128)(2,1)}, u32[]{:S(2)}, u32[]{:S(2)}) collective-permute-start(bf16[2,224,512]{2,1,0:T(8,128)(2,1)} %get-tuple-element.6), channel_id=1, source_target_pairs={{0,4},{2,6},{4,0},{6,2},{1,5},{3,7},{5,1},{7,3},{8,12},{10,14},{12... | collective-permute-start | bytes 1376264 | tf_op jit(solution)/shard_map/ppermute | solution.py:30
  156.3 6.5 %collective-permute-done.1 = bf16[2,224,512]{2,1,0:T(8,128)(2,1)S(1)} collective-permute-done((bf16[2,224,512]{2,1,0:T(8,128)(2,1)}, bf16[2,224,512]{2,1,0:T(8,128)(2,1)S(1)}, u32[]{:S(2)}, u32[]{:S(2)}) %collective-permute-start.1) | collective-permute-done | bytes 458784 | tf_op jit(solution)/shard_map/ppermute | solution.py:30
  162.9 10.7 %collective-permute-done.2 = bf16[2,224,512]{2,1,0:T(8,128)(2,1)S(1)} collective-permute-done((bf16[2,224,512]{2,1,0:T(8,128)(2,1)}, bf16[2,224,512]{2,1,0:T(8,128)(2,1)S(1)}, u32[]{:S(2)}, u32[]{:S(2)}) %collective-permute-start.2) | collective-permute-done | bytes 458784 | tf_op jit(solution)/shard_map/ppermute | solution.py:30
  173.5 0.8 copy-done.2
  174.3 1.4 fusion.12
  175.7 4.9 %collective-permute-start.4 = (bf16[224,512]{1,0:T(8,128)(2,1)S(1)}, bf16[224,512]{1,0:T(8,128)(2,1)S(1)}, u32[]{:S(2)}, u32[]{:S(2)}) collective-permute-start(bf16[224,512]{1,0:T(8,128)(2,1)S(1)} %dynamic-slice_bitcast_fusion.3), channel_id=1, source_target_pairs={{0,8},{8,0},{1,9},{9,1},{2,10},{10,2},{3,11},{11,3},{4,12},{12,4},... | collective-permute-start | bytes 688136 | tf_op jit(solution)/shard_map/ppermute | solution.py:30
  180.7 4.5 %collective-permute-done.4 = bf16[224,512]{1,0:T(8,128)(2,1)S(1)} collective-permute-done((bf16[224,512]{1,0:T(8,128)(2,1)S(1)}, bf16[224,512]{1,0:T(8,128)(2,1)S(1)}, u32[]{:S(2)}, u32[]{:S(2)}) %collective-permute-start.4) | collective-permute-done | bytes 229408 | tf_op jit(solution)/shard_map/ppermute | solution.py:30
  185.9 9.6 %all-to-all-done.2 = bf16[16,56,256]{2,1,0:T(8,128)(2,1)S(1)} async-done(((bf16[16,56,256]{2,1,0:T(8,128)(2,1)}), bf16[16,56,256]{2,1,0:T(8,128)(2,1)S(1)}, u32[]{:S(2)}, u32[]{:S(2)}) %all-to-all-start.2) | async-done | bytes 458784 | tf_op jit(solution)/shard_map/all_to_all | solution.py:40
  (18 shorter events, 2.5 us)
Async XLA Ops:
  57.4 4.5 %copy-start.4 = (f32[512]{0:T(512)S(1)}, f32[512]{0:T(512)}, u32[]{:S(2)}) copy-start(f32[512]{0:T(512)} %param.11) | copy-start | bytes 6148
  57.4 4.5 %copy-start.3 = (s32[512]{0:T(512)S(1)}, s32[512]{0:T(512)}, u32[]{:S(2)}) copy-start(s32[512]{0:T(512)} %param.10) | copy-start | bytes 6148
  57.4 28.5 %all-to-all-start = ((bf16[4,896,384]{2,1,0:T(8,128)(2,1)}), bf16[4,896,384]{2,1,0:T(8,128)(2,1)S(1)}, u32[]{:S(2)}, u32[]{:S(2)}) async-start(bf16[4,896,384]{2,1,0:T(8,128)(2,1)} %broadcast_in_dim.26), calls=%async_computation | async-start | bytes 5505024 | tf_op jit(solution)/shard_map/all_to_all | solution.py:59
  85.8 1.5 copy-start
  87.4 2.9 %copy-start.1 = (bf16[512,3584]{1,0:T(8,128)(2,1)S(1)}, bf16[512,3584]{1,0:T(8,128)(2,1)}, u32[]{:S(2)}) copy-start(bf16[512,3584]{1,0:T(8,128)(2,1)} %param.8) | copy-start | bytes 11010052
  90.2 2.0 %copy-start.5 = (bf16[512,3584]{1,0:T(8,128)(2,1)S(1)}, bf16[512,3584]{1,0:T(8,128)(2,1)}, u32[]{:S(2)}) copy-start(bf16[512,3584]{1,0:T(8,128)(2,1)} %param.9) | copy-start | bytes 11010052
  102.7 25.6 %all-to-all-start.1 = ((bf16[4,16,56,256]{3,2,1,0:T(8,128)(2,1)}), bf16[4,16,56,256]{3,2,1,0:T(8,128)(2,1)}, u32[]{:S(2)}, u32[]{:S(2)}) async-start(bf16[4,16,56,256]{3,2,1,0:T(8,128)(2,1)} %bitcast.58), calls=%async_computation.1 | async-start | bytes 3670016 | tf_op jit(solution)/shard_map/all_to_all | solution.py:40
  110.0 33.5 %collective-permute-start = (bf16[2,4,224,512]{3,2,0,1:T(8,128)(2,1)S(1)}, bf16[2,4,224,512]{3,2,0,1:T(8,128)(2,1)}, u32[]{:S(2)}, u32[]{:S(2)}) collective-permute-start(bf16[2,4,224,512]{3,2,0,1:T(8,128)(2,1)S(1)} %bitcast.60), channel_id=1, source_target_pairs={{0,1},{1,0},{2,3},{3,2},{4,5},{5,4},{6,7},{7,6},{8,9},{9,8},{10,11... | collective-permute-start | bytes 5505032 | tf_op jit(solution)/shard_map/ppermute | solution.py:30
  130.8 64.8 %all-to-all-start.2 = ((bf16[16,56,256]{2,1,0:T(8,128)(2,1)}), bf16[16,56,256]{2,1,0:T(8,128)(2,1)S(1)}, u32[]{:S(2)}, u32[]{:S(2)}) async-start(bf16[16,56,256]{2,1,0:T(8,128)(2,1)} %fusion.13), calls=%async_computation.2 | async-start | bytes 917504 | tf_op jit(solution)/shard_map/all_to_all | solution.py:40
  147.3 15.5 %collective-permute-start.1 = (bf16[2,224,512]{2,1,0:T(8,128)(2,1)}, bf16[2,224,512]{2,1,0:T(8,128)(2,1)S(1)}, u32[]{:S(2)}, u32[]{:S(2)}) collective-permute-start(bf16[2,224,512]{2,1,0:T(8,128)(2,1)} %get-tuple-element.5), channel_id=1, source_target_pairs={{0,2},{2,4},{4,6},{6,0},{1,3},{3,5},{5,7},{7,1},{8,10},{10,12},{12... | collective-permute-start | bytes 1376264 | tf_op jit(solution)/shard_map/ppermute | solution.py:30
  149.5 24.0 %collective-permute-start.2 = (bf16[2,224,512]{2,1,0:T(8,128)(2,1)}, bf16[2,224,512]{2,1,0:T(8,128)(2,1)S(1)}, u32[]{:S(2)}, u32[]{:S(2)}) collective-permute-start(bf16[2,224,512]{2,1,0:T(8,128)(2,1)} %get-tuple-element.7), channel_id=1, source_target_pairs={{0,6},{2,0},{4,2},{6,4},{1,7},{3,1},{5,3},{7,5},{8,14},{10,8},{12,... | collective-permute-start | bytes 1376264 | tf_op jit(solution)/shard_map/ppermute | solution.py:30
  153.2 21.1 %collective-permute-start.3 = (bf16[2,224,512]{2,1,0:T(8,128)(2,1)}, bf16[2,224,512]{2,1,0:T(8,128)(2,1)}, u32[]{:S(2)}, u32[]{:S(2)}) collective-permute-start(bf16[2,224,512]{2,1,0:T(8,128)(2,1)} %get-tuple-element.6), channel_id=1, source_target_pairs={{0,4},{2,6},{4,0},{6,2},{1,5},{3,7},{5,1},{7,3},{8,12},{10,14},{12... | collective-permute-start | bytes 1376264 | tf_op jit(solution)/shard_map/ppermute | solution.py:30
  173.5 0.8 copy-start.2
  175.7 9.4 %collective-permute-start.4 = (bf16[224,512]{1,0:T(8,128)(2,1)S(1)}, bf16[224,512]{1,0:T(8,128)(2,1)S(1)}, u32[]{:S(2)}, u32[]{:S(2)}) collective-permute-start(bf16[224,512]{1,0:T(8,128)(2,1)S(1)} %dynamic-slice_bitcast_fusion.3), channel_id=1, source_target_pairs={{0,8},{8,0},{1,9},{9,1},{2,10},{10,2},{3,11},{11,3},{4,12},{12,4},... | collective-permute-start | bytes 688136 | tf_op jit(solution)/shard_map/ppermute | solution.py:30

commit v2 on v1

--- a/solution.py
+++ b/solution.py
@@ -55,6 +55,9 @@
 
     owned = jnp.concatenate([gate_weight, up_weight, down_weight_t], axis=1)
     far_rows = lax.all_gather(owned, "far", axis=0, tiled=True)
+    far_rows, early_tokens = lax.optimization_barrier((far_rows, tokens))
+    feature_rows = early_tokens.T.reshape(SIDE, FAR, NEAR, own_rows, slot_count)
+    feature_rows = lax.optimization_barrier(feature_rows.swapaxes(1, 2))
     quads = jnp.broadcast_to(far_rows[None], (SIDE * NEAR, *far_rows.shape))
     quads = lax.all_to_all(quads, QUAD, 0, 0, tiled=True)
     panels = quads.reshape(SIDE, NEAR, FAR, own_rows, 3 * hidden_width)
@@ -72,15 +75,11 @@
     grad_gate = hidden_grad * up_val * gate_sigmoid * (1.0 + gate_val * (1.0 - gate_sigmoid))
     grads = jnp.concatenate([grad_gate, grad_up], axis=1).astype(jnp.bfloat16)
 
-    weight_terms = lax.dot_general(
-        tokens, grads, ROWS_CONTRACT, preferred_element_type=jnp.float32
+    weight_terms = jnp.dot(
+        feature_rows.reshape(feature_count, slot_count), grads, preferred_element_type=jnp.float32
     ).astype(jnp.bfloat16)
-    by_quad = weight_terms.reshape(SIDE, FAR, NEAR, own_rows, 2 * hidden_width)
-    by_quad = by_quad.swapaxes(1, 2).reshape(SIDE * NEAR, FAR, own_rows, 2 * hidden_width)
-    quad_sum = exchanged_sum(by_quad, QUAD).astype(jnp.bfloat16)
-    weight_share = exchanged_sum(quad_sum, "far")
-    grad_scale = float(SIDE * FAR * NEAR * slot_count) ** (-0.5)
-    weight_share = weight_share * grad_scale
+    by_quad = weight_terms.reshape(SIDE * NEAR, FAR, own_rows, 2 * hidden_width)
+    quad_terms = lax.all_to_all(by_quad, QUAD, 0, 0, tiled=True)
 
     input_terms = lax.dot_general(
         both_panels, grads, COLS_CONTRACT, preferred_element_type=jnp.float32
@@ -88,6 +87,11 @@
     own_features = feature_count // (WIDE * RING * CORE)
     by_expert = input_terms.reshape(WIDE, RING, CORE, own_features, slot_count)
     core_sum = permuted_sum(by_expert, "core", 2).astype(jnp.bfloat16)
+    quad_terms, _ = lax.optimization_barrier((quad_terms, core_sum))
+    quad_sum = summed([quad_terms[i] for i in range(SIDE * NEAR)]).astype(jnp.bfloat16)
+    weight_share = exchanged_sum(quad_sum, "far")
+    grad_scale = float(SIDE * FAR * NEAR * slot_count) ** (-0.5)
+    weight_share = weight_share * grad_scale
     ring_sum = permuted_sum(core_sum, "ring", 1).astype(jnp.bfloat16)
     wide_sum = permuted_sum(ring_sum, "wide", 0).astype(jnp.bfloat16)
     grad_tokens = wide_sum.T

time: 198 us -> 194 us (0.980)
  waiting for transfers between devices: 71.5 us -> 68 us
  local copies, waits for them, and re-layouts: 18.1 us -> 20.9 us
  other arithmetic: 8.23 us -> 6.15 us
    all_to_all x0 -> x1, waiting for transfers between devices: none -> 13.4 us  [local(): quad_terms = lax.all_to_all(by_quad, QUAD, 0, 0, tiled=True)]
    all_to_all x2 -> x1, waiting for transfers between devices: 26 us -> 15.4 us  [exchanged_sum(): terms = lax.all_to_all(parts, axes, 0, 0, tiled=True)]
    optimization_barrier x0 -> x2, local copies, waits for them, and re-layouts: none -> 10.1 us  [the longest x1 5.93 us: local(): far_rows, early_tokens = lax.optimization_barrier((far_rows, tokens))]
    all_to_all x1, waiting for transfers between devices: 23.8 us -> 13.6 us  [local(): quads = lax.all_to_all(quads, QUAD, 0, 0, tiled=True)]
    all_to_all x2 -> x1, starting transfers between devices: 17.1 us -> 12.5 us  [exchanged_sum(): terms = lax.all_to_all(parts, axes, 0, 0, tiled=True)]
    all_to_all x0 -> x1, starting transfers between devices: none -> 4.39 us  [local(): quad_terms = lax.all_to_all(by_quad, QUAD, 0, 0, tiled=True)]
    ppermute x5, waiting for transfers between devices: 21.7 us -> 25.7 us  [shifted_term(): lax.ppermute(sent, axis, [(i, (i + shift) % count) for i in range(count)])]
    convert_element_type x1 -> x0, local copies, waits for them, and re-layouts: 3.8 us -> none  [local(): weight_terms = lax.dot_general(tokens, grads, ROWS_CONTRACT, preferred_el...]
  transfers between devices with their start and end apart: 8 -> 8, of which waited for: 6 -> 7; matrix products, arithmetic and copies ran while one was open for 6% -> 8% of each run, Pallas kernels for 0% -> 0%
where the time goes in v2:
time: 194 us; the launch traced here: 193 us
  waiting for transfers between devices  68 us (35%)
  blocking collectives  54.2 us (28%)
  starting transfers between devices  36.3 us (19%)
  local copies, waits for them, and re-layouts  20.9 us (11%)
  other arithmetic  6.15 us (3%)
  matrix products  6.01 us (3%)
    all_gather x1, blocking collectives, local(): far_rows = lax.all_gather(owned, 'far', axis=0, tiled=True)  54.2 us
    ppermute x5, waiting for transfers between devices, shifted_term(): lax.ppermute(sent, axis, [(i, (i + shift) % count) for i in range(count)])  25.7 us
    ppermute x5, starting transfers between devices, shifted_term(): lax.ppermute(sent, axis, [(i, (i + shift) % count) for i in range(count)])  15.7 us
    all_to_all x1, waiting for transfers between devices, exchanged_sum(): terms = lax.all_to_all(parts, axes, 0, 0, tiled=True)  15.4 us
    all_to_all x1, waiting for transfers between devices, local(): quads = lax.all_to_all(quads, QUAD, 0, 0, tiled=True)  13.6 us
    all_to_all x1, waiting for transfers between devices, local(): quad_terms = lax.all_to_all(by_quad, QUAD, 0, 0, tiled=True)  13.4 us
    all_to_all x1, starting transfers between devices, exchanged_sum(): terms = lax.all_to_all(parts, axes, 0, 0, tiled=True)  12.5 us
    optimization_barrier x1, local copies, waits for them, and re-layouts, local(): far_rows, early_tokens = lax.optimization_barrier((far_rows, tokens))  5.93 us
  transfers between devices with their start and end apart: 8, of which 7 were waited for; matrix products, arithmetic and copies ran while one was open for 8% of the time, Pallas kernels for 0%

profile of v2, /device:TPU:24, one launch (start us, length us, event | category | flops | bytes accessed | tf_op | source)
XLA Modules:
  0.0 193.2 jit_solution(2061199679324059093)
XLA Ops:
  0.6 0.8 pad_maximum_fusion.3
  1.4 54.2 %all_gather.3 = bf16[896,384]{1,0:T(8,128)(2,1)S(1)} all-gather(bf16[56,384]{1,0:T(8,128)(2,1)S(1)} %pad_maximum_fusion.3), channel_id=1, replica_groups=mesh['side'=2,'far'=16,'near'=2,'wide'=2,'ring'=4,'core'=2] {'far'}, dimensions={0}, use_global_device_ids=true | all-gather | bytes 731136 | tf_op jit(solution)/shard_map/all_gather | solution.py:57
  55.6 1.8 broadcast_in_dim.26
  57.4 3.7 %all-to-all-start = ((bf16[4,896,384]{2,1,0:T(8,128)(2,1)}), bf16[4,896,384]{2,1,0:T(8,128)(2,1)S(1)}, u32[]{:S(2)}, u32[]{:S(2)}) async-start(bf16[4,896,384]{2,1,0:T(8,128)(2,1)} %broadcast_in_dim.26), calls=%async_computation | async-start | bytes 5505024 | tf_op jit(solution)/shard_map/all_to_all | solution.py:62
  61.8 5.9 %copy.25 = bf16[512,3584]{0,1:T(8,128)(2,1)} copy(bf16[512,3584]{1,0:T(8,128)(2,1)} %param.8) | data formatting | bytes 7340032 | tf_op jit(solution)/shard_map/optimization_barrier | solution.py:58
  67.7 4.2 %copy.26 = bf16[2,2,16,56,512]{4,3,2,1,0:T(8,128)(2,1)} copy(bf16[2,2,16,56,512]{4,3,1,2,0:T(8,128)(2,1)} %bitcast.55) | data formatting | bytes 7340032 | tf_op jit(solution)/shard_map/optimization_barrier | solution.py:60
  72.1 13.6 %all-to-all-done = bf16[4,896,384]{2,1,0:T(8,128)(2,1)S(1)} async-done(((bf16[4,896,384]{2,1,0:T(8,128)(2,1)}), bf16[4,896,384]{2,1,0:T(8,128)(2,1)S(1)}, u32[]{:S(2)}, u32[]{:S(2)}) %all-to-all-start) | async-done | bytes 2752544 | tf_op jit(solution)/shard_map/all_to_all | solution.py:62
  85.8 1.5 copy-done
  87.3 2.2 %copy.22 = bf16[2,16,2,56,384]{4,3,2,1,0:T(8,128)(2,1)S(1)} copy(bf16[2,16,2,56,384]{4,3,1,2,0:T(8,128)(2,1)} %bitcast.59) | data formatting | bytes 5505024 | tf_op jit(solution)/shard_map/transpose | solution.py:64
  90.2 1.2 fusion.4
  91.3 0.9 copy-done.6
  92.2 1.4 fusion.16
  94.3 2.4 %convolution_convert_fusion.1 = bf16[3584,256]{1,0:T(8,128)(2,1)} fusion(bf16[3584,512]{1,0:T(8,128)(2,1)S(1)} %bitcast.60, bf16[512,128]{0,1:T(8,128)(2,1)S(1)} %get-tuple-element.15, bf16[512,128]{0,1:T(8,128)(2,1)S(1)} %get-tuple-element.14), kind=kOutput, calls=%fused_computation.1 | convolution fusion | flops 940965888 | bytes 5767168 | tf_op jit(solution)/shard_map/dot_general | solution.py:78
  96.6 4.4 %all-to-all-start.1 = ((bf16[4,16,56,256]{3,2,1,0:T(8,128)(2,1)}), bf16[4,16,56,256]{3,2,1,0:T(8,128)(2,1)}, u32[]{:S(2)}, u32[]{:S(2)}) async-start(bf16[4,16,56,256]{3,2,1,0:T(8,128)(2,1)} %bitcast.61), calls=%async_computation.1 | async-start | bytes 3670016 | tf_op jit(solution)/shard_map/all_to_all | solution.py:82
  101.1 1.1 convolution_convert_fusion
  102.6 1.9 collective-permute-start
  104.6 3.8 %collective-permute-done = bf16[2,4,224,512]{3,2,0,1:T(8,128)(2,1)S(1)} collective-permute-done((bf16[2,4,224,512]{3,2,0,1:T(8,128)(2,1)S(1)}, bf16[2,4,224,512]{3,2,0,1:T(8,128)(2,1)S(1)}, u32[]{:S(2)}, u32[]{:S(2)}) %collective-permute-start) | collective-permute-done | bytes 1835040 | tf_op jit(solution)/shard_map/ppermute | solution.py:30
  108.9 13.4 %all-to-all-done.1 = bf16[4,16,56,256]{3,2,1,0:T(8,128)(2,1)} async-done(((bf16[4,16,56,256]{3,2,1,0:T(8,128)(2,1)}), bf16[4,16,56,256]{3,2,1,0:T(8,128)(2,1)}, u32[]{:S(2)}, u32[]{:S(2)}) %all-to-all-start.1) | async-done | bytes 1835040 | tf_op jit(solution)/shard_map/all_to_all | solution.py:82
  122.3 2.4 %fusion.12 = bf16[16,56,256]{2,1,0:T(8,128)(2,1)} fusion(bf16[4,16,56,256]{3,2,1,0:T(8,128)(2,1)} %all-to-all-done.1), kind=kLoop, calls=%fused_computation.20 | loop fusion | flops 1835008 | bytes 2293760 | tf_op jit(solution)/shard_map/add | solution.py:20
  124.7 12.5 %all-to-all-start.2 = ((bf16[16,56,256]{2,1,0:T(8,128)(2,1)}), bf16[16,56,256]{2,1,0:T(8,128)(2,1)S(1)}, u32[]{:S(2)}, u32[]{:S(2)}) async-start(bf16[16,56,256]{2,1,0:T(8,128)(2,1)} %fusion.12), calls=%async_computation.2 | async-start | bytes 917504 | tf_op jit(solution)/shard_map/all_to_all | solution.py:40
  137.3 1.1 dynamic-slice_bitcast_fusion.2
  138.4 2.3 %collective-permute-start.1 = (bf16[2,224,512]{2,1,0:T(8,128)(2,1)}, bf16[2,224,512]{2,1,0:T(8,128)(2,1)S(1)}, u32[]{:S(2)}, u32[]{:S(2)}) collective-permute-start(bf16[2,224,512]{2,1,0:T(8,128)(2,1)} %get-tuple-element.11), channel_id=1, source_target_pairs={{0,2},{2,4},{4,6},{6,0},{1,3},{3,5},{5,7},{7,1},{8,10},{10,12},{12... | collective-permute-start | bytes 1376264 | tf_op jit(solution)/shard_map/ppermute | solution.py:30
  140.8 3.5 %collective-permute-start.2 = (bf16[2,224,512]{2,1,0:T(8,128)(2,1)}, bf16[2,224,512]{2,1,0:T(8,128)(2,1)S(1)}, u32[]{:S(2)}, u32[]{:S(2)}) collective-permute-start(bf16[2,224,512]{2,1,0:T(8,128)(2,1)} %get-tuple-element.13), channel_id=1, source_target_pairs={{0,6},{2,0},{4,2},{6,4},{1,7},{3,1},{5,3},{7,5},{8,14},{10,8},{12,... | collective-permute-start | bytes 1376264 | tf_op jit(solution)/shard_map/ppermute | solution.py:30
  144.3 3.1 %collective-permute-start.3 = (bf16[2,224,512]{2,1,0:T(8,128)(2,1)}, bf16[2,224,512]{2,1,0:T(8,128)(2,1)}, u32[]{:S(2)}, u32[]{:S(2)}) collective-permute-start(bf16[2,224,512]{2,1,0:T(8,128)(2,1)} %get-tuple-element.12), channel_id=1, source_target_pairs={{0,4},{2,6},{4,0},{6,2},{1,5},{3,7},{5,1},{7,3},{8,12},{10,14},{12... | collective-permute-start | bytes 1376264 | tf_op jit(solution)/shard_map/ppermute | solution.py:30
  147.5 6.5 %collective-permute-done.1 = bf16[2,224,512]{2,1,0:T(8,128)(2,1)S(1)} collective-permute-done((bf16[2,224,512]{2,1,0:T(8,128)(2,1)}, bf16[2,224,512]{2,1,0:T(8,128)(2,1)S(1)}, u32[]{:S(2)}, u32[]{:S(2)}) %collective-permute-start.1) | collective-permute-done | bytes 458784 | tf_op jit(solution)/shard_map/ppermute | solution.py:30
  154.0 10.8 %collective-permute-done.2 = bf16[2,224,512]{2,1,0:T(8,128)(2,1)S(1)} collective-permute-done((bf16[2,224,512]{2,1,0:T(8,128)(2,1)}, bf16[2,224,512]{2,1,0:T(8,128)(2,1)S(1)}, u32[]{:S(2)}, u32[]{:S(2)}) %collective-permute-start.2) | collective-permute-done | bytes 458784 | tf_op jit(solution)/shard_map/ppermute | solution.py:30
  164.8 0.8 copy-done.3
  165.6 1.4 fusion.11
  167.0 4.8 %collective-permute-start.4 = (bf16[224,512]{1,0:T(8,128)(2,1)S(1)}, bf16[224,512]{1,0:T(8,128)(2,1)S(1)}, u32[]{:S(2)}, u32[]{:S(2)}) collective-permute-start(bf16[224,512]{1,0:T(8,128)(2,1)S(1)} %dynamic-slice_bitcast_fusion.3), channel_id=1, source_target_pairs={{0,8},{8,0},{1,9},{9,1},{2,10},{10,2},{3,11},{11,3},{4,12},{12,4},... | collective-permute-start | bytes 688136 | tf_op jit(solution)/shard_map/ppermute | solution.py:30
  171.8 4.6 %collective-permute-done.4 = bf16[224,512]{1,0:T(8,128)(2,1)S(1)} collective-permute-done((bf16[224,512]{1,0:T(8,128)(2,1)S(1)}, bf16[224,512]{1,0:T(8,128)(2,1)S(1)}, u32[]{:S(2)}, u32[]{:S(2)}) %collective-permute-start.4) | collective-permute-done | bytes 229408 | tf_op jit(solution)/shard_map/ppermute | solution.py:30
  176.4 0.7 fusion.17
  177.2 15.4 %all-to-all-done.2 = bf16[16,56,256]{2,1,0:T(8,128)(2,1)S(1)} async-done(((bf16[16,56,256]{2,1,0:T(8,128)(2,1)}), bf16[16,56,256]{2,1,0:T(8,128)(2,1)S(1)}, u32[]{:S(2)}, u32[]{:S(2)}) %all-to-all-start.2) | async-done | bytes 458784 | tf_op jit(solution)/shard_map/all_to_all | solution.py:40
  (20 shorter events, 3.3 us)
Async XLA Ops:
  57.4 28.3 %all-to-all-start = ((bf16[4,896,384]{2,1,0:T(8,128)(2,1)}), bf16[4,896,384]{2,1,0:T(8,128)(2,1)S(1)}, u32[]{:S(2)}, u32[]{:S(2)}) async-start(bf16[4,896,384]{2,1,0:T(8,128)(2,1)} %broadcast_in_dim.26), calls=%async_computation | async-start | bytes 5505024 | tf_op jit(solution)/shard_map/all_to_all | solution.py:62
  67.7 4.2 %copy-start.5 = (f32[512]{0:T(512)S(1)}, f32[512]{0:T(512)}, u32[]{:S(2)}) copy-start(f32[512]{0:T(512)} %param.11) | copy-start | bytes 6148
  67.7 4.2 %copy-start.4 = (s32[512]{0:T(512)S(1)}, s32[512]{0:T(512)}, u32[]{:S(2)}) copy-start(s32[512]{0:T(512)} %param.10) | copy-start | bytes 6148
  85.8 1.6 copy-start
  87.3 2.9 %copy-start.1 = (bf16[512,3584]{1,0:T(8,128)(2,1)S(1)}, bf16[512,3584]{1,0:T(8,128)(2,1)}, u32[]{:S(2)}) copy-start(bf16[512,3584]{1,0:T(8,128)(2,1)} %param.8) | copy-start | bytes 11010052
  90.2 2.0 %copy-start.6 = (bf16[512,3584]{1,0:T(8,128)(2,1)S(1)}, bf16[512,3584]{1,0:T(8,128)(2,1)}, u32[]{:S(2)}) copy-start(bf16[512,3584]{1,0:T(8,128)(2,1)} %param.9) | copy-start | bytes 11010052
  92.2 2.0 %copy-start.2 = (bf16[2,2,16,56,512]{4,3,2,1,0:T(8,128)(2,1)S(1)}, bf16[2,2,16,56,512]{4,3,2,1,0:T(8,128)(2,1)}, u32[]{:S(2)}) copy-start(bf16[2,2,16,56,512]{4,3,2,1,0:T(8,128)(2,1)} %copy.26) | copy-start | bytes 11010052
  96.6 25.6 %all-to-all-start.1 = ((bf16[4,16,56,256]{3,2,1,0:T(8,128)(2,1)}), bf16[4,16,56,256]{3,2,1,0:T(8,128)(2,1)}, u32[]{:S(2)}, u32[]{:S(2)}) async-start(bf16[4,16,56,256]{3,2,1,0:T(8,128)(2,1)} %bitcast.61), calls=%async_computation.1 | async-start | bytes 3670016 | tf_op jit(solution)/shard_map/all_to_all | solution.py:82
  102.6 5.7 %collective-permute-start = (bf16[2,4,224,512]{3,2,0,1:T(8,128)(2,1)S(1)}, bf16[2,4,224,512]{3,2,0,1:T(8,128)(2,1)S(1)}, u32[]{:S(2)}, u32[]{:S(2)}) collective-permute-start(bf16[2,4,224,512]{3,2,0,1:T(8,128)(2,1)S(1)} %bitcast.62), channel_id=1, source_target_pairs={{0,1},{1,0},{2,3},{3,2},{4,5},{5,4},{6,7},{7,6},{8,9},{9,8},{10,11... | collective-permute-start | bytes 5505032 | tf_op jit(solution)/shard_map/ppermute | solution.py:30
  124.7 67.8 %all-to-all-start.2 = ((bf16[16,56,256]{2,1,0:T(8,128)(2,1)}), bf16[16,56,256]{2,1,0:T(8,128)(2,1)S(1)}, u32[]{:S(2)}, u32[]{:S(2)}) async-start(bf16[16,56,256]{2,1,0:T(8,128)(2,1)} %fusion.12), calls=%async_computation.2 | async-start | bytes 917504 | tf_op jit(solution)/shard_map/all_to_all | solution.py:40
  138.4 15.5 %collective-permute-start.1 = (bf16[2,224,512]{2,1,0:T(8,128)(2,1)}, bf16[2,224,512]{2,1,0:T(8,128)(2,1)S(1)}, u32[]{:S(2)}, u32[]{:S(2)}) collective-permute-start(bf16[2,224,512]{2,1,0:T(8,128)(2,1)} %get-tuple-element.11), channel_id=1, source_target_pairs={{0,2},{2,4},{4,6},{6,0},{1,3},{3,5},{5,7},{7,1},{8,10},{10,12},{12... | collective-permute-start | bytes 1376264 | tf_op jit(solution)/shard_map/ppermute | solution.py:30
  140.8 24.0 %collective-permute-start.2 = (bf16[2,224,512]{2,1,0:T(8,128)(2,1)}, bf16[2,224,512]{2,1,0:T(8,128)(2,1)S(1)}, u32[]{:S(2)}, u32[]{:S(2)}) collective-permute-start(bf16[2,224,512]{2,1,0:T(8,128)(2,1)} %get-tuple-element.13), channel_id=1, source_target_pairs={{0,6},{2,0},{4,2},{6,4},{1,7},{3,1},{5,3},{7,5},{8,14},{10,8},{12,... | collective-permute-start | bytes 1376264 | tf_op jit(solution)/shard_map/ppermute | solution.py:30
  144.3 21.3 %collective-permute-start.3 = (bf16[2,224,512]{2,1,0:T(8,128)(2,1)}, bf16[2,224,512]{2,1,0:T(8,128)(2,1)}, u32[]{:S(2)}, u32[]{:S(2)}) collective-permute-start(bf16[2,224,512]{2,1,0:T(8,128)(2,1)} %get-tuple-element.12), channel_id=1, source_target_pairs={{0,4},{2,6},{4,0},{6,2},{1,5},{3,7},{5,1},{7,3},{8,12},{10,14},{12... | collective-permute-start | bytes 1376264 | tf_op jit(solution)/shard_map/ppermute | solution.py:30
  164.8 0.8 copy-start.3
  167.0 9.4 %collective-permute-start.4 = (bf16[224,512]{1,0:T(8,128)(2,1)S(1)}, bf16[224,512]{1,0:T(8,128)(2,1)S(1)}, u32[]{:S(2)}, u32[]{:S(2)}) collective-permute-start(bf16[224,512]{1,0:T(8,128)(2,1)S(1)} %dynamic-slice_bitcast_fusion.3), channel_id=1, source_target_pairs={{0,8},{8,0},{1,9},{9,1},{2,10},{10,2},{3,11},{11,3},{4,12},{12,4},... | collective-permute-start | bytes 688136 | tf_op jit(solution)/shard_map/ppermute | solution.py:30

commit v3 on v2

--- a/solution.py
+++ b/solution.py
@@ -1,17 +1,25 @@
 import jax
 import jax.numpy as jnp
 from jax import lax
+from jax.experimental.layout import Layout, with_layout_constraint
 from jax.sharding import Mesh, PartitionSpec as P
 
 BLOCK = 128
-SIZES = {"side": 2, "far": 16, "near": 2, "wide": 2, "ring": 4, "core": 2}
-SIDE, FAR, NEAR, WIDE, RING, CORE = SIZES.values()
-DP = ("side", "far", "near")
+SIZES = {"side": 2, "far": 8, "mid": 2, "near": 2, "wide": 2, "ring": 4, "core": 2}
+SIDE, FAR, MID, NEAR, WIDE, RING, CORE = SIZES.values()
+DP = ("side", "far", "mid", "near")
+SECONDS = ("far", "mid")
 QUAD = ("side", "near")
+NEIGHBOURS = ("mid", "near")
+SWAP = [(0, 1), (1, 0)]
 EXPERT = ("wide", "ring", "core")
 
 ROWS_CONTRACT = (((0,), (0,)), ((), ()))
 COLS_CONTRACT = (((1,), (1,)), ((), ()))
+
+
+def row_major(array):
+    return with_layout_constraint(array, Layout(major_to_minor=(0, 1)))
 
 
 def summed(terms):
@@ -53,14 +61,31 @@
     carried = route_rows[:, None] == slots[None, :]
     token_gate = jnp.sum(jnp.where(carried, slot_gate[:, None], 0.0), axis=0)
 
+    side_index = lax.axis_index("side")
+    core_index = lax.axis_index("core")
+    half_features = feature_count // SIDE
+    half_slots = slot_count // CORE
+    sent_tokens = lax.dynamic_slice(
+        tokens,
+        (core_index * half_slots, (1 - side_index) * half_features),
+        (half_slots, half_features),
+    )
+    fetched_tokens = row_major(lax.ppermute(row_major(sent_tokens), "side", SWAP))
+
     owned = jnp.concatenate([gate_weight, up_weight, down_weight_t], axis=1)
-    far_rows = lax.all_gather(owned, "far", axis=0, tiled=True)
-    far_rows, early_tokens = lax.optimization_barrier((far_rows, tokens))
-    feature_rows = early_tokens.T.reshape(SIDE, FAR, NEAR, own_rows, slot_count)
-    feature_rows = lax.optimization_barrier(feature_rows.swapaxes(1, 2))
+    far_rows = lax.all_gather(owned, SECONDS, axis=0, tiled=True)
+    far_rows, fetched_tokens, early_tokens = lax.optimization_barrier(
+        (far_rows, fetched_tokens, tokens)
+    )
+    swapped_tokens = row_major(lax.ppermute(fetched_tokens, "core", SWAP))
+    kept_tokens = lax.dynamic_slice_in_dim(early_tokens, side_index * half_features, half_features, 1)
+    feature_rows = jnp.concatenate([kept_tokens, fetched_tokens, swapped_tokens], axis=0).T
+    feature_rows = feature_rows.reshape(FAR, MID * NEAR, own_rows, SIDE * slot_count)
+    feature_rows = lax.optimization_barrier(feature_rows.swapaxes(0, 1))
     quads = jnp.broadcast_to(far_rows[None], (SIDE * NEAR, *far_rows.shape))
     quads = lax.all_to_all(quads, QUAD, 0, 0, tiled=True)
-    panels = quads.reshape(SIDE, NEAR, FAR, own_rows, 3 * hidden_width)
+    quads, feature_rows = lax.optimization_barrier((quads, feature_rows))
+    panels = quads.reshape(SIDE, NEAR, FAR * MID, own_rows, 3 * hidden_width)
     panels = panels.swapaxes(1, 2).reshape(feature_count, 3 * hidden_width)
     both_panels = panels[:, : 2 * hidden_width]
     down_panel = panels[:, 2 * hidden_width :]
@@ -75,11 +100,16 @@
     grad_gate = hidden_grad * up_val * gate_sigmoid * (1.0 + gate_val * (1.0 - gate_sigmoid))
     grads = jnp.concatenate([grad_gate, grad_up], axis=1).astype(jnp.bfloat16)
 
+    turned = jnp.concatenate([grads[half_slots:], grads[:half_slots]], axis=0)
+    sent_grads = jnp.where(core_index == 0, grads, turned)
+    both_grads = jnp.concatenate([grads, lax.ppermute(sent_grads, "side", SWAP)], axis=0)
     weight_terms = jnp.dot(
-        feature_rows.reshape(feature_count, slot_count), grads, preferred_element_type=jnp.float32
+        feature_rows.reshape(half_features, SIDE * slot_count),
+        both_grads,
+        preferred_element_type=jnp.float32,
     ).astype(jnp.bfloat16)
-    by_quad = weight_terms.reshape(SIDE * NEAR, FAR, own_rows, 2 * hidden_width)
-    quad_terms = lax.all_to_all(by_quad, QUAD, 0, 0, tiled=True)
+    weight_terms = weight_terms.reshape(MID * NEAR, FAR, own_rows, 2 * hidden_width)
+    near_terms = lax.all_to_all(weight_terms, NEIGHBOURS, 0, 0, tiled=True)
 
     input_terms = lax.dot_general(
         both_panels, grads, COLS_CONTRACT, preferred_element_type=jnp.float32
@@ -87,10 +117,10 @@
     own_features = feature_count // (WIDE * RING * CORE)
     by_expert = input_terms.reshape(WIDE, RING, CORE, own_features, slot_count)
     core_sum = permuted_sum(by_expert, "core", 2).astype(jnp.bfloat16)
-    quad_terms, _ = lax.optimization_barrier((quad_terms, core_sum))
-    quad_sum = summed([quad_terms[i] for i in range(SIDE * NEAR)]).astype(jnp.bfloat16)
-    weight_share = exchanged_sum(quad_sum, "far")
-    grad_scale = float(SIDE * FAR * NEAR * slot_count) ** (-0.5)
+    near_terms, _ = lax.optimization_barrier((near_terms, core_sum))
+    near_sum = summed([near_terms[i] for i in range(MID * NEAR)]).astype(jnp.bfloat16)
+    weight_share = exchanged_sum(near_sum, "far")
+    grad_scale = float(SIDE * FAR * MID * NEAR * slot_count) ** (-0.5)
     weight_share = weight_share * grad_scale
     ring_sum = permuted_sum(core_sum, "ring", 1).astype(jnp.bfloat16)
     wide_sum = permuted_sum(ring_sum, "wide", 0).astype(jnp.bfloat16)

time: 194 us -> 190 us (0.979)
  waiting for transfers between devices: 68 us -> 49.3 us
  starting transfers between devices: 36.3 us -> 44.3 us
  other arithmetic: 6.15 us -> 9.25 us
  local copies, waits for them, and re-layouts: 20.9 us -> 23.9 us
    all_to_all x1, waiting for transfers between devices: 15.4 us -> 0.01 us  [exchanged_sum(): terms = lax.all_to_all(parts, axes, 0, 0, tiled=True)]
    ppermute x0 -> x3, starting transfers between devices: none -> 8.69 us  [the longest x1 3.4 us: local(): lax.ppermute(row_major(sent_tokens), 'side', SWAP)]
    all_to_all x1, waiting for transfers between devices: 13.6 us -> 5.16 us  [local(): quads = lax.all_to_all(quads, QUAD, 0, 0, tiled=True)]
    ppermute x0 -> x3, waiting for transfers between devices: none -> 5.01 us  [the longest x1 5.01 us: local(): lax.ppermute(sent_grads, 'side', SWAP)]
    dynamic_slice x0 -> x2, local copies, waits for them, and re-layouts: none -> 4.13 us  [the longest x1 2.88 us: local(): lax.dynamic_slice_in_dim(early_tokens, side_index * half_features, half_f...]
    concatenate x0 -> x2, other arithmetic: none -> 3.54 us  [the longest x1 3.52 us: local(): jnp.concatenate([kept_tokens, fetched_tokens, swapped_tokens], axis=0)]
    another operation x0 -> x1, local copies, waits for them, and re-layouts: none -> 2.22 us  [row_major(): return with_layout_constraint(array, Layout(major_to_minor=(0, 1)))]
    unnamed x14 -> x12, local copies, waits for them, and re-layouts: 4.54 us -> 2.6 us
  transfers between devices with their start and end apart: 8 -> 11, of which waited for: 7 -> 7; matrix products, arithmetic and copies ran while one was open for 8% -> 13% of each run, Pallas kernels for 0% -> 0%
where the time goes in v3:
time: 190 us; the launch traced here: 188 us
  blocking collectives  54.1 us (28%)
  waiting for transfers between devices  49.3 us (26%)
  starting transfers between devices  44.3 us (23%)
  local copies, waits for them, and re-layouts  23.9 us (13%)
  other arithmetic  9.25 us (5%)
  matrix products  5.83 us (3%)
    all_gather x1, blocking collectives, local(): far_rows = lax.all_gather(owned, SECONDS, axis=0, tiled=True)  54.1 us
    ppermute x5, waiting for transfers between devices, shifted_term(): lax.ppermute(sent, axis, [(i, (i + shift) % count) for i in range(count)])  25.8 us
    ppermute x5, starting transfers between devices, shifted_term(): lax.ppermute(sent, axis, [(i, (i + shift) % count) for i in range(count)])  15.5 us
    all_to_all x1, waiting for transfers between devices, local(): near_terms = lax.all_to_all(weight_terms, NEIGHBOURS, 0, 0, tiled=True)  13.4 us
    all_to_all x1, starting transfers between devices, exchanged_sum(): terms = lax.all_to_all(parts, axes, 0, 0, tiled=True)  12.2 us
    optimization_barrier x2, local copies, waits for them, and re-layouts, local(): lax.optimization_barrier((far_rows, fetched_tokens, tokens))  8.18 us
    all_to_all x1, waiting for transfers between devices, local(): quads = lax.all_to_all(quads, QUAD, 0, 0, tiled=True)  5.16 us
    ppermute x1, waiting for transfers between devices, local(): lax.ppermute(sent_grads, 'side', SWAP)  5.01 us
  transfers between devices with their start and end apart: 11, of which 7 were waited for; matrix products, arithmetic and copies ran while one was open for 13% of the time, Pallas kernels for 0%

profile of v3, /device:TPU:24, one launch (start us, length us, event | category | flops | bytes accessed | tf_op | source)
XLA Modules:
  0.0 188.3 jit_solution(9040287828223675367)
XLA Ops:
  0.6 1.2 dynamic_slice.33
  1.9 3.4 %collective-permute-start = (bf16[256,1792]{1,0:T(8,128)(2,1)S(1)}, bf16[256,1792]{1,0:T(8,128)(2,1)}, u32[]{:S(2)}, u32[]{:S(2)}) collective-permute-start(bf16[256,1792]{1,0:T(8,128)(2,1)S(1)} %dynamic_slice.33), channel_id=1, source_target_pairs={{0,512},{512,0},{1,513},{513,1},{2,514},{514,2},{3,515},{515,3},{4... | collective-permute-start | bytes 2752520 | tf_op jit(solution)/shard_map/ppermute | solution.py:73
  6.1 54.1 %all_gather.3 = bf16[896,384]{1,0:T(8,128)(2,1)S(1)} all-gather(bf16[56,384]{1,0:T(8,128)(2,1)S(1)} %pad_maximum_fusion.3), channel_id=1, replica_groups=mesh['side'=2,'far'=8,'mid'=2,'near'=2,'wide'=2,'ring'=4,'core'=2] {'far..., dimensions={0}, use_global_device_ids=true | all-gather | bytes 731136 | tf_op jit(solution)/shard_map/all_gather | solution.py:76
  60.2 1.8 broadcast_in_dim.26
  62.0 3.7 %all-to-all-start = ((bf16[4,896,384]{2,1,0:T(8,128)(2,1)}), bf16[4,896,384]{2,1,0:T(8,128)(2,1)S(1)}, u32[]{:S(2)}, u32[]{:S(2)}) async-start(bf16[4,896,384]{2,1,0:T(8,128)(2,1)} %broadcast_in_dim.26), calls=%async_computation | async-start | bytes 5505024 | tf_op jit(solution)/shard_map/all_to_all | solution.py:86
  65.6 1.9 %collective-permute-start.1 = (bf16[256,1792]{1,0:T(8,128)(2,1)}, bf16[256,1792]{1,0:T(8,128)(2,1)}, u32[]{:S(2)}, u32[]{:S(2)}) collective-permute-start(bf16[256,1792]{1,0:T(8,128)(2,1)} %collective-permute-done), channel_id=1, source_target_pairs={{0,1},{1,0},{2,3},{3,2},{4,5},{5,4},{6,7},{7,6},{8,9},{9,8},{10,11... | collective-permute-start | bytes 2752520 | tf_op jit(solution)/shard_map/ppermute | solution.py:80
  68.5 2.3 %copy.27 = bf16[256,1792]{0,1:T(8,128)(2,1)} copy(bf16[256,1792]{1,0:T(8,128)(2,1)} %collective-permute-done) | data formatting | bytes 1835008 | tf_op jit(solution)/shard_map/optimization_barrier | solution.py:77
  70.7 5.9 %copy.26 = bf16[512,3584]{0,1:T(8,128)(2,1)} copy(bf16[512,3584]{1,0:T(8,128)(2,1)} %param.8) | data formatting | bytes 7340032 | tf_op jit(solution)/shard_map/optimization_barrier | solution.py:77
  76.7 2.9 %constant_dynamic-slice_fusion.2 = bf16[512,1792]{0,1:T(8,128)(2,1)} fusion(bf16[512,3584]{0,1:T(8,128)(2,1)} %copy.26, s32[]{:T(128)S(6)} %select_n.94), kind=kLoop, calls=%fused_computation.56 | loop fusion | bytes 3670020 | tf_op jit(solution)/shard_map/dynamic_slice | solution.py:81
  79.5 2.2 %copy.28 = bf16[256,1792]{0,1:T(8,128)(2,1)} copy(bf16[256,1792]{1,0:T(8,128)(2,1)} %collective-permute-done.1) | data formatting | bytes 1835008 | tf_op jit(solution)/shard_map/layout_constraint | solution.py:22
  81.8 3.5 %pad_maximum_fusion = bf16[1024,1792]{0,1:T(8,128)(2,1)} fusion(bf16[256,1792]{0,1:T(8,128)(2,1)} %copy.28, bf16[256,1792]{0,1:T(8,128)(2,1)} %copy.27, bf16[512,1792]{0,1:T(8,128)(2,1)} %constant_dynamic-slice_fusion.2), kind=kLoop, calls=%fused_computation.1 | loop fusion | flops 11010048 | bytes 7340032 | tf_op jit(solution)/shard_map/concatenate | solution.py:82
  85.3 5.2 %all-to-all-done = bf16[4,896,384]{2,1,0:T(8,128)(2,1)S(1)} async-done(((bf16[4,896,384]{2,1,0:T(8,128)(2,1)}), bf16[4,896,384]{2,1,0:T(8,128)(2,1)S(1)}, u32[]{:S(2)}, u32[]{:S(2)}) %all-to-all-start) | async-done | bytes 2752544 | tf_op jit(solution)/shard_map/all_to_all | solution.py:86
  90.4 1.6 copy-done.1
  92.0 2.2 %copy.29 = bf16[2,16,2,56,384]{4,3,2,1,0:T(8,128)(2,1)S(1)} copy(bf16[2,16,2,56,384]{4,3,1,2,0:T(8,128)(2,1)} %bitcast.54) | data formatting | bytes 5505024 | tf_op jit(solution)/shard_map/transpose | solution.py:89
  96.4 1.4 fusion.20
  97.9 3.4 %collective-permute-start.7 = (bf16[512,256]{0,1:T(8,128)(2,1)S(1)}, bf16[512,256]{0,1:T(8,128)(2,1)S(1)}, u32[]{:S(2)}, u32[]{:S(2)}) collective-permute-start(bf16[512,256]{0,1:T(8,128)(2,1)S(1)} %maximum_select_fusion), channel_id=1, source_target_pairs={{0,512},{512,0},{1,513},{513,1},{2,514},{514,2},{3,515},{515,3},{4... | collective-permute-start | bytes 786440 | tf_op jit(solution)/shard_map/ppermute | solution.py:105
  101.8 5.0 %collective-permute-done.7 = bf16[512,256]{0,1:T(8,128)(2,1)S(1)} collective-permute-done((bf16[512,256]{0,1:T(8,128)(2,1)S(1)}, bf16[512,256]{0,1:T(8,128)(2,1)S(1)}, u32[]{:S(2)}, u32[]{:S(2)}) %collective-permute-start.7) | collective-permute-done | bytes 262176 | tf_op jit(solution)/shard_map/ppermute | solution.py:105
  106.8 2.2 %convolution_convert_fusion.1 = bf16[1792,256]{1,0:T(8,128)(2,1)} fusion(bf16[1792,1024]{1,0:T(8,128)(2,1)S(1)} %bitcast.55, bf16[512,256]{0,1:T(8,128)(2,1)S(1)} %collective-permute-done.7, bf16[512,128]{0,1:T(8,128)(2,1)S(1)} %get-tuple-element.21, bf16[512,128]{0,1:T(8,128)(2,1)S(1)} %get-tuple-element.20), kind=kOutput, calls=%fused_computation.4 | convolution fusion | flops 941555712 | bytes 5111808 | tf_op jit(solution)/shard_map/dot_general | solution.py:106
  109.0 4.2 %all-to-all-start.1 = ((bf16[4,8,56,256]{3,2,1,0:T(8,128)(2,1)}), bf16[4,8,56,256]{3,2,1,0:T(8,128)(2,1)}, u32[]{:S(2)}, u32[]{:S(2)}) async-start(bf16[4,8,56,256]{3,2,1,0:T(8,128)(2,1)} %bitcast.57), calls=%async_computation.1 | async-start | bytes 1835008 | tf_op jit(solution)/shard_map/all_to_all | solution.py:112
  114.9 1.9 %collective-permute-start.2 = (bf16[2,4,224,512]{3,2,0,1:T(8,128)(2,1)S(1)}, bf16[2,4,224,512]{3,2,0,1:T(8,128)(2,1)S(1)}, u32[]{:S(2)}, u32[]{:S(2)}) collective-permute-start(bf16[2,4,224,512]{3,2,0,1:T(8,128)(2,1)S(1)} %bitcast.56), channel_id=1, source_target_pairs={{0,1},{1,0},{2,3},{3,2},{4,5},{5,4},{6,7},{7,6},{8,9},{9,8},{10,11... | collective-permute-start | bytes 5505032 | tf_op jit(solution)/shard_map/ppermute | solution.py:38
  116.8 3.8 %collective-permute-done.2 = bf16[2,4,224,512]{3,2,0,1:T(8,128)(2,1)S(1)} collective-permute-done((bf16[2,4,224,512]{3,2,0,1:T(8,128)(2,1)S(1)}, bf16[2,4,224,512]{3,2,0,1:T(8,128)(2,1)S(1)}, u32[]{:S(2)}, u32[]{:S(2)}) %collective-permute-start.2) | collective-permute-done | bytes 1835040 | tf_op jit(solution)/shard_map/ppermute | solution.py:38
  121.1 13.4 %all-to-all-done.1 = bf16[4,8,56,256]{3,2,1,0:T(8,128)(2,1)} async-done(((bf16[4,8,56,256]{3,2,1,0:T(8,128)(2,1)}), bf16[4,8,56,256]{3,2,1,0:T(8,128)(2,1)}, u32[]{:S(2)}, u32[]{:S(2)}) %all-to-all-start.1) | async-done | bytes 917536 | tf_op jit(solution)/shard_map/all_to_all | solution.py:112
  134.5 2.1 %fusion.21 = bf16[8,56,256]{2,1,0:T(8,128)(2,1)} fusion(bf16[4,8,56,256]{3,2,1,0:T(8,128)(2,1)} %all-to-all-done.1), kind=kLoop, calls=%fused_computation.43 | loop fusion | flops 917504 | bytes 1146880 | tf_op jit(solution)/shard_map/add | solution.py:28
  136.6 12.2 %all-to-all-start.2 = ((bf16[8,56,256]{2,1,0:T(8,128)(2,1)}), bf16[8,56,256]{2,1,0:T(8,128)(2,1)S(1)}, u32[]{:S(2)}, u32[]{:S(2)}) async-start(bf16[8,56,256]{2,1,0:T(8,128)(2,1)} %fusion.21), calls=%async_computation.2 | async-start | bytes 458752 | tf_op jit(solution)/shard_map/all_to_all | solution.py:48
  149.9 2.1 %collective-permute-start.3 = (bf16[2,224,512]{2,1,0:T(8,128)(2,1)}, bf16[2,224,512]{2,1,0:T(8,128)(2,1)S(1)}, u32[]{:S(2)}, u32[]{:S(2)}) collective-permute-start(bf16[2,224,512]{2,1,0:T(8,128)(2,1)} %get-tuple-element.17), channel_id=1, source_target_pairs={{0,2},{2,4},{4,6},{6,0},{1,3},{3,5},{5,7},{7,1},{8,10},{10,12},{12... | collective-permute-start | bytes 1376264 | tf_op jit(solution)/shard_map/ppermute | solution.py:38
  152.0 3.7 %collective-permute-start.4 = (bf16[2,224,512]{2,1,0:T(8,128)(2,1)}, bf16[2,224,512]{2,1,0:T(8,128)(2,1)S(1)}, u32[]{:S(2)}, u32[]{:S(2)}) collective-permute-start(bf16[2,224,512]{2,1,0:T(8,128)(2,1)} %get-tuple-element.19), channel_id=1, source_target_pairs={{0,6},{2,0},{4,2},{6,4},{1,7},{3,1},{5,3},{7,5},{8,14},{10,8},{12,... | collective-permute-start | bytes 1376264 | tf_op jit(solution)/shard_map/ppermute | solution.py:38
  155.8 3.1 %collective-permute-start.5 = (bf16[2,224,512]{2,1,0:T(8,128)(2,1)S(1)}, bf16[2,224,512]{2,1,0:T(8,128)(2,1)}, u32[]{:S(2)}, u32[]{:S(2)}) collective-permute-start(bf16[2,224,512]{2,1,0:T(8,128)(2,1)S(1)} %get-tuple-element.18), channel_id=1, source_target_pairs={{0,4},{2,6},{4,0},{6,2},{1,5},{3,7},{5,1},{7,3},{8,12},{10,14},{12... | collective-permute-start | bytes 1376264 | tf_op jit(solution)/shard_map/ppermute | solution.py:38
  158.9 6.5 %collective-permute-done.3 = bf16[2,224,512]{2,1,0:T(8,128)(2,1)S(1)} collective-permute-done((bf16[2,224,512]{2,1,0:T(8,128)(2,1)}, bf16[2,224,512]{2,1,0:T(8,128)(2,1)S(1)}, u32[]{:S(2)}, u32[]{:S(2)}) %collective-permute-start.3) | collective-permute-done | bytes 458784 | tf_op jit(solution)/shard_map/ppermute | solution.py:38
  165.5 10.7 %collective-permute-done.4 = bf16[2,224,512]{2,1,0:T(8,128)(2,1)S(1)} collective-permute-done((bf16[2,224,512]{2,1,0:T(8,128)(2,1)}, bf16[2,224,512]{2,1,0:T(8,128)(2,1)S(1)}, u32[]{:S(2)}, u32[]{:S(2)}) %collective-permute-start.4) | collective-permute-done | bytes 458784 | tf_op jit(solution)/shard_map/ppermute | solution.py:38
  176.2 1.3 fusion.11
  177.5 4.6 %collective-permute-start.6 = (bf16[224,512]{1,0:T(8,128)(2,1)S(1)}, bf16[224,512]{1,0:T(8,128)(2,1)S(1)}, u32[]{:S(2)}, u32[]{:S(2)}) collective-permute-start(bf16[224,512]{1,0:T(8,128)(2,1)S(1)} %dynamic-slice_bitcast_fusion.3), channel_id=1, source_target_pairs={{0,8},{8,0},{1,9},{9,1},{2,10},{10,2},{3,11},{11,3},{4,12},{12,4},... | collective-permute-start | bytes 688136 | tf_op jit(solution)/shard_map/ppermute | solution.py:38
  182.1 4.8 %collective-permute-done.6 = bf16[224,512]{1,0:T(8,128)(2,1)S(1)} collective-permute-done((bf16[224,512]{1,0:T(8,128)(2,1)S(1)}, bf16[224,512]{1,0:T(8,128)(2,1)S(1)}, u32[]{:S(2)}, u32[]{:S(2)}) %collective-permute-start.6) | collective-permute-done | bytes 229408 | tf_op jit(solution)/shard_map/ppermute | solution.py:38
  (31 shorter events, 8.5 us)
Async XLA Ops:
  1.9 58.3 %collective-permute-start = (bf16[256,1792]{1,0:T(8,128)(2,1)S(1)}, bf16[256,1792]{1,0:T(8,128)(2,1)}, u32[]{:S(2)}, u32[]{:S(2)}) collective-permute-start(bf16[256,1792]{1,0:T(8,128)(2,1)S(1)} %dynamic_slice.33), channel_id=1, source_target_pairs={{0,512},{512,0},{1,513},{513,1},{2,514},{514,2},{3,515},{515,3},{4... | collective-permute-start | bytes 2752520 | tf_op jit(solution)/shard_map/ppermute | solution.py:73
  60.2 8.1 %copy-start.4 = (f32[512]{0:T(512)S(1)}, f32[512]{0:T(512)}, u32[]{:S(2)}) copy-start(f32[512]{0:T(512)} %param.11) | copy-start | bytes 6148
  60.2 8.1 %copy-start.3 = (s32[512]{0:T(512)S(1)}, s32[512]{0:T(512)}, u32[]{:S(2)}) copy-start(s32[512]{0:T(512)} %param.10) | copy-start | bytes 6148
  62.0 28.5 %all-to-all-start = ((bf16[4,896,384]{2,1,0:T(8,128)(2,1)}), bf16[4,896,384]{2,1,0:T(8,128)(2,1)S(1)}, u32[]{:S(2)}, u32[]{:S(2)}) async-start(bf16[4,896,384]{2,1,0:T(8,128)(2,1)} %broadcast_in_dim.26), calls=%async_computation | async-start | bytes 5505024 | tf_op jit(solution)/shard_map/all_to_all | solution.py:86
  65.6 13.9 %collective-permute-start.1 = (bf16[256,1792]{1,0:T(8,128)(2,1)}, bf16[256,1792]{1,0:T(8,128)(2,1)}, u32[]{:S(2)}, u32[]{:S(2)}) collective-permute-start(bf16[256,1792]{1,0:T(8,128)(2,1)} %collective-permute-done), channel_id=1, source_target_pairs={{0,1},{1,0},{2,3},{3,2},{4,5},{5,4},{6,7},{7,6},{8,9},{9,8},{10,11... | collective-permute-start | bytes 2752520 | tf_op jit(solution)/shard_map/ppermute | solution.py:80
  90.4 1.6 copy-start.1
  92.0 2.9 %copy-start.2 = (bf16[512,3584]{1,0:T(8,128)(2,1)S(1)}, bf16[512,3584]{1,0:T(8,128)(2,1)}, u32[]{:S(2)}) copy-start(bf16[512,3584]{1,0:T(8,128)(2,1)} %param.8) | copy-start | bytes 11010052
  94.2 2.2 %copy-start.5 = (bf16[512,3584]{1,0:T(8,128)(2,1)S(1)}, bf16[512,3584]{1,0:T(8,128)(2,1)}, u32[]{:S(2)}) copy-start(bf16[512,3584]{1,0:T(8,128)(2,1)} %param.9) | copy-start | bytes 11010052
  96.4 4.9 %copy-start = (bf16[1024,1792]{0,1:T(8,128)(2,1)S(1)}, bf16[1024,1792]{0,1:T(8,128)(2,1)}, u32[]{:S(2)}) copy-start(bf16[1024,1792]{0,1:T(8,128)(2,1)} %pad_maximum_fusion) | copy-start | bytes 11010052
  97.9 8.9 %collective-permute-start.7 = (bf16[512,256]{0,1:T(8,128)(2,1)S(1)}, bf16[512,256]{0,1:T(8,128)(2,1)S(1)}, u32[]{:S(2)}, u32[]{:S(2)}) collective-permute-start(bf16[512,256]{0,1:T(8,128)(2,1)S(1)} %maximum_select_fusion), channel_id=1, source_target_pairs={{0,512},{512,0},{1,513},{513,1},{2,514},{514,2},{3,515},{515,3},{4... | collective-permute-start | bytes 786440 | tf_op jit(solution)/shard_map/ppermute | solution.py:105
  109.0 25.5 %all-to-all-start.1 = ((bf16[4,8,56,256]{3,2,1,0:T(8,128)(2,1)}), bf16[4,8,56,256]{3,2,1,0:T(8,128)(2,1)}, u32[]{:S(2)}, u32[]{:S(2)}) async-start(bf16[4,8,56,256]{3,2,1,0:T(8,128)(2,1)} %bitcast.57), calls=%async_computation.1 | async-start | bytes 1835008 | tf_op jit(solution)/shard_map/all_to_all | solution.py:112
  114.9 5.7 %collective-permute-start.2 = (bf16[2,4,224,512]{3,2,0,1:T(8,128)(2,1)S(1)}, bf16[2,4,224,512]{3,2,0,1:T(8,128)(2,1)S(1)}, u32[]{:S(2)}, u32[]{:S(2)}) collective-permute-start(bf16[2,4,224,512]{3,2,0,1:T(8,128)(2,1)S(1)} %bitcast.56), channel_id=1, source_target_pairs={{0,1},{1,0},{2,3},{3,2},{4,5},{5,4},{6,7},{7,6},{8,9},{9,8},{10,11... | collective-permute-start | bytes 5505032 | tf_op jit(solution)/shard_map/ppermute | solution.py:38
  136.6 51.0 %all-to-all-start.2 = ((bf16[8,56,256]{2,1,0:T(8,128)(2,1)}), bf16[8,56,256]{2,1,0:T(8,128)(2,1)S(1)}, u32[]{:S(2)}, u32[]{:S(2)}) async-start(bf16[8,56,256]{2,1,0:T(8,128)(2,1)} %fusion.21), calls=%async_computation.2 | async-start | bytes 458752 | tf_op jit(solution)/shard_map/all_to_all | solution.py:48
  149.9 15.5 %collective-permute-start.3 = (bf16[2,224,512]{2,1,0:T(8,128)(2,1)}, bf16[2,224,512]{2,1,0:T(8,128)(2,1)S(1)}, u32[]{:S(2)}, u32[]{:S(2)}) collective-permute-start(bf16[2,224,512]{2,1,0:T(8,128)(2,1)} %get-tuple-element.17), channel_id=1, source_target_pairs={{0,2},{2,4},{4,6},{6,0},{1,3},{3,5},{5,7},{7,1},{8,10},{10,12},{12... | collective-permute-start | bytes 1376264 | tf_op jit(solution)/shard_map/ppermute | solution.py:38
  152.0 24.1 %collective-permute-start.4 = (bf16[2,224,512]{2,1,0:T(8,128)(2,1)}, bf16[2,224,512]{2,1,0:T(8,128)(2,1)S(1)}, u32[]{:S(2)}, u32[]{:S(2)}) collective-permute-start(bf16[2,224,512]{2,1,0:T(8,128)(2,1)} %get-tuple-element.19), channel_id=1, source_target_pairs={{0,6},{2,0},{4,2},{6,4},{1,7},{3,1},{5,3},{7,5},{8,14},{10,8},{12,... | collective-permute-start | bytes 1376264 | tf_op jit(solution)/shard_map/ppermute | solution.py:38
  155.8 20.4 %collective-permute-start.5 = (bf16[2,224,512]{2,1,0:T(8,128)(2,1)S(1)}, bf16[2,224,512]{2,1,0:T(8,128)(2,1)}, u32[]{:S(2)}, u32[]{:S(2)}) collective-permute-start(bf16[2,224,512]{2,1,0:T(8,128)(2,1)S(1)} %get-tuple-element.18), channel_id=1, source_target_pairs={{0,4},{2,6},{4,0},{6,2},{1,5},{3,7},{5,1},{7,3},{8,12},{10,14},{12... | collective-permute-start | bytes 1376264 | tf_op jit(solution)/shard_map/ppermute | solution.py:38
  177.5 9.4 %collective-permute-start.6 = (bf16[224,512]{1,0:T(8,128)(2,1)S(1)}, bf16[224,512]{1,0:T(8,128)(2,1)S(1)}, u32[]{:S(2)}, u32[]{:S(2)}) collective-permute-start(bf16[224,512]{1,0:T(8,128)(2,1)S(1)} %dynamic-slice_bitcast_fusion.3), channel_id=1, source_target_pairs={{0,8},{8,0},{1,9},{9,1},{2,10},{10,2},{3,11},{11,3},{4,12},{12,4},... | collective-permute-start | bytes 688136 | tf_op jit(solution)/shard_map/ppermute | solution.py:38

commit v4 on v3

--- a/solution.py
+++ b/solution.py
@@ -29,19 +29,13 @@
     return total
 
 
-def shifted_term(parts, axis, dim, shift):
-    count = SIZES[axis]
-    index = lax.axis_index(axis)
-    sent = lax.dynamic_index_in_dim(parts, (index + shift) % count, dim, keepdims=False)
-    if shift == 0:
-        return sent
-    return lax.ppermute(sent, axis, [(i, (i + shift) % count) for i in range(count)])
+def part_for(parts, axis, dim, shift):
+    index = (lax.axis_index(axis) + shift) % SIZES[axis]
+    return lax.dynamic_index_in_dim(parts, index, dim, keepdims=False)
 
 
-def permuted_sum(parts, axis, dim):
-    shifts = [0, 1, SIZES[axis] - 1] + list(range(2, SIZES[axis] - 1))
-    shifts = shifts[: SIZES[axis]]
-    return summed([shifted_term(parts, axis, dim, shift) for shift in shifts])
+def moved(part, axis, shift):
+    return lax.ppermute(part, axis, [(i, (i + shift) % SIZES[axis]) for i in range(SIZES[axis])])
 
 
 def exchanged_sum(parts, axes):
@@ -102,7 +96,18 @@
 
     turned = jnp.concatenate([grads[half_slots:], grads[:half_slots]], axis=0)
     sent_grads = jnp.where(core_index == 0, grads, turned)
-    both_grads = jnp.concatenate([grads, lax.ppermute(sent_grads, "side", SWAP)], axis=0)
+    partner_grads = lax.ppermute(sent_grads, "side", SWAP)
+
+    input_terms = lax.dot_general(
+        both_panels, grads, COLS_CONTRACT, preferred_element_type=jnp.float32
+    ).astype(jnp.bfloat16)
+    own_features = feature_count // (WIDE * RING * CORE)
+    by_expert = input_terms.reshape(WIDE, RING, CORE, own_features, slot_count)
+    core_sent = part_for(by_expert, "core", 2, 1)
+    core_terms = [part_for(by_expert, "core", 2, 0), moved(core_sent, "core", 1)]
+
+    partner_grads, _ = lax.optimization_barrier((partner_grads, core_sent))
+    both_grads = jnp.concatenate([grads, partner_grads], axis=0)
     weight_terms = jnp.dot(
         feature_rows.reshape(half_features, SIDE * slot_count),
         both_grads,
@@ -111,20 +116,19 @@
     weight_terms = weight_terms.reshape(MID * NEAR, FAR, own_rows, 2 * hidden_width)
     near_terms = lax.all_to_all(weight_terms, NEIGHBOURS, 0, 0, tiled=True)
 
-    input_terms = lax.dot_general(
-        both_panels, grads, COLS_CONTRACT, preferred_element_type=jnp.float32
-    ).astype(jnp.bfloat16)
-    own_features = feature_count // (WIDE * RING * CORE)
-    by_expert = input_terms.reshape(WIDE, RING, CORE, own_features, slot_count)
-    core_sum = permuted_sum(by_expert, "core", 2).astype(jnp.bfloat16)
-    near_terms, _ = lax.optimization_barrier((near_terms, core_sum))
+    core_sum = summed(core_terms).astype(jnp.bfloat16)
+    ring_terms = [part_for(core_sum, "ring", 1, 0)]
+    for shift in (1, RING - 1, 2):
+        ring_terms.append(moved(part_for(core_sum, "ring", 1, shift), "ring", shift))
+    near_terms, ring_terms = lax.optimization_barrier((near_terms, ring_terms))
     near_sum = summed([near_terms[i] for i in range(MID * NEAR)]).astype(jnp.bfloat16)
     weight_share = exchanged_sum(near_sum, "far")
+
+    ring_sum = summed(ring_terms).astype(jnp.bfloat16)
+    wide_terms = [part_for(ring_sum, "wide", 0, 0), moved(part_for(ring_sum, "wide", 0, 1), "wide", 1)]
+    grad_tokens = summed(wide_terms).astype(jnp.bfloat16).T
     grad_scale = float(SIDE * FAR * MID * NEAR * slot_count) ** (-0.5)
     weight_share = weight_share * grad_scale
-    ring_sum = permuted_sum(core_sum, "ring", 1).astype(jnp.bfloat16)
-    wide_sum = permuted_sum(ring_sum, "wide", 0).astype(jnp.bfloat16)
-    grad_tokens = wide_sum.T
     return grad_tokens, weight_share[:, :hidden_width], weight_share[:, hidden_width:]
 
 

time: 190 us -> 198 us (1.042)
  the two profiles are of different devices: /device:TPU:24 before, /device:TPU:40 now
where the time goes in v4:
time: 198 us; the launch traced here: 197 us
  waiting for transfers between devices  60.1 us (30%)
  blocking collectives  50.6 us (26%)
  starting transfers between devices  48.8 us (25%)
  local copies, waits for them, and re-layouts  21.1 us (11%)
  other arithmetic  8.97 us (5%)
  matrix products  5.78 us (3%)
    all_gather x1, blocking collectives, local(): far_rows = lax.all_gather(owned, SECONDS, axis=0, tiled=True)  50.6 us
    ppermute x5, waiting for transfers between devices, moved(): lax.ppermute(part, axis, [(i, (i + shift) % SIZES[axis]) for i in range(S...  26.9 us
    all_to_all x1, waiting for transfers between devices, exchanged_sum(): terms = lax.all_to_all(parts, axes, 0, 0, tiled=True)  25.8 us
    ppermute x5, starting transfers between devices, moved(): lax.ppermute(part, axis, [(i, (i + shift) % SIZES[axis]) for i in range(S...  16.6 us
    all_to_all x1, starting transfers between devices, exchanged_sum(): terms = lax.all_to_all(parts, axes, 0, 0, tiled=True)  12.1 us
    optimization_barrier x2, local copies, waits for them, and re-layouts, local(): lax.optimization_barrier((far_rows, fetched_tokens, tokens))  8.16 us
    all_to_all x1, starting transfers between devices, local(): quads = lax.all_to_all(quads, QUAD, 0, 0, tiled=True)  7.3 us
    all_to_all x1, starting transfers between devices, local(): near_terms = lax.all_to_all(weight_terms, NEIGHBOURS, 0, 0, tiled=True)  4.77 us
  transfers between devices with their start and end apart: 11, of which 8 were waited for; matrix products, arithmetic and copies ran while one was open for 12% of the time, Pallas kernels for 0%

profile of v4, /device:TPU:40, one launch (start us, length us, event | category | flops | bytes accessed | tf_op | source)
XLA Modules:
  0.0 196.8 jit_solution(16500600864695490138)
XLA Ops:
  0.6 1.2 dynamic_slice.33
  1.9 3.4 %collective-permute-start = (bf16[256,1792]{1,0:T(8,128)(2,1)S(1)}, bf16[256,1792]{1,0:T(8,128)(2,1)}, u32[]{:S(2)}, u32[]{:S(2)}) collective-permute-start(bf16[256,1792]{1,0:T(8,128)(2,1)S(1)} %dynamic_slice.33), channel_id=1, source_target_pairs={{0,512},{512,0},{1,513},{513,1},{2,514},{514,2},{3,515},{515,3},{4... | collective-permute-start | bytes 2752520 | tf_op jit(solution)/shard_map/ppermute | solution.py:67
  6.1 50.6 %all_gather.3 = bf16[896,384]{1,0:T(8,128)(2,1)S(1)} all-gather(bf16[56,384]{1,0:T(8,128)(2,1)S(1)} %pad_maximum_fusion.3), channel_id=1, replica_groups=mesh['side'=2,'far'=8,'mid'=2,'near'=2,'wide'=2,'ring'=4,'core'=2] {'far..., dimensions={0}, use_global_device_ids=true | all-gather | bytes 731136 | tf_op jit(solution)/shard_map/all_gather | solution.py:70
  56.6 1.8 broadcast_in_dim.26
  58.4 7.3 %all-to-all-start = ((bf16[4,896,384]{2,1,0:T(8,128)(2,1)}), bf16[4,896,384]{2,1,0:T(8,128)(2,1)S(1)}, u32[]{:S(2)}, u32[]{:S(2)}) async-start(bf16[4,896,384]{2,1,0:T(8,128)(2,1)} %broadcast_in_dim.26), calls=%async_computation | async-start | bytes 5505024 | tf_op jit(solution)/shard_map/all_to_all | solution.py:80
  65.7 1.9 collective-permute-start.1
  68.5 2.2 %copy.21 = bf16[256,1792]{0,1:T(8,128)(2,1)} copy(bf16[256,1792]{1,0:T(8,128)(2,1)} %collective-permute-done) | data formatting | bytes 1835008 | tf_op jit(solution)/shard_map/optimization_barrier | solution.py:71
  70.8 5.9 %copy.20 = bf16[512,3584]{0,1:T(8,128)(2,1)} copy(bf16[512,3584]{1,0:T(8,128)(2,1)} %param.8) | data formatting | bytes 7340032 | tf_op jit(solution)/shard_map/optimization_barrier | solution.py:71
  76.7 2.9 %constant_dynamic-slice_fusion = bf16[512,1792]{0,1:T(8,128)(2,1)} fusion(bf16[512,3584]{0,1:T(8,128)(2,1)} %copy.20, s32[]{:T(128)S(6)} %select_n.94), kind=kLoop, calls=%fused_computation.51 | loop fusion | bytes 3670020 | tf_op jit(solution)/shard_map/dynamic_slice | solution.py:75
  79.6 2.2 %copy.22 = bf16[256,1792]{0,1:T(8,128)(2,1)} copy(bf16[256,1792]{1,0:T(8,128)(2,1)} %collective-permute-done.1) | data formatting | bytes 1835008 | tf_op jit(solution)/shard_map/layout_constraint | solution.py:22
  81.8 3.5 %pad_maximum_fusion = bf16[1024,1792]{0,1:T(8,128)(2,1)} fusion(bf16[256,1792]{0,1:T(8,128)(2,1)} %copy.22, bf16[256,1792]{0,1:T(8,128)(2,1)} %copy.21, bf16[512,1792]{0,1:T(8,128)(2,1)} %constant_dynamic-slice_fusion), kind=kLoop, calls=%fused_computation.1 | loop fusion | flops 11010048 | bytes 7340032 | tf_op jit(solution)/shard_map/concatenate | solution.py:76
  85.3 4.6 %all-to-all-done = bf16[4,896,384]{2,1,0:T(8,128)(2,1)S(1)} async-done(((bf16[4,896,384]{2,1,0:T(8,128)(2,1)}), bf16[4,896,384]{2,1,0:T(8,128)(2,1)S(1)}, u32[]{:S(2)}, u32[]{:S(2)}) %all-to-all-start) | async-done | bytes 2752544 | tf_op jit(solution)/shard_map/all_to_all | solution.py:80
  90.2 1.7 copy-done.2
  93.1 1.4 multiply_convert_fusion
  94.6 2.7 %collective-permute-start.2 = (bf16[512,256]{0,1:T(8,128)(2,1)S(1)}, bf16[512,256]{0,1:T(8,128)(2,1)S(1)}, u32[]{:S(2)}, u32[]{:S(2)}) collective-permute-start(bf16[512,256]{0,1:T(8,128)(2,1)S(1)} %maximum_select_fusion), channel_id=1, source_target_pairs={{0,512},{512,0},{1,513},{513,1},{2,514},{514,2},{3,515},{515,3},{4... | collective-permute-start | bytes 786440 | tf_op jit(solution)/shard_map/ppermute | solution.py:99
  99.0 1.3 copy-done
  100.5 2.7 %collective-permute-done.2 = bf16[512,256]{0,1:T(8,128)(2,1)S(1)} collective-permute-done((bf16[512,256]{0,1:T(8,128)(2,1)S(1)}, bf16[512,256]{0,1:T(8,128)(2,1)S(1)}, u32[]{:S(2)}, u32[]{:S(2)}) %collective-permute-start.2) | collective-permute-done | bytes 262176 | tf_op jit(solution)/shard_map/ppermute | solution.py:99
  103.2 2.1 %convolution_convert_fusion.1 = bf16[1792,256]{1,0:T(8,128)(2,1)} fusion(bf16[1792,1024]{1,0:T(8,128)(2,1)S(1)} %bitcast.52, bf16[512,256]{0,1:T(8,128)(2,1)S(1)} %collective-permute-done.2, bf16[512,128]{0,1:T(8,128)(2,1)S(1)} %get-tuple-element.29, bf16[512,128]{0,1:T(8,128)(2,1)S(1)} %get-tuple-element.30), kind=kOutput, calls=%fused_computation.4 | convolution fusion | flops 941555712 | bytes 5111808 | tf_op jit(solution)/shard_map/dot_general | solution.py:111
  105.3 4.8 %all-to-all-start.1 = ((bf16[4,8,56,256]{3,2,1,0:T(8,128)(2,1)}), bf16[4,8,56,256]{3,2,1,0:T(8,128)(2,1)S(1)}, u32[]{:S(2)}, u32[]{:S(2)}) async-start(bf16[4,8,56,256]{3,2,1,0:T(8,128)(2,1)} %bitcast.53), calls=%async_computation.1 | async-start | bytes 1835008 | tf_op jit(solution)/shard_map/all_to_all | solution.py:117
  110.1 1.9 collective-permute-start.3
  112.1 3.8 %collective-permute-done.3 = bf16[2,4,224,512]{3,2,1,0:T(8,128)(2,1)} collective-permute-done((bf16[2,4,224,512]{3,2,1,0:T(8,128)(2,1)S(1)}, bf16[2,4,224,512]{3,2,1,0:T(8,128)(2,1)}, u32[]{:S(2)}, u32[]{:S(2)}) %collective-permute-start.3) | collective-permute-done | bytes 1835040 | tf_op jit(solution)/shard_map/ppermute | solution.py:38
  115.9 2.6 %fusion = bf16[2,4,224,512]{3,2,1,0:T(8,128)(2,1)S(1)} fusion(bf16[2,4,224,512]{3,2,1,0:T(8,128)(2,1)} %collective-permute-done.3, bf16[2,4,2,224,512]{4,3,2,1,0:T(8,128)(2,1)} %bitcast.46, s32[]{:T(128)S(6)} %select_n.103), kind=kLoop, calls=%fused_computation.3 | loop fusion | flops 3670016 | bytes 5505028 | tf_op jit(solution)/shard_map/convert_element_type | solution.py:119
  118.6 3.5 %collective-permute-start.4 = (bf16[2,224,512]{2,1,0:T(8,128)(2,1)S(1)}, bf16[2,224,512]{2,1,0:T(8,128)(2,1)S(1)}, u32[]{:S(2)}, u32[]{:S(2)}) collective-permute-start(bf16[2,224,512]{2,1,0:T(8,128)(2,1)S(1)} %get-tuple-element.27), channel_id=1, source_target_pairs={{0,2},{2,4},{4,6},{6,0},{1,3},{3,5},{5,7},{7,1},{8,10},{10,12},{12... | collective-permute-start | bytes 1376264 | tf_op jit(solution)/shard_map/ppermute | solution.py:38
  122.1 2.3 %collective-permute-start.5 = (bf16[2,224,512]{2,1,0:T(8,128)(2,1)S(1)}, bf16[2,224,512]{2,1,0:T(8,128)(2,1)S(1)}, u32[]{:S(2)}, u32[]{:S(2)}) collective-permute-start(bf16[2,224,512]{2,1,0:T(8,128)(2,1)S(1)} %get-tuple-element.26), channel_id=1, source_target_pairs={{0,6},{2,0},{4,2},{6,4},{1,7},{3,1},{5,3},{7,5},{8,14},{10,8},{12,... | collective-permute-start | bytes 1376264 | tf_op jit(solution)/shard_map/ppermute | solution.py:38
  124.5 4.2 %collective-permute-start.6 = (bf16[2,224,512]{2,1,0:T(8,128)(2,1)S(1)}, bf16[2,224,512]{2,1,0:T(8,128)(2,1)S(1)}, u32[]{:S(2)}, u32[]{:S(2)}) collective-permute-start(bf16[2,224,512]{2,1,0:T(8,128)(2,1)S(1)} %get-tuple-element.25), channel_id=1, source_target_pairs={{0,4},{2,6},{4,0},{6,2},{1,5},{3,7},{5,1},{7,3},{8,12},{10,14},{12... | collective-permute-start | bytes 1376264 | tf_op jit(solution)/shard_map/ppermute | solution.py:38
  128.7 5.2 %collective-permute-done.4 = bf16[2,224,512]{2,1,0:T(8,128)(2,1)S(1)} collective-permute-done((bf16[2,224,512]{2,1,0:T(8,128)(2,1)S(1)}, bf16[2,224,512]{2,1,0:T(8,128)(2,1)S(1)}, u32[]{:S(2)}, u32[]{:S(2)}) %collective-permute-start.4) | collective-permute-done | bytes 458784 | tf_op jit(solution)/shard_map/ppermute | solution.py:38
  133.9 2.8 %collective-permute-done.5 = bf16[2,224,512]{2,1,0:T(8,128)(2,1)S(1)} collective-permute-done((bf16[2,224,512]{2,1,0:T(8,128)(2,1)S(1)}, bf16[2,224,512]{2,1,0:T(8,128)(2,1)S(1)}, u32[]{:S(2)}, u32[]{:S(2)}) %collective-permute-start.5) | collective-permute-done | bytes 458784 | tf_op jit(solution)/shard_map/ppermute | solution.py:38
  136.7 10.1 %collective-permute-done.6 = bf16[2,224,512]{2,1,0:T(8,128)(2,1)S(1)} collective-permute-done((bf16[2,224,512]{2,1,0:T(8,128)(2,1)S(1)}, bf16[2,224,512]{2,1,0:T(8,128)(2,1)S(1)}, u32[]{:S(2)}, u32[]{:S(2)}) %collective-permute-start.6) | collective-permute-done | bytes 458784 | tf_op jit(solution)/shard_map/ppermute | solution.py:38
  147.6 12.1 %all-to-all-start.2 = ((bf16[8,56,256]{2,1,0:T(8,128)(2,1)}), bf16[8,56,256]{2,1,0:T(8,128)(2,1)S(1)}, u32[]{:S(2)}, u32[]{:S(2)}) async-start(bf16[8,56,256]{2,1,0:T(8,128)(2,1)} %fusion.18), calls=%async_computation.2 | async-start | bytes 458752 | tf_op jit(solution)/shard_map/all_to_all | solution.py:42
  160.0 4.7 %collective-permute-start.7 = (bf16[224,512]{1,0:T(8,128)(2,1)S(1)}, bf16[224,512]{1,0:T(8,128)(2,1)S(1)}, u32[]{:S(2)}, u32[]{:S(2)}) collective-permute-start(bf16[224,512]{1,0:T(8,128)(2,1)S(1)} %dynamic-slice_bitcast_fusion.5), channel_id=1, source_target_pairs={{0,8},{8,0},{1,9},{9,1},{2,10},{10,2},{3,11},{11,3},{4,12},{12,4},... | collective-permute-start | bytes 688136 | tf_op jit(solution)/shard_map/ppermute | solution.py:38
  164.6 4.9 %collective-permute-done.7 = bf16[224,512]{1,0:T(8,128)(2,1)S(1)} collective-permute-done((bf16[224,512]{1,0:T(8,128)(2,1)S(1)}, bf16[224,512]{1,0:T(8,128)(2,1)S(1)}, u32[]{:S(2)}, u32[]{:S(2)}) %collective-permute-start.7) | collective-permute-done | bytes 229408 | tf_op jit(solution)/shard_map/ppermute | solution.py:38
  170.3 25.8 %all-to-all-done.2 = bf16[8,56,256]{2,1,0:T(8,128)(2,1)S(1)} async-done(((bf16[8,56,256]{2,1,0:T(8,128)(2,1)}), bf16[8,56,256]{2,1,0:T(8,128)(2,1)S(1)}, u32[]{:S(2)}, u32[]{:S(2)}) %all-to-all-start.2) | async-done | bytes 229408 | tf_op jit(solution)/shard_map/all_to_all | solution.py:42
  (30 shorter events, 6.9 us)
Async XLA Ops:
  1.9 54.7 %collective-permute-start = (bf16[256,1792]{1,0:T(8,128)(2,1)S(1)}, bf16[256,1792]{1,0:T(8,128)(2,1)}, u32[]{:S(2)}, u32[]{:S(2)}) collective-permute-start(bf16[256,1792]{1,0:T(8,128)(2,1)S(1)} %dynamic_slice.33), channel_id=1, source_target_pairs={{0,512},{512,0},{1,513},{513,1},{2,514},{514,2},{3,515},{515,3},{4... | collective-permute-start | bytes 2752520 | tf_op jit(solution)/shard_map/ppermute | solution.py:67
  56.6 11.7 %copy-start.4 = (f32[512]{0:T(512)S(1)}, f32[512]{0:T(512)}, u32[]{:S(2)}) copy-start(f32[512]{0:T(512)} %param.11) | copy-start | bytes 6148
  56.6 11.7 %copy-start.3 = (s32[512]{0:T(512)S(1)}, s32[512]{0:T(512)}, u32[]{:S(2)}) copy-start(s32[512]{0:T(512)} %param.10) | copy-start | bytes 6148
  58.4 31.5 %all-to-all-start = ((bf16[4,896,384]{2,1,0:T(8,128)(2,1)}), bf16[4,896,384]{2,1,0:T(8,128)(2,1)S(1)}, u32[]{:S(2)}, u32[]{:S(2)}) async-start(bf16[4,896,384]{2,1,0:T(8,128)(2,1)} %broadcast_in_dim.26), calls=%async_computation | async-start | bytes 5505024 | tf_op jit(solution)/shard_map/all_to_all | solution.py:80
  65.7 13.9 %collective-permute-start.1 = (bf16[256,1792]{1,0:T(8,128)(2,1)}, bf16[256,1792]{1,0:T(8,128)(2,1)}, u32[]{:S(2)}, u32[]{:S(2)}) collective-permute-start(bf16[256,1792]{1,0:T(8,128)(2,1)} %collective-permute-done), channel_id=1, source_target_pairs={{0,1},{1,0},{2,3},{3,2},{4,5},{5,4},{6,7},{7,6},{8,9},{9,8},{10,11... | collective-permute-start | bytes 2752520 | tf_op jit(solution)/shard_map/ppermute | solution.py:74
  89.9 2.0 %copy-start.2 = (bf16[512,3584]{1,0:T(8,128)(2,1)S(1)}, bf16[512,3584]{1,0:T(8,128)(2,1)}, u32[]{:S(2)}) copy-start(bf16[512,3584]{1,0:T(8,128)(2,1)} %param.8) | copy-start | bytes 11010052
  90.2 2.9 %copy-start.5 = (bf16[512,3584]{1,0:T(8,128)(2,1)S(1)}, bf16[512,3584]{1,0:T(8,128)(2,1)}, u32[]{:S(2)}) copy-start(bf16[512,3584]{1,0:T(8,128)(2,1)} %param.9) | copy-start | bytes 11010052
  94.6 3.9 %copy-start.1 = (bf16[1024,1792]{0,1:T(8,128)(2,1)S(1)}, bf16[1024,1792]{0,1:T(8,128)(2,1)}, u32[]{:S(2)}) copy-start(bf16[1024,1792]{0,1:T(8,128)(2,1)} %pad_maximum_fusion) | copy-start | bytes 11010052
  94.6 8.5 %collective-permute-start.2 = (bf16[512,256]{0,1:T(8,128)(2,1)S(1)}, bf16[512,256]{0,1:T(8,128)(2,1)S(1)}, u32[]{:S(2)}, u32[]{:S(2)}) collective-permute-start(bf16[512,256]{0,1:T(8,128)(2,1)S(1)} %maximum_select_fusion), channel_id=1, source_target_pairs={{0,512},{512,0},{1,513},{513,1},{2,514},{514,2},{3,515},{515,3},{4... | collective-permute-start | bytes 786440 | tf_op jit(solution)/shard_map/ppermute | solution.py:99
  98.5 1.8 copy-start
  105.3 41.5 %all-to-all-start.1 = ((bf16[4,8,56,256]{3,2,1,0:T(8,128)(2,1)}), bf16[4,8,56,256]{3,2,1,0:T(8,128)(2,1)S(1)}, u32[]{:S(2)}, u32[]{:S(2)}) async-start(bf16[4,8,56,256]{3,2,1,0:T(8,128)(2,1)} %bitcast.53), calls=%async_computation.1 | async-start | bytes 1835008 | tf_op jit(solution)/shard_map/all_to_all | solution.py:117
  110.1 5.8 %collective-permute-start.3 = (bf16[2,4,224,512]{3,2,1,0:T(8,128)(2,1)S(1)}, bf16[2,4,224,512]{3,2,1,0:T(8,128)(2,1)}, u32[]{:S(2)}, u32[]{:S(2)}) collective-permute-start(bf16[2,4,224,512]{3,2,1,0:T(8,128)(2,1)S(1)} %dynamic-slice_bitcast_fusion), channel_id=1, source_target_pairs={{0,1},{1,0},{2,3},{3,2},{4,5},{5,4},{6,7},{7,6},{8,9},{9,8},{10,11... | collective-permute-start | bytes 5505032 | tf_op jit(solution)/shard_map/ppermute | solution.py:38
  118.6 15.3 %collective-permute-start.4 = (bf16[2,224,512]{2,1,0:T(8,128)(2,1)S(1)}, bf16[2,224,512]{2,1,0:T(8,128)(2,1)S(1)}, u32[]{:S(2)}, u32[]{:S(2)}) collective-permute-start(bf16[2,224,512]{2,1,0:T(8,128)(2,1)S(1)} %get-tuple-element.27), channel_id=1, source_target_pairs={{0,2},{2,4},{4,6},{6,0},{1,3},{3,5},{5,7},{7,1},{8,10},{10,12},{12... | collective-permute-start | bytes 1376264 | tf_op jit(solution)/shard_map/ppermute | solution.py:38
  122.1 14.6 %collective-permute-start.5 = (bf16[2,224,512]{2,1,0:T(8,128)(2,1)S(1)}, bf16[2,224,512]{2,1,0:T(8,128)(2,1)S(1)}, u32[]{:S(2)}, u32[]{:S(2)}) collective-permute-start(bf16[2,224,512]{2,1,0:T(8,128)(2,1)S(1)} %get-tuple-element.26), channel_id=1, source_target_pairs={{0,6},{2,0},{4,2},{6,4},{1,7},{3,1},{5,3},{7,5},{8,14},{10,8},{12,... | collective-permute-start | bytes 1376264 | tf_op jit(solution)/shard_map/ppermute | solution.py:38
  124.5 22.4 %collective-permute-start.6 = (bf16[2,224,512]{2,1,0:T(8,128)(2,1)S(1)}, bf16[2,224,512]{2,1,0:T(8,128)(2,1)S(1)}, u32[]{:S(2)}, u32[]{:S(2)}) collective-permute-start(bf16[2,224,512]{2,1,0:T(8,128)(2,1)S(1)} %get-tuple-element.25), channel_id=1, source_target_pairs={{0,4},{2,6},{4,0},{6,2},{1,5},{3,7},{5,1},{7,3},{8,12},{10,14},{12... | collective-permute-start | bytes 1376264 | tf_op jit(solution)/shard_map/ppermute | solution.py:38
  147.6 48.5 %all-to-all-start.2 = ((bf16[8,56,256]{2,1,0:T(8,128)(2,1)}), bf16[8,56,256]{2,1,0:T(8,128)(2,1)S(1)}, u32[]{:S(2)}, u32[]{:S(2)}) async-start(bf16[8,56,256]{2,1,0:T(8,128)(2,1)} %fusion.18), calls=%async_computation.2 | async-start | bytes 458752 | tf_op jit(solution)/shard_map/all_to_all | solution.py:42
  160.0 9.6 %collective-permute-start.7 = (bf16[224,512]{1,0:T(8,128)(2,1)S(1)}, bf16[224,512]{1,0:T(8,128)(2,1)S(1)}, u32[]{:S(2)}, u32[]{:S(2)}) collective-permute-start(bf16[224,512]{1,0:T(8,128)(2,1)S(1)} %dynamic-slice_bitcast_fusion.5), channel_id=1, source_target_pairs={{0,8},{8,0},{1,9},{9,1},{2,10},{10,2},{3,11},{11,3},{4,12},{12,4},... | collective-permute-start | bytes 688136 | tf_op jit(solution)/shard_map/ppermute | solution.py:38

commit v5 on v4

--- a/solution.py
+++ b/solution.py
@@ -118,12 +118,16 @@
 
     core_sum = summed(core_terms).astype(jnp.bfloat16)
     ring_terms = [part_for(core_sum, "ring", 1, 0)]
-    for shift in (1, RING - 1, 2):
+    for shift in (1, RING - 1):
         ring_terms.append(moved(part_for(core_sum, "ring", 1, shift), "ring", shift))
-    near_terms, ring_terms = lax.optimization_barrier((near_terms, ring_terms))
+    across_sent = part_for(core_sum, "ring", 1, 2)
+    near_terms, ring_terms, across_sent = lax.optimization_barrier(
+        (near_terms, ring_terms, across_sent)
+    )
     near_sum = summed([near_terms[i] for i in range(MID * NEAR)]).astype(jnp.bfloat16)
     weight_share = exchanged_sum(near_sum, "far")
 
+    ring_terms.append(moved(across_sent, "ring", 2))
     ring_sum = summed(ring_terms).astype(jnp.bfloat16)
     wide_terms = [part_for(ring_sum, "wide", 0, 0), moved(part_for(ring_sum, "wide", 0, 1), "wide", 1)]
     grad_tokens = summed(wide_terms).astype(jnp.bfloat16).T

time: 198 us -> 187 us (0.944)
  waiting for transfers between devices: 60.1 us -> 49.6 us
    all_to_all x1, waiting for transfers between devices: 25.8 us -> 11.5 us  [exchanged_sum(): terms = lax.all_to_all(parts, axes, 0, 0, tiled=True)]
    ppermute x5, waiting for transfers between devices: 26.9 us -> 30.8 us  [moved(): lax.ppermute(part, axis, [(i, (i + shift) % SIZES[axis]) for i in range(S...]
where the time goes in v5:
time: 187 us; the launch traced here: 186 us
  blocking collectives  50.6 us (27%)
  waiting for transfers between devices  49.6 us (27%)
  starting transfers between devices  48.7 us (26%)
  local copies, waits for them, and re-layouts  21.1 us (11%)
  other arithmetic  8.97 us (5%)
  matrix products  5.78 us (3%)
    all_gather x1, blocking collectives, local(): far_rows = lax.all_gather(owned, SECONDS, axis=0, tiled=True)  50.6 us
    ppermute x5, waiting for transfers between devices, moved(): lax.ppermute(part, axis, [(i, (i + shift) % SIZES[axis]) for i in range(S...  30.8 us
    ppermute x5, starting transfers between devices, moved(): lax.ppermute(part, axis, [(i, (i + shift) % SIZES[axis]) for i in range(S...  16.5 us
    all_to_all x1, starting transfers between devices, exchanged_sum(): terms = lax.all_to_all(parts, axes, 0, 0, tiled=True)  12.1 us
    all_to_all x1, waiting for transfers between devices, exchanged_sum(): terms = lax.all_to_all(parts, axes, 0, 0, tiled=True)  11.5 us
    optimization_barrier x2, local copies, waits for them, and re-layouts, local(): lax.optimization_barrier((far_rows, fetched_tokens, tokens))  8.16 us
    all_to_all x1, starting transfers between devices, local(): quads = lax.all_to_all(quads, QUAD, 0, 0, tiled=True)  7.3 us
    all_to_all x1, starting transfers between devices, local(): near_terms = lax.all_to_all(weight_terms, NEIGHBOURS, 0, 0, tiled=True)  4.77 us
  transfers between devices with their start and end apart: 11, of which 8 were waited for; matrix products, arithmetic and copies ran while one was open for 12% of the time, Pallas kernels for 0%

profile of v5, /device:TPU:40, one launch (start us, length us, event | category | flops | bytes accessed | tf_op | source)
XLA Modules:
  0.0 186.3 jit_solution(3844499078022907084)
XLA Ops:
  0.6 1.2 dynamic_slice.33
  1.9 3.4 %collective-permute-start = (bf16[256,1792]{1,0:T(8,128)(2,1)S(1)}, bf16[256,1792]{1,0:T(8,128)(2,1)}, u32[]{:S(2)}, u32[]{:S(2)}) collective-permute-start(bf16[256,1792]{1,0:T(8,128)(2,1)S(1)} %dynamic_slice.33), channel_id=1, source_target_pairs={{0,512},{512,0},{1,513},{513,1},{2,514},{514,2},{3,515},{515,3},{4... | collective-permute-start | bytes 2752520 | tf_op jit(solution)/shard_map/ppermute | solution.py:67
  6.1 50.6 %all_gather.3 = bf16[896,384]{1,0:T(8,128)(2,1)S(1)} all-gather(bf16[56,384]{1,0:T(8,128)(2,1)S(1)} %pad_maximum_fusion.3), channel_id=1, replica_groups=mesh['side'=2,'far'=8,'mid'=2,'near'=2,'wide'=2,'ring'=4,'core'=2] {'far..., dimensions={0}, use_global_device_ids=true | all-gather | bytes 731136 | tf_op jit(solution)/shard_map/all_gather | solution.py:70
  56.6 1.8 broadcast_in_dim.26
  58.4 7.3 %all-to-all-start = ((bf16[4,896,384]{2,1,0:T(8,128)(2,1)}), bf16[4,896,384]{2,1,0:T(8,128)(2,1)S(1)}, u32[]{:S(2)}, u32[]{:S(2)}) async-start(bf16[4,896,384]{2,1,0:T(8,128)(2,1)} %broadcast_in_dim.26), calls=%async_computation | async-start | bytes 5505024 | tf_op jit(solution)/shard_map/all_to_all | solution.py:80
  65.7 1.9 %collective-permute-start.1 = (bf16[256,1792]{1,0:T(8,128)(2,1)}, bf16[256,1792]{1,0:T(8,128)(2,1)}, u32[]{:S(2)}, u32[]{:S(2)}) collective-permute-start(bf16[256,1792]{1,0:T(8,128)(2,1)} %collective-permute-done), channel_id=1, source_target_pairs={{0,1},{1,0},{2,3},{3,2},{4,5},{5,4},{6,7},{7,6},{8,9},{9,8},{10,11... | collective-permute-start | bytes 2752520 | tf_op jit(solution)/shard_map/ppermute | solution.py:74
  68.5 2.2 %copy.21 = bf16[256,1792]{0,1:T(8,128)(2,1)} copy(bf16[256,1792]{1,0:T(8,128)(2,1)} %collective-permute-done) | data formatting | bytes 1835008 | tf_op jit(solution)/shard_map/optimization_barrier | solution.py:71
  70.8 5.9 %copy.20 = bf16[512,3584]{0,1:T(8,128)(2,1)} copy(bf16[512,3584]{1,0:T(8,128)(2,1)} %param.8) | data formatting | bytes 7340032 | tf_op jit(solution)/shard_map/optimization_barrier | solution.py:71
  76.7 2.9 %constant_dynamic-slice_fusion = bf16[512,1792]{0,1:T(8,128)(2,1)} fusion(bf16[512,3584]{0,1:T(8,128)(2,1)} %copy.20, s32[]{:T(128)S(6)} %select_n.94), kind=kLoop, calls=%fused_computation.51 | loop fusion | bytes 3670020 | tf_op jit(solution)/shard_map/dynamic_slice | solution.py:75
  79.6 2.2 %copy.22 = bf16[256,1792]{0,1:T(8,128)(2,1)} copy(bf16[256,1792]{1,0:T(8,128)(2,1)} %collective-permute-done.1) | data formatting | bytes 1835008 | tf_op jit(solution)/shard_map/layout_constraint | solution.py:22
  81.8 3.5 %pad_maximum_fusion = bf16[1024,1792]{0,1:T(8,128)(2,1)} fusion(bf16[256,1792]{0,1:T(8,128)(2,1)} %copy.22, bf16[256,1792]{0,1:T(8,128)(2,1)} %copy.21, bf16[512,1792]{0,1:T(8,128)(2,1)} %constant_dynamic-slice_fusion), kind=kLoop, calls=%fused_computation.1 | loop fusion | flops 11010048 | bytes 7340032 | tf_op jit(solution)/shard_map/concatenate | solution.py:76
  85.3 4.6 %all-to-all-done = bf16[4,896,384]{2,1,0:T(8,128)(2,1)S(1)} async-done(((bf16[4,896,384]{2,1,0:T(8,128)(2,1)}), bf16[4,896,384]{2,1,0:T(8,128)(2,1)S(1)}, u32[]{:S(2)}, u32[]{:S(2)}) %all-to-all-start) | async-done | bytes 2752544 | tf_op jit(solution)/shard_map/all_to_all | solution.py:80
  90.2 1.7 copy-done.2
  93.1 1.4 multiply_convert_fusion
  94.6 2.7 %collective-permute-start.2 = (bf16[512,256]{0,1:T(8,128)(2,1)S(1)}, bf16[512,256]{0,1:T(8,128)(2,1)S(1)}, u32[]{:S(2)}, u32[]{:S(2)}) collective-permute-start(bf16[512,256]{0,1:T(8,128)(2,1)S(1)} %maximum_select_fusion), channel_id=1, source_target_pairs={{0,512},{512,0},{1,513},{513,1},{2,514},{514,2},{3,515},{515,3},{4... | collective-permute-start | bytes 786440 | tf_op jit(solution)/shard_map/ppermute | solution.py:99
  99.0 1.3 copy-done
  100.5 2.7 %collective-permute-done.2 = bf16[512,256]{0,1:T(8,128)(2,1)S(1)} collective-permute-done((bf16[512,256]{0,1:T(8,128)(2,1)S(1)}, bf16[512,256]{0,1:T(8,128)(2,1)S(1)}, u32[]{:S(2)}, u32[]{:S(2)}) %collective-permute-start.2) | collective-permute-done | bytes 262176 | tf_op jit(solution)/shard_map/ppermute | solution.py:99
  103.2 2.1 %convolution_convert_fusion.1 = bf16[1792,256]{1,0:T(8,128)(2,1)} fusion(bf16[1792,1024]{1,0:T(8,128)(2,1)S(1)} %bitcast.52, bf16[512,256]{0,1:T(8,128)(2,1)S(1)} %collective-permute-done.2, bf16[512,128]{0,1:T(8,128)(2,1)S(1)} %get-tuple-element.29, bf16[512,128]{0,1:T(8,128)(2,1)S(1)} %get-tuple-element.30), kind=kOutput, calls=%fused_computation.4 | convolution fusion | flops 941555712 | bytes 5111808 | tf_op jit(solution)/shard_map/dot_general | solution.py:111
  105.3 4.8 %all-to-all-start.1 = ((bf16[4,8,56,256]{3,2,1,0:T(8,128)(2,1)}), bf16[4,8,56,256]{3,2,1,0:T(8,128)(2,1)S(1)}, u32[]{:S(2)}, u32[]{:S(2)}) async-start(bf16[4,8,56,256]{3,2,1,0:T(8,128)(2,1)} %bitcast.53), calls=%async_computation.1 | async-start | bytes 1835008 | tf_op jit(solution)/shard_map/all_to_all | solution.py:117
  110.1 1.9 %collective-permute-start.3 = (bf16[2,4,224,512]{3,2,1,0:T(8,128)(2,1)S(1)}, bf16[2,4,224,512]{3,2,1,0:T(8,128)(2,1)}, u32[]{:S(2)}, u32[]{:S(2)}) collective-permute-start(bf16[2,4,224,512]{3,2,1,0:T(8,128)(2,1)S(1)} %dynamic-slice_bitcast_fusion), channel_id=1, source_target_pairs={{0,1},{1,0},{2,3},{3,2},{4,5},{5,4},{6,7},{7,6},{8,9},{9,8},{10,11... | collective-permute-start | bytes 5505032 | tf_op jit(solution)/shard_map/ppermute | solution.py:38
  112.1 3.8 %collective-permute-done.3 = bf16[2,4,224,512]{3,2,1,0:T(8,128)(2,1)} collective-permute-done((bf16[2,4,224,512]{3,2,1,0:T(8,128)(2,1)S(1)}, bf16[2,4,224,512]{3,2,1,0:T(8,128)(2,1)}, u32[]{:S(2)}, u32[]{:S(2)}) %collective-permute-start.3) | collective-permute-done | bytes 1835040 | tf_op jit(solution)/shard_map/ppermute | solution.py:38
  115.9 2.6 %fusion = bf16[2,4,224,512]{3,2,1,0:T(8,128)(2,1)S(1)} fusion(bf16[2,4,224,512]{3,2,1,0:T(8,128)(2,1)} %collective-permute-done.3, bf16[2,4,2,224,512]{4,3,2,1,0:T(8,128)(2,1)} %bitcast.46, s32[]{:T(128)S(6)} %select_n.103), kind=kLoop, calls=%fused_computation.3 | loop fusion | flops 3670016 | bytes 5505028 | tf_op jit(solution)/shard_map/convert_element_type | solution.py:119
  118.6 3.5 %collective-permute-start.4 = (bf16[2,224,512]{2,1,0:T(8,128)(2,1)S(1)}, bf16[2,224,512]{2,1,0:T(8,128)(2,1)S(1)}, u32[]{:S(2)}, u32[]{:S(2)}) collective-permute-start(bf16[2,224,512]{2,1,0:T(8,128)(2,1)S(1)} %get-tuple-element.27), channel_id=1, source_target_pairs={{0,2},{2,4},{4,6},{6,0},{1,3},{3,5},{5,7},{7,1},{8,10},{10,12},{12... | collective-permute-start | bytes 1376264 | tf_op jit(solution)/shard_map/ppermute | solution.py:38
  122.1 2.3 %collective-permute-start.5 = (bf16[2,224,512]{2,1,0:T(8,128)(2,1)S(1)}, bf16[2,224,512]{2,1,0:T(8,128)(2,1)S(1)}, u32[]{:S(2)}, u32[]{:S(2)}) collective-permute-start(bf16[2,224,512]{2,1,0:T(8,128)(2,1)S(1)} %get-tuple-element.26), channel_id=1, source_target_pairs={{0,6},{2,0},{4,2},{6,4},{1,7},{3,1},{5,3},{7,5},{8,14},{10,8},{12,... | collective-permute-start | bytes 1376264 | tf_op jit(solution)/shard_map/ppermute | solution.py:38
  124.5 8.6 %collective-permute-done.4 = bf16[2,224,512]{2,1,0:T(8,128)(2,1)S(1)} collective-permute-done((bf16[2,224,512]{2,1,0:T(8,128)(2,1)S(1)}, bf16[2,224,512]{2,1,0:T(8,128)(2,1)S(1)}, u32[]{:S(2)}, u32[]{:S(2)}) %collective-permute-start.4) | collective-permute-done | bytes 458784 | tf_op jit(solution)/shard_map/ppermute | solution.py:38
  133.1 3.2 %collective-permute-done.5 = bf16[2,224,512]{2,1,0:T(8,128)(2,1)S(1)} collective-permute-done((bf16[2,224,512]{2,1,0:T(8,128)(2,1)S(1)}, bf16[2,224,512]{2,1,0:T(8,128)(2,1)S(1)}, u32[]{:S(2)}, u32[]{:S(2)}) %collective-permute-start.5) | collective-permute-done | bytes 458784 | tf_op jit(solution)/shard_map/ppermute | solution.py:38
  137.1 12.1 %all-to-all-start.2 = ((bf16[8,56,256]{2,1,0:T(8,128)(2,1)}), bf16[8,56,256]{2,1,0:T(8,128)(2,1)S(1)}, u32[]{:S(2)}, u32[]{:S(2)}) async-start(bf16[8,56,256]{2,1,0:T(8,128)(2,1)} %fusion.18), calls=%async_computation.2 | async-start | bytes 458752 | tf_op jit(solution)/shard_map/all_to_all | solution.py:42
  149.1 4.1 %collective-permute-start.6 = (bf16[2,224,512]{2,1,0:T(8,128)(2,1)S(1)}, bf16[2,224,512]{2,1,0:T(8,128)(2,1)S(1)}, u32[]{:S(2)}, u32[]{:S(2)}) collective-permute-start(bf16[2,224,512]{2,1,0:T(8,128)(2,1)S(1)} %get-tuple-element.23), channel_id=1, source_target_pairs={{0,4},{2,6},{4,0},{6,2},{1,5},{3,7},{5,1},{7,3},{8,12},{10,14},{12... | collective-permute-start | bytes 1376264 | tf_op jit(solution)/shard_map/ppermute | solution.py:38
  153.3 10.4 %collective-permute-done.6 = bf16[2,224,512]{2,1,0:T(8,128)(2,1)S(1)} collective-permute-done((bf16[2,224,512]{2,1,0:T(8,128)(2,1)S(1)}, bf16[2,224,512]{2,1,0:T(8,128)(2,1)S(1)}, u32[]{:S(2)}, u32[]{:S(2)}) %collective-permute-start.6) | collective-permute-done | bytes 458784 | tf_op jit(solution)/shard_map/ppermute | solution.py:38
  163.9 4.7 %collective-permute-start.7 = (bf16[224,512]{1,0:T(8,128)(2,1)S(1)}, bf16[224,512]{1,0:T(8,128)(2,1)S(1)}, u32[]{:S(2)}, u32[]{:S(2)}) collective-permute-start(bf16[224,512]{1,0:T(8,128)(2,1)S(1)} %dynamic-slice_bitcast_fusion.5), channel_id=1, source_target_pairs={{0,8},{8,0},{1,9},{9,1},{2,10},{10,2},{3,11},{11,3},{4,12},{12,4},... | collective-permute-start | bytes 688136 | tf_op jit(solution)/shard_map/ppermute | solution.py:38
  168.6 4.7 %collective-permute-done.7 = bf16[224,512]{1,0:T(8,128)(2,1)S(1)} collective-permute-done((bf16[224,512]{1,0:T(8,128)(2,1)S(1)}, bf16[224,512]{1,0:T(8,128)(2,1)S(1)}, u32[]{:S(2)}, u32[]{:S(2)}) %collective-permute-start.7) | collective-permute-done | bytes 229408 | tf_op jit(solution)/shard_map/ppermute | solution.py:38
  174.1 11.5 %all-to-all-done.2 = bf16[8,56,256]{2,1,0:T(8,128)(2,1)S(1)} async-done(((bf16[8,56,256]{2,1,0:T(8,128)(2,1)}), bf16[8,56,256]{2,1,0:T(8,128)(2,1)S(1)}, u32[]{:S(2)}, u32[]{:S(2)}) %all-to-all-start.2) | async-done | bytes 229408 | tf_op jit(solution)/shard_map/all_to_all | solution.py:42
  (30 shorter events, 6.9 us)
Async XLA Ops:
  1.9 54.7 %collective-permute-start = (bf16[256,1792]{1,0:T(8,128)(2,1)S(1)}, bf16[256,1792]{1,0:T(8,128)(2,1)}, u32[]{:S(2)}, u32[]{:S(2)}) collective-permute-start(bf16[256,1792]{1,0:T(8,128)(2,1)S(1)} %dynamic_slice.33), channel_id=1, source_target_pairs={{0,512},{512,0},{1,513},{513,1},{2,514},{514,2},{3,515},{515,3},{4... | collective-permute-start | bytes 2752520 | tf_op jit(solution)/shard_map/ppermute | solution.py:67
  56.6 11.7 %copy-start.4 = (f32[512]{0:T(512)S(1)}, f32[512]{0:T(512)}, u32[]{:S(2)}) copy-start(f32[512]{0:T(512)} %param.11) | copy-start | bytes 6148
  56.6 11.7 %copy-start.3 = (s32[512]{0:T(512)S(1)}, s32[512]{0:T(512)}, u32[]{:S(2)}) copy-start(s32[512]{0:T(512)} %param.10) | copy-start | bytes 6148
  58.4 31.5 %all-to-all-start = ((bf16[4,896,384]{2,1,0:T(8,128)(2,1)}), bf16[4,896,384]{2,1,0:T(8,128)(2,1)S(1)}, u32[]{:S(2)}, u32[]{:S(2)}) async-start(bf16[4,896,384]{2,1,0:T(8,128)(2,1)} %broadcast_in_dim.26), calls=%async_computation | async-start | bytes 5505024 | tf_op jit(solution)/shard_map/all_to_all | solution.py:80
  65.7 13.9 %collective-permute-start.1 = (bf16[256,1792]{1,0:T(8,128)(2,1)}, bf16[256,1792]{1,0:T(8,128)(2,1)}, u32[]{:S(2)}, u32[]{:S(2)}) collective-permute-start(bf16[256,1792]{1,0:T(8,128)(2,1)} %collective-permute-done), channel_id=1, source_target_pairs={{0,1},{1,0},{2,3},{3,2},{4,5},{5,4},{6,7},{7,6},{8,9},{9,8},{10,11... | collective-permute-start | bytes 2752520 | tf_op jit(solution)/shard_map/ppermute | solution.py:74
  89.9 2.0 %copy-start.2 = (bf16[512,3584]{1,0:T(8,128)(2,1)S(1)}, bf16[512,3584]{1,0:T(8,128)(2,1)}, u32[]{:S(2)}) copy-start(bf16[512,3584]{1,0:T(8,128)(2,1)} %param.8) | copy-start | bytes 11010052
  90.2 2.9 %copy-start.5 = (bf16[512,3584]{1,0:T(8,128)(2,1)S(1)}, bf16[512,3584]{1,0:T(8,128)(2,1)}, u32[]{:S(2)}) copy-start(bf16[512,3584]{1,0:T(8,128)(2,1)} %param.9) | copy-start | bytes 11010052
  94.6 3.9 %copy-start.1 = (bf16[1024,1792]{0,1:T(8,128)(2,1)S(1)}, bf16[1024,1792]{0,1:T(8,128)(2,1)}, u32[]{:S(2)}) copy-start(bf16[1024,1792]{0,1:T(8,128)(2,1)} %pad_maximum_fusion) | copy-start | bytes 11010052
  94.6 8.5 %collective-permute-start.2 = (bf16[512,256]{0,1:T(8,128)(2,1)S(1)}, bf16[512,256]{0,1:T(8,128)(2,1)S(1)}, u32[]{:S(2)}, u32[]{:S(2)}) collective-permute-start(bf16[512,256]{0,1:T(8,128)(2,1)S(1)} %maximum_select_fusion), channel_id=1, source_target_pairs={{0,512},{512,0},{1,513},{513,1},{2,514},{514,2},{3,515},{515,3},{4... | collective-permute-start | bytes 786440 | tf_op jit(solution)/shard_map/ppermute | solution.py:99
  98.5 1.8 copy-start
  105.3 31.0 %all-to-all-start.1 = ((bf16[4,8,56,256]{3,2,1,0:T(8,128)(2,1)}), bf16[4,8,56,256]{3,2,1,0:T(8,128)(2,1)S(1)}, u32[]{:S(2)}, u32[]{:S(2)}) async-start(bf16[4,8,56,256]{3,2,1,0:T(8,128)(2,1)} %bitcast.53), calls=%async_computation.1 | async-start | bytes 1835008 | tf_op jit(solution)/shard_map/all_to_all | solution.py:117
  110.1 5.8 %collective-permute-start.3 = (bf16[2,4,224,512]{3,2,1,0:T(8,128)(2,1)S(1)}, bf16[2,4,224,512]{3,2,1,0:T(8,128)(2,1)}, u32[]{:S(2)}, u32[]{:S(2)}) collective-permute-start(bf16[2,4,224,512]{3,2,1,0:T(8,128)(2,1)S(1)} %dynamic-slice_bitcast_fusion), channel_id=1, source_target_pairs={{0,1},{1,0},{2,3},{3,2},{4,5},{5,4},{6,7},{7,6},{8,9},{9,8},{10,11... | collective-permute-start | bytes 5505032 | tf_op jit(solution)/shard_map/ppermute | solution.py:38
  118.6 14.5 %collective-permute-start.4 = (bf16[2,224,512]{2,1,0:T(8,128)(2,1)S(1)}, bf16[2,224,512]{2,1,0:T(8,128)(2,1)S(1)}, u32[]{:S(2)}, u32[]{:S(2)}) collective-permute-start(bf16[2,224,512]{2,1,0:T(8,128)(2,1)S(1)} %get-tuple-element.27), channel_id=1, source_target_pairs={{0,2},{2,4},{4,6},{6,0},{1,3},{3,5},{5,7},{7,1},{8,10},{10,12},{12... | collective-permute-start | bytes 1376264 | tf_op jit(solution)/shard_map/ppermute | solution.py:38
  122.1 14.2 %collective-permute-start.5 = (bf16[2,224,512]{2,1,0:T(8,128)(2,1)S(1)}, bf16[2,224,512]{2,1,0:T(8,128)(2,1)S(1)}, u32[]{:S(2)}, u32[]{:S(2)}) collective-permute-start(bf16[2,224,512]{2,1,0:T(8,128)(2,1)S(1)} %get-tuple-element.26), channel_id=1, source_target_pairs={{0,6},{2,0},{4,2},{6,4},{1,7},{3,1},{5,3},{7,5},{8,14},{10,8},{12,... | collective-permute-start | bytes 1376264 | tf_op jit(solution)/shard_map/ppermute | solution.py:38
  137.1 48.5 %all-to-all-start.2 = ((bf16[8,56,256]{2,1,0:T(8,128)(2,1)}), bf16[8,56,256]{2,1,0:T(8,128)(2,1)S(1)}, u32[]{:S(2)}, u32[]{:S(2)}) async-start(bf16[8,56,256]{2,1,0:T(8,128)(2,1)} %fusion.18), calls=%async_computation.2 | async-start | bytes 458752 | tf_op jit(solution)/shard_map/all_to_all | solution.py:42
  149.1 14.5 %collective-permute-start.6 = (bf16[2,224,512]{2,1,0:T(8,128)(2,1)S(1)}, bf16[2,224,512]{2,1,0:T(8,128)(2,1)S(1)}, u32[]{:S(2)}, u32[]{:S(2)}) collective-permute-start(bf16[2,224,512]{2,1,0:T(8,128)(2,1)S(1)} %get-tuple-element.23), channel_id=1, source_target_pairs={{0,4},{2,6},{4,0},{6,2},{1,5},{3,7},{5,1},{7,3},{8,12},{10,14},{12... | collective-permute-start | bytes 1376264 | tf_op jit(solution)/shard_map/ppermute | solution.py:38
  163.9 9.4 %collective-permute-start.7 = (bf16[224,512]{1,0:T(8,128)(2,1)S(1)}, bf16[224,512]{1,0:T(8,128)(2,1)S(1)}, u32[]{:S(2)}, u32[]{:S(2)}) collective-permute-start(bf16[224,512]{1,0:T(8,128)(2,1)S(1)} %dynamic-slice_bitcast_fusion.5), channel_id=1, source_target_pairs={{0,8},{8,0},{1,9},{9,1},{2,10},{10,2},{3,11},{11,3},{4,12},{12,4},... | collective-permute-start | bytes 688136 | tf_op jit(solution)/shard_map/ppermute | solution.py:38

commit v6 on v4

--- a/solution.py
+++ b/solution.py
@@ -117,13 +117,18 @@
     near_terms = lax.all_to_all(weight_terms, NEIGHBOURS, 0, 0, tiled=True)
 
     core_sum = summed(core_terms).astype(jnp.bfloat16)
-    ring_terms = [part_for(core_sum, "ring", 1, 0)]
-    for shift in (1, RING - 1, 2):
-        ring_terms.append(moved(part_for(core_sum, "ring", 1, shift), "ring", shift))
-    near_terms, ring_terms = lax.optimization_barrier((near_terms, ring_terms))
+    ring_terms = [
+        part_for(core_sum, "ring", 1, 0),
+        moved(part_for(core_sum, "ring", 1, 1), "ring", 1),
+    ]
+    ring_sent = [part_for(core_sum, "ring", 1, shift) for shift in range(2, RING)]
+    near_terms, ring_terms, ring_sent = lax.optimization_barrier(
+        (near_terms, ring_terms, ring_sent)
+    )
     near_sum = summed([near_terms[i] for i in range(MID * NEAR)]).astype(jnp.bfloat16)
     weight_share = exchanged_sum(near_sum, "far")
 
+    ring_terms += [moved(sent, "ring", shift) for shift, sent in enumerate(ring_sent, start=2)]
     ring_sum = summed(ring_terms).astype(jnp.bfloat16)
     wide_terms = [part_for(ring_sum, "wide", 0, 0), moved(part_for(ring_sum, "wide", 0, 1), "wide", 1)]
     grad_tokens = summed(wide_terms).astype(jnp.bfloat16).T

time: 198 us -> 186 us (0.939)
  the two profiles are of different devices: /device:TPU:40 before, /device:TPU:24 now
where the time goes in v6:
time: 186 us; the launch traced here: 182 us
  blocking collectives  54.1 us (29%)
  waiting for transfers between devices  46.1 us (25%)
  starting transfers between devices  43.7 us (23%)
  local copies, waits for them, and re-layouts  21.1 us (11%)
  other arithmetic  10 us (5%)
  matrix products  5.78 us (3%)
    all_gather x1, blocking collectives, local(): far_rows = lax.all_gather(owned, SECONDS, axis=0, tiled=True)  54.1 us
    ppermute x5, waiting for transfers between devices, moved(): lax.ppermute(part, axis, [(i, (i + shift) % SIZES[axis]) for i in range(S...  38.4 us
    ppermute x5, starting transfers between devices, moved(): lax.ppermute(part, axis, [(i, (i + shift) % SIZES[axis]) for i in range(S...  15.5 us
    all_to_all x1, starting transfers between devices, exchanged_sum(): terms = lax.all_to_all(parts, axes, 0, 0, tiled=True)  12.1 us
    optimization_barrier x2, local copies, waits for them, and re-layouts, local(): lax.optimization_barrier((far_rows, fetched_tokens, tokens))  8.16 us
    all_to_all x1, waiting for transfers between devices, local(): quads = lax.all_to_all(quads, QUAD, 0, 0, tiled=True)  5.22 us
  transfers between devices with their start and end apart: 11, of which 6 were waited for; matrix products, arithmetic and copies ran while one was open for 13% of the time, Pallas kernels for 0%

profile of v6, /device:TPU:24, one launch (start us, length us, event | category | flops | bytes accessed | tf_op | source)
XLA Modules:
  0.0 182.4 jit_solution(18375481637515496541)
XLA Ops:
  0.6 1.2 dynamic_slice.33
  1.9 3.4 %collective-permute-start = (bf16[256,1792]{1,0:T(8,128)(2,1)S(1)}, bf16[256,1792]{1,0:T(8,128)(2,1)}, u32[]{:S(2)}, u32[]{:S(2)}) collective-permute-start(bf16[256,1792]{1,0:T(8,128)(2,1)S(1)} %dynamic_slice.33), channel_id=1, source_target_pairs={{0,512},{512,0},{1,513},{513,1},{2,514},{514,2},{3,515},{515,3},{4... | collective-permute-start | bytes 2752520 | tf_op jit(solution)/shard_map/ppermute | solution.py:67
  6.1 54.1 %all_gather.3 = bf16[896,384]{1,0:T(8,128)(2,1)S(1)} all-gather(bf16[56,384]{1,0:T(8,128)(2,1)S(1)} %pad_maximum_fusion.3), channel_id=1, replica_groups=mesh['side'=2,'far'=8,'mid'=2,'near'=2,'wide'=2,'ring'=4,'core'=2] {'far..., dimensions={0}, use_global_device_ids=true | all-gather | bytes 731136 | tf_op jit(solution)/shard_map/all_gather | solution.py:70
  60.2 1.8 broadcast_in_dim.26
  62.0 3.7 %all-to-all-start = ((bf16[4,896,384]{2,1,0:T(8,128)(2,1)}), bf16[4,896,384]{2,1,0:T(8,128)(2,1)S(1)}, u32[]{:S(2)}, u32[]{:S(2)}) async-start(bf16[4,896,384]{2,1,0:T(8,128)(2,1)} %broadcast_in_dim.26), calls=%async_computation | async-start | bytes 5505024 | tf_op jit(solution)/shard_map/all_to_all | solution.py:80
  65.6 1.9 %collective-permute-start.1 = (bf16[256,1792]{1,0:T(8,128)(2,1)}, bf16[256,1792]{1,0:T(8,128)(2,1)}, u32[]{:S(2)}, u32[]{:S(2)}) collective-permute-start(bf16[256,1792]{1,0:T(8,128)(2,1)} %collective-permute-done), channel_id=1, source_target_pairs={{0,1},{1,0},{2,3},{3,2},{4,5},{5,4},{6,7},{7,6},{8,9},{9,8},{10,11... | collective-permute-start | bytes 2752520 | tf_op jit(solution)/shard_map/ppermute | solution.py:74
  68.5 2.2 %copy.21 = bf16[256,1792]{0,1:T(8,128)(2,1)} copy(bf16[256,1792]{1,0:T(8,128)(2,1)} %collective-permute-done) | data formatting | bytes 1835008 | tf_op jit(solution)/shard_map/optimization_barrier | solution.py:71
  70.7 5.9 %copy.20 = bf16[512,3584]{0,1:T(8,128)(2,1)} copy(bf16[512,3584]{1,0:T(8,128)(2,1)} %param.8) | data formatting | bytes 7340032 | tf_op jit(solution)/shard_map/optimization_barrier | solution.py:71
  76.6 2.9 %constant_dynamic-slice_fusion = bf16[512,1792]{0,1:T(8,128)(2,1)} fusion(bf16[512,3584]{0,1:T(8,128)(2,1)} %copy.20, s32[]{:T(128)S(6)} %select_n.94), kind=kLoop, calls=%fused_computation.51 | loop fusion | bytes 3670020 | tf_op jit(solution)/shard_map/dynamic_slice | solution.py:75
  79.5 2.2 %copy.22 = bf16[256,1792]{0,1:T(8,128)(2,1)} copy(bf16[256,1792]{1,0:T(8,128)(2,1)} %collective-permute-done.1) | data formatting | bytes 1835008 | tf_op jit(solution)/shard_map/layout_constraint | solution.py:22
  81.7 3.5 %pad_maximum_fusion = bf16[1024,1792]{0,1:T(8,128)(2,1)} fusion(bf16[256,1792]{0,1:T(8,128)(2,1)} %copy.22, bf16[256,1792]{0,1:T(8,128)(2,1)} %copy.21, bf16[512,1792]{0,1:T(8,128)(2,1)} %constant_dynamic-slice_fusion), kind=kLoop, calls=%fused_computation.1 | loop fusion | flops 11010048 | bytes 7340032 | tf_op jit(solution)/shard_map/concatenate | solution.py:76
  85.2 5.2 %all-to-all-done = bf16[4,896,384]{2,1,0:T(8,128)(2,1)S(1)} async-done(((bf16[4,896,384]{2,1,0:T(8,128)(2,1)}), bf16[4,896,384]{2,1,0:T(8,128)(2,1)S(1)}, u32[]{:S(2)}, u32[]{:S(2)}) %all-to-all-start) | async-done | bytes 2752544 | tf_op jit(solution)/shard_map/all_to_all | solution.py:80
  90.7 1.7 copy-done.2
  92.5 1.2 fusion.4
  93.7 1.4 multiply_convert_fusion
  95.2 3.7 %collective-permute-start.2 = (bf16[512,256]{0,1:T(8,128)(2,1)S(1)}, bf16[512,256]{0,1:T(8,128)(2,1)S(1)}, u32[]{:S(2)}, u32[]{:S(2)}) collective-permute-start(bf16[512,256]{0,1:T(8,128)(2,1)S(1)} %maximum_select_fusion), channel_id=1, source_target_pairs={{0,512},{512,0},{1,513},{513,1},{2,514},{514,2},{3,515},{515,3},{4... | collective-permute-start | bytes 786440 | tf_op jit(solution)/shard_map/ppermute | solution.py:99
  100.5 1.3 copy-done
  101.9 2.4 %collective-permute-done.2 = bf16[512,256]{0,1:T(8,128)(2,1)S(1)} collective-permute-done((bf16[512,256]{0,1:T(8,128)(2,1)S(1)}, bf16[512,256]{0,1:T(8,128)(2,1)S(1)}, u32[]{:S(2)}, u32[]{:S(2)}) %collective-permute-start.2) | collective-permute-done | bytes 262176 | tf_op jit(solution)/shard_map/ppermute | solution.py:99
  104.4 2.1 %convolution_convert_fusion.1 = bf16[1792,256]{1,0:T(8,128)(2,1)} fusion(bf16[1792,1024]{1,0:T(8,128)(2,1)S(1)} %bitcast.52, bf16[512,256]{0,1:T(8,128)(2,1)S(1)} %collective-permute-done.2, bf16[512,128]{0,1:T(8,128)(2,1)S(1)} %get-tuple-element.29, bf16[512,128]{0,1:T(8,128)(2,1)S(1)} %get-tuple-element.30), kind=kOutput, calls=%fused_computation.4 | convolution fusion | flops 941555712 | bytes 5111808 | tf_op jit(solution)/shard_map/dot_general | solution.py:111
  106.5 3.5 %all-to-all-start.1 = ((bf16[4,8,56,256]{3,2,1,0:T(8,128)(2,1)}), bf16[4,8,56,256]{3,2,1,0:T(8,128)(2,1)S(1)}, u32[]{:S(2)}, u32[]{:S(2)}) async-start(bf16[4,8,56,256]{3,2,1,0:T(8,128)(2,1)} %bitcast.53), calls=%async_computation.1 | async-start | bytes 1835008 | tf_op jit(solution)/shard_map/all_to_all | solution.py:117
  110.0 1.9 %collective-permute-start.3 = (bf16[2,4,224,512]{3,2,1,0:T(8,128)(2,1)S(1)}, bf16[2,4,224,512]{3,2,1,0:T(8,128)(2,1)}, u32[]{:S(2)}, u32[]{:S(2)}) collective-permute-start(bf16[2,4,224,512]{3,2,1,0:T(8,128)(2,1)S(1)} %dynamic-slice_bitcast_fusion), channel_id=1, source_target_pairs={{0,1},{1,0},{2,3},{3,2},{4,5},{5,4},{6,7},{7,6},{8,9},{9,8},{10,11... | collective-permute-start | bytes 5505032 | tf_op jit(solution)/shard_map/ppermute | solution.py:38
  112.0 3.8 %collective-permute-done.3 = bf16[2,4,224,512]{3,2,1,0:T(8,128)(2,1)} collective-permute-done((bf16[2,4,224,512]{3,2,1,0:T(8,128)(2,1)S(1)}, bf16[2,4,224,512]{3,2,1,0:T(8,128)(2,1)}, u32[]{:S(2)}, u32[]{:S(2)}) %collective-permute-start.3) | collective-permute-done | bytes 1835040 | tf_op jit(solution)/shard_map/ppermute | solution.py:38
  115.8 2.6 %fusion = bf16[2,4,224,512]{3,2,1,0:T(8,128)(2,1)S(1)} fusion(bf16[2,4,224,512]{3,2,1,0:T(8,128)(2,1)} %collective-permute-done.3, bf16[2,4,2,224,512]{4,3,2,1,0:T(8,128)(2,1)} %bitcast.46, s32[]{:T(128)S(6)} %select_n.103), kind=kLoop, calls=%fused_computation.3 | loop fusion | flops 3670016 | bytes 5505028 | tf_op jit(solution)/shard_map/convert_element_type | solution.py:119
  118.5 2.1 %collective-permute-start.4 = (bf16[2,224,512]{2,1,0:T(8,128)(2,1)S(1)}, bf16[2,224,512]{2,1,0:T(8,128)(2,1)S(1)}, u32[]{:S(2)}, u32[]{:S(2)}) collective-permute-start(bf16[2,224,512]{2,1,0:T(8,128)(2,1)S(1)} %get-tuple-element.27), channel_id=1, source_target_pairs={{0,2},{2,4},{4,6},{6,0},{1,3},{3,5},{5,7},{7,1},{8,10},{10,12},{12... | collective-permute-start | bytes 1376264 | tf_op jit(solution)/shard_map/ppermute | solution.py:38
  120.7 12.3 %collective-permute-done.4 = bf16[2,224,512]{2,1,0:T(8,128)(2,1)S(1)} collective-permute-done((bf16[2,224,512]{2,1,0:T(8,128)(2,1)S(1)}, bf16[2,224,512]{2,1,0:T(8,128)(2,1)S(1)}, u32[]{:S(2)}, u32[]{:S(2)}) %collective-permute-start.4) | collective-permute-done | bytes 458784 | tf_op jit(solution)/shard_map/ppermute | solution.py:38
  133.8 12.1 %all-to-all-start.2 = ((bf16[8,56,256]{2,1,0:T(8,128)(2,1)}), bf16[8,56,256]{2,1,0:T(8,128)(2,1)S(1)}, u32[]{:S(2)}, u32[]{:S(2)}) async-start(bf16[8,56,256]{2,1,0:T(8,128)(2,1)} %fusion.18), calls=%async_computation.2 | async-start | bytes 458752 | tf_op jit(solution)/shard_map/all_to_all | solution.py:42
  145.9 2.6 %collective-permute-start.6 = (bf16[2,224,512]{2,1,0:T(8,128)(2,1)S(1)}, bf16[2,224,512]{2,1,0:T(8,128)(2,1)S(1)}, u32[]{:S(2)}, u32[]{:S(2)}) collective-permute-start(bf16[2,224,512]{2,1,0:T(8,128)(2,1)S(1)} %get-tuple-element.23), channel_id=1, source_target_pairs={{0,6},{2,0},{4,2},{6,4},{1,7},{3,1},{5,3},{7,5},{8,14},{10,8},{12,... | collective-permute-start | bytes 1376264 | tf_op jit(solution)/shard_map/ppermute | solution.py:38
  148.5 4.1 %collective-permute-start.5 = (bf16[2,224,512]{2,1,0:T(8,128)(2,1)S(1)}, bf16[2,224,512]{2,1,0:T(8,128)(2,1)}, u32[]{:S(2)}, u32[]{:S(2)}) collective-permute-start(bf16[2,224,512]{2,1,0:T(8,128)(2,1)S(1)} %get-tuple-element.22), channel_id=1, source_target_pairs={{0,4},{2,6},{4,0},{6,2},{1,5},{3,7},{5,1},{7,3},{8,12},{10,14},{12... | collective-permute-start | bytes 1376264 | tf_op jit(solution)/shard_map/ppermute | solution.py:38
  152.7 17.6 %collective-permute-done.6 = bf16[2,224,512]{2,1,0:T(8,128)(2,1)S(1)} collective-permute-done((bf16[2,224,512]{2,1,0:T(8,128)(2,1)S(1)}, bf16[2,224,512]{2,1,0:T(8,128)(2,1)S(1)}, u32[]{:S(2)}, u32[]{:S(2)}) %collective-permute-start.6) | collective-permute-done | bytes 458784 | tf_op jit(solution)/shard_map/ppermute | solution.py:38
  170.3 1.3 add_convert_fusion
  171.6 4.7 %collective-permute-start.7 = (bf16[224,512]{1,0:T(8,128)(2,1)S(1)}, bf16[224,512]{1,0:T(8,128)(2,1)S(1)}, u32[]{:S(2)}, u32[]{:S(2)}) collective-permute-start(bf16[224,512]{1,0:T(8,128)(2,1)S(1)} %dynamic-slice_bitcast_fusion.5), channel_id=1, source_target_pairs={{0,8},{8,0},{1,9},{9,1},{2,10},{10,2},{3,11},{11,3},{4,12},{12,4},... | collective-permute-start | bytes 688136 | tf_op jit(solution)/shard_map/ppermute | solution.py:38
  176.3 4.7 %collective-permute-done.7 = bf16[224,512]{1,0:T(8,128)(2,1)S(1)} collective-permute-done((bf16[224,512]{1,0:T(8,128)(2,1)S(1)}, bf16[224,512]{1,0:T(8,128)(2,1)S(1)}, u32[]{:S(2)}, u32[]{:S(2)}) %collective-permute-start.7) | collective-permute-done | bytes 229408 | tf_op jit(solution)/shard_map/ppermute | solution.py:38
  (30 shorter events, 5.5 us)
Async XLA Ops:
  1.9 58.3 %collective-permute-start = (bf16[256,1792]{1,0:T(8,128)(2,1)S(1)}, bf16[256,1792]{1,0:T(8,128)(2,1)}, u32[]{:S(2)}, u32[]{:S(2)}) collective-permute-start(bf16[256,1792]{1,0:T(8,128)(2,1)S(1)} %dynamic_slice.33), channel_id=1, source_target_pairs={{0,512},{512,0},{1,513},{513,1},{2,514},{514,2},{3,515},{515,3},{4... | collective-permute-start | bytes 2752520 | tf_op jit(solution)/shard_map/ppermute | solution.py:67
  60.2 8.1 %copy-start.4 = (f32[512]{0:T(512)S(1)}, f32[512]{0:T(512)}, u32[]{:S(2)}) copy-start(f32[512]{0:T(512)} %param.11) | copy-start | bytes 6148
  60.2 8.1 %copy-start.3 = (s32[512]{0:T(512)S(1)}, s32[512]{0:T(512)}, u32[]{:S(2)}) copy-start(s32[512]{0:T(512)} %param.10) | copy-start | bytes 6148
  62.0 28.5 %all-to-all-start = ((bf16[4,896,384]{2,1,0:T(8,128)(2,1)}), bf16[4,896,384]{2,1,0:T(8,128)(2,1)S(1)}, u32[]{:S(2)}, u32[]{:S(2)}) async-start(bf16[4,896,384]{2,1,0:T(8,128)(2,1)} %broadcast_in_dim.26), calls=%async_computation | async-start | bytes 5505024 | tf_op jit(solution)/shard_map/all_to_all | solution.py:80
  65.6 13.9 %collective-permute-start.1 = (bf16[256,1792]{1,0:T(8,128)(2,1)}, bf16[256,1792]{1,0:T(8,128)(2,1)}, u32[]{:S(2)}, u32[]{:S(2)}) collective-permute-start(bf16[256,1792]{1,0:T(8,128)(2,1)} %collective-permute-done), channel_id=1, source_target_pairs={{0,1},{1,0},{2,3},{3,2},{4,5},{5,4},{6,7},{7,6},{8,9},{9,8},{10,11... | collective-permute-start | bytes 2752520 | tf_op jit(solution)/shard_map/ppermute | solution.py:74
  90.4 2.0 %copy-start.2 = (bf16[512,3584]{1,0:T(8,128)(2,1)S(1)}, bf16[512,3584]{1,0:T(8,128)(2,1)}, u32[]{:S(2)}) copy-start(bf16[512,3584]{1,0:T(8,128)(2,1)} %param.8) | copy-start | bytes 11010052
  90.7 2.9 %copy-start.5 = (bf16[512,3584]{1,0:T(8,128)(2,1)S(1)}, bf16[512,3584]{1,0:T(8,128)(2,1)}, u32[]{:S(2)}) copy-start(bf16[512,3584]{1,0:T(8,128)(2,1)} %param.9) | copy-start | bytes 11010052
  95.2 4.8 %copy-start.1 = (bf16[1024,1792]{0,1:T(8,128)(2,1)S(1)}, bf16[1024,1792]{0,1:T(8,128)(2,1)}, u32[]{:S(2)}) copy-start(bf16[1024,1792]{0,1:T(8,128)(2,1)} %pad_maximum_fusion) | copy-start | bytes 11010052
  95.2 9.2 %collective-permute-start.2 = (bf16[512,256]{0,1:T(8,128)(2,1)S(1)}, bf16[512,256]{0,1:T(8,128)(2,1)S(1)}, u32[]{:S(2)}, u32[]{:S(2)}) collective-permute-start(bf16[512,256]{0,1:T(8,128)(2,1)S(1)} %maximum_select_fusion), channel_id=1, source_target_pairs={{0,512},{512,0},{1,513},{513,1},{2,514},{514,2},{3,515},{515,3},{4... | collective-permute-start | bytes 786440 | tf_op jit(solution)/shard_map/ppermute | solution.py:99
  100.0 1.8 %copy-start = (bf16[3584,512]{1,0:T(8,128)(2,1)}, bf16[3584,512]{1,0:T(8,128)(2,1)S(1)}, u32[]{:S(2)}) copy-start(bf16[3584,512]{1,0:T(8,128)(2,1)S(1)} %convolution_convert_fusion) | copy-start | bytes 11010052
  106.5 26.5 %all-to-all-start.1 = ((bf16[4,8,56,256]{3,2,1,0:T(8,128)(2,1)}), bf16[4,8,56,256]{3,2,1,0:T(8,128)(2,1)S(1)}, u32[]{:S(2)}, u32[]{:S(2)}) async-start(bf16[4,8,56,256]{3,2,1,0:T(8,128)(2,1)} %bitcast.53), calls=%async_computation.1 | async-start | bytes 1835008 | tf_op jit(solution)/shard_map/all_to_all | solution.py:117
  110.0 5.8 %collective-permute-start.3 = (bf16[2,4,224,512]{3,2,1,0:T(8,128)(2,1)S(1)}, bf16[2,4,224,512]{3,2,1,0:T(8,128)(2,1)}, u32[]{:S(2)}, u32[]{:S(2)}) collective-permute-start(bf16[2,4,224,512]{3,2,1,0:T(8,128)(2,1)S(1)} %dynamic-slice_bitcast_fusion), channel_id=1, source_target_pairs={{0,1},{1,0},{2,3},{3,2},{4,5},{5,4},{6,7},{7,6},{8,9},{9,8},{10,11... | collective-permute-start | bytes 5505032 | tf_op jit(solution)/shard_map/ppermute | solution.py:38
  118.5 14.5 %collective-permute-start.4 = (bf16[2,224,512]{2,1,0:T(8,128)(2,1)S(1)}, bf16[2,224,512]{2,1,0:T(8,128)(2,1)S(1)}, u32[]{:S(2)}, u32[]{:S(2)}) collective-permute-start(bf16[2,224,512]{2,1,0:T(8,128)(2,1)S(1)} %get-tuple-element.27), channel_id=1, source_target_pairs={{0,2},{2,4},{4,6},{6,0},{1,3},{3,5},{5,7},{7,1},{8,10},{10,12},{12... | collective-permute-start | bytes 1376264 | tf_op jit(solution)/shard_map/ppermute | solution.py:38
  133.8 47.9 %all-to-all-start.2 = ((bf16[8,56,256]{2,1,0:T(8,128)(2,1)}), bf16[8,56,256]{2,1,0:T(8,128)(2,1)S(1)}, u32[]{:S(2)}, u32[]{:S(2)}) async-start(bf16[8,56,256]{2,1,0:T(8,128)(2,1)} %fusion.18), calls=%async_computation.2 | async-start | bytes 458752 | tf_op jit(solution)/shard_map/all_to_all | solution.py:42
  145.9 24.4 %collective-permute-start.6 = (bf16[2,224,512]{2,1,0:T(8,128)(2,1)S(1)}, bf16[2,224,512]{2,1,0:T(8,128)(2,1)S(1)}, u32[]{:S(2)}, u32[]{:S(2)}) collective-permute-start(bf16[2,224,512]{2,1,0:T(8,128)(2,1)S(1)} %get-tuple-element.23), channel_id=1, source_target_pairs={{0,6},{2,0},{4,2},{6,4},{1,7},{3,1},{5,3},{7,5},{8,14},{10,8},{12,... | collective-permute-start | bytes 1376264 | tf_op jit(solution)/shard_map/ppermute | solution.py:38
  148.5 21.7 %collective-permute-start.5 = (bf16[2,224,512]{2,1,0:T(8,128)(2,1)S(1)}, bf16[2,224,512]{2,1,0:T(8,128)(2,1)}, u32[]{:S(2)}, u32[]{:S(2)}) collective-permute-start(bf16[2,224,512]{2,1,0:T(8,128)(2,1)S(1)} %get-tuple-element.22), channel_id=1, source_target_pairs={{0,4},{2,6},{4,0},{6,2},{1,5},{3,7},{5,1},{7,3},{8,12},{10,14},{12... | collective-permute-start | bytes 1376264 | tf_op jit(solution)/shard_map/ppermute | solution.py:38
  171.6 9.4 %collective-permute-start.7 = (bf16[224,512]{1,0:T(8,128)(2,1)S(1)}, bf16[224,512]{1,0:T(8,128)(2,1)S(1)}, u32[]{:S(2)}, u32[]{:S(2)}) collective-permute-start(bf16[224,512]{1,0:T(8,128)(2,1)S(1)} %dynamic-slice_bitcast_fusion.5), channel_id=1, source_target_pairs={{0,8},{8,0},{1,9},{9,1},{2,10},{10,2},{3,11},{11,3},{4,12},{12,4},... | collective-permute-start | bytes 688136 | tf_op jit(solution)/shard_map/ppermute | solution.py:38

commit v7 on v6

--- a/solution.py
+++ b/solution.py
@@ -72,15 +72,26 @@
         (far_rows, fetched_tokens, tokens)
     )
     swapped_tokens = row_major(lax.ppermute(fetched_tokens, "core", SWAP))
-    kept_tokens = lax.dynamic_slice_in_dim(early_tokens, side_index * half_features, half_features, 1)
+    kept_tokens = row_major(
+        lax.dynamic_slice_in_dim(early_tokens, side_index * half_features, half_features, 1)
+    )
     feature_rows = jnp.concatenate([kept_tokens, fetched_tokens, swapped_tokens], axis=0).T
     feature_rows = feature_rows.reshape(FAR, MID * NEAR, own_rows, SIDE * slot_count)
     feature_rows = lax.optimization_barrier(feature_rows.swapaxes(0, 1))
-    quads = jnp.broadcast_to(far_rows[None], (SIDE * NEAR, *far_rows.shape))
-    quads = lax.all_to_all(quads, QUAD, 0, 0, tiled=True)
-    quads, feature_rows = lax.optimization_barrier((quads, feature_rows))
-    panels = quads.reshape(SIDE, NEAR, FAR * MID, own_rows, 3 * hidden_width)
-    panels = panels.swapaxes(1, 2).reshape(feature_count, 3 * hidden_width)
+    near_index = lax.axis_index("near")
+    panels = jnp.zeros((SIDE, FAR * MID, NEAR, own_rows, 3 * hidden_width), jnp.bfloat16)
+    for side_step, near_step, rows in (
+        (0, 0, far_rows),
+        (0, 1, lax.ppermute(far_rows, "near", SWAP)),
+        (1, 0, lax.ppermute(far_rows, "side", SWAP)),
+        (1, 1, lax.ppermute(far_rows, QUAD, [(i, 3 - i) for i in range(4)])),
+    ):
+        block = rows.reshape(1, FAR * MID, 1, own_rows, 3 * hidden_width)
+        place = ((side_index + side_step) % SIDE, 0, (near_index + near_step) % NEAR, 0, 0)
+        panels = lax.dynamic_update_slice(panels, block, place)
+        if side_step == near_step == 0:
+            panels, feature_rows = lax.optimization_barrier((panels, feature_rows))
+    panels = panels.reshape(feature_count, 3 * hidden_width)
     both_panels = panels[:, : 2 * hidden_width]
     down_panel = panels[:, 2 * hidden_width :]
 

time: 186 us -> 196 us (1.054)
  waiting for transfers between devices: 46.1 us -> 55.6 us
  local copies, waits for them, and re-layouts: 21.1 us -> 16.6 us
  starting transfers between devices: 43.7 us -> 47.7 us
    ppermute x0 -> x3, waiting for transfers between devices: none -> 12.8 us  [the longest x1 12.8 us: local(): lax.ppermute(far_rows, 'side', SWAP)]
    ppermute x0 -> x3, starting transfers between devices: none -> 9.21 us  [the longest x1 4.85 us: local(): lax.ppermute(far_rows, QUAD, [(i, 3 - i) for i in range(4)])]
    optimization_barrier x3 -> x1, local copies, waits for them, and re-layouts: 8.66 us -> 0.51 us  [local(): panels, feature_rows = lax.optimization_barrier((panels, feature_rows))]
    transpose x1, local copies, waits for them, and re-layouts: 0.28 us -> 5.94 us  [local(): jnp.concatenate([kept_tokens, fetched_tokens, swapped_tokens], axis=0)]
    all_to_all x1 -> x0, waiting for transfers between devices: 5.22 us -> none  [local(): quads = lax.all_to_all(quads, QUAD, 0, 0, tiled=True)]
    transpose x0 -> x1, other arithmetic: none -> 5.12 us  [local(): jnp.concatenate([kept_tokens, fetched_tokens, swapped_tokens], axis=0)]
    dynamic_update_slice x0 -> x4, local copies, waits for them, and re-layouts: none -> 3.95 us  [local(): panels = lax.dynamic_update_slice(panels, block, place)]
    all_to_all x1 -> x0, starting transfers between devices: 3.66 us -> none  [local(): quads = lax.all_to_all(quads, QUAD, 0, 0, tiled=True)]
  transfers between devices with their start and end apart: 11 -> 13, of which waited for: 6 -> 6; matrix products, arithmetic and copies ran while one was open for 13% -> 12% of each run, Pallas kernels for 0% -> 0%
where the time goes in v7:
time: 196 us; the launch traced here: 193 us
  waiting for transfers between devices  55.6 us (28%)
  blocking collectives  54.1 us (28%)
  starting transfers between devices  47.7 us (24%)
  local copies, waits for them, and re-layouts  16.6 us (8%)
  other arithmetic  11.6 us (6%)
  matrix products  5.83 us (3%)
    all_gather x1, blocking collectives, local(): far_rows = lax.all_gather(owned, SECONDS, axis=0, tiled=True)  54.1 us
    ppermute x5, waiting for transfers between devices, moved(): lax.ppermute(part, axis, [(i, (i + shift) % SIZES[axis]) for i in range(S...  38.5 us
    ppermute x5, starting transfers between devices, moved(): lax.ppermute(part, axis, [(i, (i + shift) % SIZES[axis]) for i in range(S...  15.5 us
    ppermute x1, waiting for transfers between devices, local(): lax.ppermute(far_rows, 'side', SWAP)  12.8 us
    all_to_all x1, starting transfers between devices, exchanged_sum(): terms = lax.all_to_all(parts, axes, 0, 0, tiled=True)  11.5 us
    transpose x1, local copies, waits for them, and re-layouts, local(): jnp.concatenate([kept_tokens, fetched_tokens, swapped_tokens], axis=0)  5.94 us
    transpose x1, other arithmetic, local(): jnp.concatenate([kept_tokens, fetched_tokens, swapped_tokens], axis=0)  5.12 us
    ppermute x1, starting transfers between devices, local(): lax.ppermute(far_rows, QUAD, [(i, 3 - i) for i in range(4)])  4.85 us
  transfers between devices with their start and end apart: 13, of which 6 were waited for; matrix products, arithmetic and copies ran while one was open for 12% of the time, Pallas kernels for 0%

profile of v7, /device:TPU:24, one launch (start us, length us, event | category | flops | bytes accessed | tf_op | source)
XLA Modules:
  0.0 193.2 jit_solution(1085192290243906660)
XLA Ops:
  0.7 1.2 dynamic_slice.33
  1.9 3.4 %collective-permute-start = (bf16[256,1792]{1,0:T(8,128)(2,1)S(1)}, bf16[256,1792]{1,0:T(8,128)(2,1)}, u32[]{:S(2)}, u32[]{:S(2)}) collective-permute-start(bf16[256,1792]{1,0:T(8,128)(2,1)S(1)} %dynamic_slice.33), channel_id=1, source_target_pairs={{0,512},{512,0},{1,513},{513,1},{2,514},{514,2},{3,515},{515,3},{4... | collective-permute-start | bytes 2752520 | tf_op jit(solution)/shard_map/ppermute | solution.py:67
  6.1 54.1 %all_gather.3 = bf16[896,384]{1,0:T(8,128)(2,1)S(1)} all-gather(bf16[56,384]{1,0:T(8,128)(2,1)S(1)} %pad_maximum_fusion.2), channel_id=1, replica_groups=mesh['side'=2,'far'=8,'mid'=2,'near'=2,'wide'=2,'ring'=4,'core'=2] {'far..., dimensions={0}, use_global_device_ids=true | all-gather | bytes 731136 | tf_op jit(solution)/shard_map/all_gather | solution.py:70
  60.2 1.9 collective-permute-start.1
  63.1 1.9 collective-permute-start.2
  65.0 2.4 %collective-permute-start.3 = (bf16[896,384]{1,0:T(8,128)(2,1)S(1)}, bf16[896,384]{1,0:T(8,128)(2,1)}, u32[]{:S(2)}, u32[]{:S(2)}) collective-permute-start(bf16[896,384]{1,0:T(8,128)(2,1)S(1)} %all_gather.3), channel_id=1, source_target_pairs={{0,512},{512,0},{1,513},{513,1},{2,514},{514,2},{3,515},{515,3},{4... | collective-permute-start | bytes 2064392 | tf_op jit(solution)/shard_map/ppermute | solution.py:86
  67.5 4.9 %collective-permute-start.4 = (bf16[896,384]{1,0:T(8,128)(2,1)S(1)}, bf16[896,384]{1,0:T(8,128)(2,1)}, u32[]{:S(2)}, u32[]{:S(2)}) collective-permute-start(bf16[896,384]{1,0:T(8,128)(2,1)S(1)} %all_gather.3), channel_id=1, source_target_pairs={{0,528},{16,512},{512,16},{528,0},{1,529},{17,513},{513,17},{529,1... | collective-permute-start | bytes 2064392 | tf_op jit(solution)/shard_map/ppermute | solution.py:87
  72.3 1.6 constant_dynamic-slice_fusion
  74.3 5.1 %maximum_bitcast_fusion = bf16[1792,1024]{0,1:T(8,128)(2,1)} fusion(bf16[256,1792]{1,0:T(8,128)(2,1)} %collective-permute-done.1, bf16[256,1792]{1,0:T(8,128)(2,1)} %collective-permute-done, bf16[512,1792]{1,0:T(8,128)(2,1)S(1)} %constant_dynamic-slice_fusion), kind=kLoop, calls=%fused_computation.1 | loop fusion | flops 11010048 | bytes 7340032 | tf_op jit(solution)/shard_map/transpose | solution.py:78
  79.5 5.9 %copy.13 = bf16[1792,1024]{1,0:T(8,128)(2,1)} copy(bf16[1792,1024]{0,1:T(8,128)(2,1)} %maximum_bitcast_fusion) | data formatting | bytes 7340032 | tf_op jit(solution)/shard_map/transpose | solution.py:78
  85.4 1.4 constant_dynamic-update-slice_fusion.2
  86.8 12.8 %collective-permute-done.3 = bf16[896,384]{1,0:T(8,128)(2,1)} collective-permute-done((bf16[896,384]{1,0:T(8,128)(2,1)S(1)}, bf16[896,384]{1,0:T(8,128)(2,1)}, u32[]{:S(2)}, u32[]{:S(2)}) %collective-permute-start.3) | collective-permute-done | bytes 688160 | tf_op jit(solution)/shard_map/ppermute | solution.py:86
  99.6 1.2 constant_dynamic-update-slice_fusion.1
  100.8 1.2 constant_dynamic-update-slice_fusion
  104.1 1.4 multiply_convert_fusion
  105.6 2.7 %collective-permute-start.5 = (bf16[512,256]{0,1:T(8,128)(2,1)S(1)}, bf16[512,256]{0,1:T(8,128)(2,1)S(1)}, u32[]{:S(2)}, u32[]{:S(2)}) collective-permute-start(bf16[512,256]{0,1:T(8,128)(2,1)S(1)} %maximum_select_fusion), channel_id=1, source_target_pairs={{0,512},{512,0},{1,513},{513,1},{2,514},{514,2},{3,515},{515,3},{4... | collective-permute-start | bytes 786440 | tf_op jit(solution)/shard_map/ppermute | solution.py:110
  110.0 1.3 copy-done
  111.4 4.3 %collective-permute-done.5 = bf16[512,256]{0,1:T(8,128)(2,1)S(1)} collective-permute-done((bf16[512,256]{0,1:T(8,128)(2,1)S(1)}, bf16[512,256]{0,1:T(8,128)(2,1)S(1)}, u32[]{:S(2)}, u32[]{:S(2)}) %collective-permute-start.5) | collective-permute-done | bytes 262176 | tf_op jit(solution)/shard_map/ppermute | solution.py:110
  115.7 2.1 %convolution_convert_fusion.1 = bf16[1792,256]{1,0:T(8,128)(2,1)} fusion(bf16[1792,1024]{1,0:T(8,128)(2,1)S(1)} %bitcast.52, bf16[512,256]{0,1:T(8,128)(2,1)S(1)} %collective-permute-done.5, bf16[512,128]{0,1:T(8,128)(2,1)S(1)} %get-tuple-element.29, bf16[512,128]{0,1:T(8,128)(2,1)S(1)} %get-tuple-element.30), kind=kOutput, calls=%fused_computation.4 | convolution fusion | flops 941555712 | bytes 5111808 | tf_op jit(solution)/shard_map/dot_general | solution.py:122
  117.8 3.5 %all-to-all-start = ((bf16[4,8,56,256]{3,2,1,0:T(8,128)(2,1)}), bf16[4,8,56,256]{3,2,1,0:T(8,128)(2,1)S(1)}, u32[]{:S(2)}, u32[]{:S(2)}) async-start(bf16[4,8,56,256]{3,2,1,0:T(8,128)(2,1)} %bitcast.54), calls=%async_computation | async-start | bytes 1835008 | tf_op jit(solution)/shard_map/all_to_all | solution.py:128
  121.3 1.9 collective-permute-start.6
  123.3 3.8 %collective-permute-done.6 = bf16[2,4,224,512]{3,2,1,0:T(8,128)(2,1)} collective-permute-done((bf16[2,4,224,512]{3,2,1,0:T(8,128)(2,1)S(1)}, bf16[2,4,224,512]{3,2,1,0:T(8,128)(2,1)}, u32[]{:S(2)}, u32[]{:S(2)}) %collective-permute-start.6) | collective-permute-done | bytes 1835040 | tf_op jit(solution)/shard_map/ppermute | solution.py:38
  127.2 2.6 %fusion = bf16[2,4,224,512]{3,2,1,0:T(8,128)(2,1)S(1)} fusion(bf16[2,4,224,512]{3,2,1,0:T(8,128)(2,1)} %collective-permute-done.6, bf16[2,4,2,224,512]{4,3,2,1,0:T(8,128)(2,1)} %bitcast.47, s32[]{:T(128)S(6)} %select_n.151), kind=kLoop, calls=%fused_computation.3 | loop fusion | flops 3670016 | bytes 5505028 | tf_op jit(solution)/shard_map/convert_element_type | solution.py:130
  129.9 2.1 %collective-permute-start.7 = (bf16[2,224,512]{2,1,0:T(8,128)(2,1)S(1)}, bf16[2,224,512]{2,1,0:T(8,128)(2,1)S(1)}, u32[]{:S(2)}, u32[]{:S(2)}) collective-permute-start(bf16[2,224,512]{2,1,0:T(8,128)(2,1)S(1)} %get-tuple-element.27), channel_id=1, source_target_pairs={{0,2},{2,4},{4,6},{6,0},{1,3},{3,5},{5,7},{7,1},{8,10},{10,12},{12... | collective-permute-start | bytes 1376264 | tf_op jit(solution)/shard_map/ppermute | solution.py:38
  132.0 12.3 %collective-permute-done.7 = bf16[2,224,512]{2,1,0:T(8,128)(2,1)S(1)} collective-permute-done((bf16[2,224,512]{2,1,0:T(8,128)(2,1)S(1)}, bf16[2,224,512]{2,1,0:T(8,128)(2,1)S(1)}, u32[]{:S(2)}, u32[]{:S(2)}) %collective-permute-start.7) | collective-permute-done | bytes 458784 | tf_op jit(solution)/shard_map/ppermute | solution.py:38
  145.1 11.5 %all-to-all-start.1 = ((bf16[8,56,256]{2,1,0:T(8,128)(2,1)}), bf16[8,56,256]{2,1,0:T(8,128)(2,1)S(1)}, u32[]{:S(2)}, u32[]{:S(2)}) async-start(bf16[8,56,256]{2,1,0:T(8,128)(2,1)} %fusion.18), calls=%async_computation.1 | async-start | bytes 458752 | tf_op jit(solution)/shard_map/all_to_all | solution.py:42
  156.7 2.6 %collective-permute-start.9 = (bf16[2,224,512]{2,1,0:T(8,128)(2,1)S(1)}, bf16[2,224,512]{2,1,0:T(8,128)(2,1)S(1)}, u32[]{:S(2)}, u32[]{:S(2)}) collective-permute-start(bf16[2,224,512]{2,1,0:T(8,128)(2,1)S(1)} %get-tuple-element.23), channel_id=1, source_target_pairs={{0,6},{2,0},{4,2},{6,4},{1,7},{3,1},{5,3},{7,5},{8,14},{10,8},{12,... | collective-permute-start | bytes 1376264 | tf_op jit(solution)/shard_map/ppermute | solution.py:38
  159.3 4.1 %collective-permute-start.8 = (bf16[2,224,512]{2,1,0:T(8,128)(2,1)S(1)}, bf16[2,224,512]{2,1,0:T(8,128)(2,1)}, u32[]{:S(2)}, u32[]{:S(2)}) collective-permute-start(bf16[2,224,512]{2,1,0:T(8,128)(2,1)S(1)} %get-tuple-element.22), channel_id=1, source_target_pairs={{0,4},{2,6},{4,0},{6,2},{1,5},{3,7},{5,1},{7,3},{8,12},{10,14},{12... | collective-permute-start | bytes 1376264 | tf_op jit(solution)/shard_map/ppermute | solution.py:38
  163.5 17.6 %collective-permute-done.9 = bf16[2,224,512]{2,1,0:T(8,128)(2,1)S(1)} collective-permute-done((bf16[2,224,512]{2,1,0:T(8,128)(2,1)S(1)}, bf16[2,224,512]{2,1,0:T(8,128)(2,1)S(1)}, u32[]{:S(2)}, u32[]{:S(2)}) %collective-permute-start.9) | collective-permute-done | bytes 458784 | tf_op jit(solution)/shard_map/ppermute | solution.py:38
  181.1 1.3 add_convert_fusion
  182.4 4.6 %collective-permute-start.10 = (bf16[224,512]{1,0:T(8,128)(2,1)S(1)}, bf16[224,512]{1,0:T(8,128)(2,1)S(1)}, u32[]{:S(2)}, u32[]{:S(2)}) collective-permute-start(bf16[224,512]{1,0:T(8,128)(2,1)S(1)} %dynamic-slice_bitcast_fusion.5), channel_id=1, source_target_pairs={{0,8},{8,0},{1,9},{9,1},{2,10},{10,2},{3,11},{11,3},{4,12},{12,4},... | collective-permute-start | bytes 688136 | tf_op jit(solution)/shard_map/ppermute | solution.py:38
  187.0 4.8 %collective-permute-done.10 = bf16[224,512]{1,0:T(8,128)(2,1)S(1)} collective-permute-done((bf16[224,512]{1,0:T(8,128)(2,1)S(1)}, bf16[224,512]{1,0:T(8,128)(2,1)S(1)}, u32[]{:S(2)}, u32[]{:S(2)}) %collective-permute-start.10) | collective-permute-done | bytes 229408 | tf_op jit(solution)/shard_map/ppermute | solution.py:38
  (35 shorter events, 7.6 us)
Async XLA Ops:
  0.6 62.2 %copy-start.4 = (f32[512]{0:T(512)S(1)}, f32[512]{0:T(512)}, u32[]{:S(2)}) copy-start(f32[512]{0:T(512)} %param.11) | copy-start | bytes 6148
  0.6 62.2 %copy-start.3 = (s32[512]{0:T(512)S(1)}, s32[512]{0:T(512)}, u32[]{:S(2)}) copy-start(s32[512]{0:T(512)} %param.10) | copy-start | bytes 6148
  1.9 58.3 %collective-permute-start = (bf16[256,1792]{1,0:T(8,128)(2,1)S(1)}, bf16[256,1792]{1,0:T(8,128)(2,1)}, u32[]{:S(2)}, u32[]{:S(2)}) collective-permute-start(bf16[256,1792]{1,0:T(8,128)(2,1)S(1)} %dynamic_slice.33), channel_id=1, source_target_pairs={{0,512},{512,0},{1,513},{513,1},{2,514},{514,2},{3,515},{515,3},{4... | collective-permute-start | bytes 2752520 | tf_op jit(solution)/shard_map/ppermute | solution.py:67
  60.2 14.1 %collective-permute-start.1 = (bf16[256,1792]{1,0:T(8,128)(2,1)}, bf16[256,1792]{1,0:T(8,128)(2,1)}, u32[]{:S(2)}, u32[]{:S(2)}) collective-permute-start(bf16[256,1792]{1,0:T(8,128)(2,1)} %collective-permute-done), channel_id=1, source_target_pairs={{0,1},{1,0},{2,3},{3,2},{4,5},{5,4},{6,7},{7,6},{8,9},{9,8},{10,11... | collective-permute-start | bytes 2752520 | tf_op jit(solution)/shard_map/ppermute | solution.py:74
  63.1 22.3 %collective-permute-start.2 = (bf16[896,384]{1,0:T(8,128)(2,1)S(1)}, bf16[896,384]{1,0:T(8,128)(2,1)}, u32[]{:S(2)}, u32[]{:S(2)}) collective-permute-start(bf16[896,384]{1,0:T(8,128)(2,1)S(1)} %all_gather.3), channel_id=1, source_target_pairs={{0,16},{16,0},{1,17},{17,1},{2,18},{18,2},{3,19},{19,3},{4,20},{20... | collective-permute-start | bytes 2064392 | tf_op jit(solution)/shard_map/ppermute | solution.py:85
  65.0 34.6 %collective-permute-start.3 = (bf16[896,384]{1,0:T(8,128)(2,1)S(1)}, bf16[896,384]{1,0:T(8,128)(2,1)}, u32[]{:S(2)}, u32[]{:S(2)}) collective-permute-start(bf16[896,384]{1,0:T(8,128)(2,1)S(1)} %all_gather.3), channel_id=1, source_target_pairs={{0,512},{512,0},{1,513},{513,1},{2,514},{514,2},{3,515},{515,3},{4... | collective-permute-start | bytes 2064392 | tf_op jit(solution)/shard_map/ppermute | solution.py:86
  67.5 33.4 %collective-permute-start.4 = (bf16[896,384]{1,0:T(8,128)(2,1)S(1)}, bf16[896,384]{1,0:T(8,128)(2,1)}, u32[]{:S(2)}, u32[]{:S(2)}) collective-permute-start(bf16[896,384]{1,0:T(8,128)(2,1)S(1)} %all_gather.3), channel_id=1, source_target_pairs={{0,528},{16,512},{512,16},{528,0},{1,529},{17,513},{513,17},{529,1... | collective-permute-start | bytes 2064392 | tf_op jit(solution)/shard_map/ppermute | solution.py:87
  85.4 16.7 %copy-start.2 = (bf16[512,3584]{1,0:T(8,128)(2,1)S(1)}, bf16[512,3584]{1,0:T(8,128)(2,1)}, u32[]{:S(2)}) copy-start(bf16[512,3584]{1,0:T(8,128)(2,1)} %param.8) | copy-start | bytes 11010052
  102.1 2.0 %copy-start.5 = (bf16[512,3584]{1,0:T(8,128)(2,1)S(1)}, bf16[512,3584]{1,0:T(8,128)(2,1)}, u32[]{:S(2)}) copy-start(bf16[512,3584]{1,0:T(8,128)(2,1)} %param.9) | copy-start | bytes 11010052
  105.6 3.8 %copy-start.1 = (bf16[1792,1024]{1,0:T(8,128)(2,1)S(1)}, bf16[1792,1024]{1,0:T(8,128)(2,1)}, u32[]{:S(2)}) copy-start(bf16[1792,1024]{1,0:T(8,128)(2,1)} %copy.13) | copy-start | bytes 11010052
  105.6 10.1 %collective-permute-start.5 = (bf16[512,256]{0,1:T(8,128)(2,1)S(1)}, bf16[512,256]{0,1:T(8,128)(2,1)S(1)}, u32[]{:S(2)}, u32[]{:S(2)}) collective-permute-start(bf16[512,256]{0,1:T(8,128)(2,1)S(1)} %maximum_select_fusion), channel_id=1, source_target_pairs={{0,512},{512,0},{1,513},{513,1},{2,514},{514,2},{3,515},{515,3},{4... | collective-permute-start | bytes 786440 | tf_op jit(solution)/shard_map/ppermute | solution.py:110
  109.5 1.8 copy-start
  117.8 26.5 %all-to-all-start = ((bf16[4,8,56,256]{3,2,1,0:T(8,128)(2,1)}), bf16[4,8,56,256]{3,2,1,0:T(8,128)(2,1)S(1)}, u32[]{:S(2)}, u32[]{:S(2)}) async-start(bf16[4,8,56,256]{3,2,1,0:T(8,128)(2,1)} %bitcast.54), calls=%async_computation | async-start | bytes 1835008 | tf_op jit(solution)/shard_map/all_to_all | solution.py:128
  121.3 5.8 %collective-permute-start.6 = (bf16[2,4,224,512]{3,2,1,0:T(8,128)(2,1)S(1)}, bf16[2,4,224,512]{3,2,1,0:T(8,128)(2,1)}, u32[]{:S(2)}, u32[]{:S(2)}) collective-permute-start(bf16[2,4,224,512]{3,2,1,0:T(8,128)(2,1)S(1)} %dynamic-slice_bitcast_fusion), channel_id=1, source_target_pairs={{0,1},{1,0},{2,3},{3,2},{4,5},{5,4},{6,7},{7,6},{8,9},{9,8},{10,11... | collective-permute-start | bytes 5505032 | tf_op jit(solution)/shard_map/ppermute | solution.py:38
  129.9 14.5 %collective-permute-start.7 = (bf16[2,224,512]{2,1,0:T(8,128)(2,1)S(1)}, bf16[2,224,512]{2,1,0:T(8,128)(2,1)S(1)}, u32[]{:S(2)}, u32[]{:S(2)}) collective-permute-start(bf16[2,224,512]{2,1,0:T(8,128)(2,1)S(1)} %get-tuple-element.27), channel_id=1, source_target_pairs={{0,2},{2,4},{4,6},{6,0},{1,3},{3,5},{5,7},{7,1},{8,10},{10,12},{12... | collective-permute-start | bytes 1376264 | tf_op jit(solution)/shard_map/ppermute | solution.py:38
  145.1 47.4 %all-to-all-start.1 = ((bf16[8,56,256]{2,1,0:T(8,128)(2,1)}), bf16[8,56,256]{2,1,0:T(8,128)(2,1)S(1)}, u32[]{:S(2)}, u32[]{:S(2)}) async-start(bf16[8,56,256]{2,1,0:T(8,128)(2,1)} %fusion.18), calls=%async_computation.1 | async-start | bytes 458752 | tf_op jit(solution)/shard_map/all_to_all | solution.py:42
  156.7 24.4 %collective-permute-start.9 = (bf16[2,224,512]{2,1,0:T(8,128)(2,1)S(1)}, bf16[2,224,512]{2,1,0:T(8,128)(2,1)S(1)}, u32[]{:S(2)}, u32[]{:S(2)}) collective-permute-start(bf16[2,224,512]{2,1,0:T(8,128)(2,1)S(1)} %get-tuple-element.23), channel_id=1, source_target_pairs={{0,6},{2,0},{4,2},{6,4},{1,7},{3,1},{5,3},{7,5},{8,14},{10,8},{12,... | collective-permute-start | bytes 1376264 | tf_op jit(solution)/shard_map/ppermute | solution.py:38
  159.3 21.8 %collective-permute-start.8 = (bf16[2,224,512]{2,1,0:T(8,128)(2,1)S(1)}, bf16[2,224,512]{2,1,0:T(8,128)(2,1)}, u32[]{:S(2)}, u32[]{:S(2)}) collective-permute-start(bf16[2,224,512]{2,1,0:T(8,128)(2,1)S(1)} %get-tuple-element.22), channel_id=1, source_target_pairs={{0,4},{2,6},{4,0},{6,2},{1,5},{3,7},{5,1},{7,3},{8,12},{10,14},{12... | collective-permute-start | bytes 1376264 | tf_op jit(solution)/shard_map/ppermute | solution.py:38
  182.4 9.4 %collective-permute-start.10 = (bf16[224,512]{1,0:T(8,128)(2,1)S(1)}, bf16[224,512]{1,0:T(8,128)(2,1)S(1)}, u32[]{:S(2)}, u32[]{:S(2)}) collective-permute-start(bf16[224,512]{1,0:T(8,128)(2,1)S(1)} %dynamic-slice_bitcast_fusion.5), channel_id=1, source_target_pairs={{0,8},{8,0},{1,9},{9,1},{2,10},{10,2},{3,11},{11,3},{4,12},{12,4},... | collective-permute-start | bytes 688136 | tf_op jit(solution)/shard_map/ppermute | solution.py:38
